TPU v7x, 32 devices: a whole 2x2x4 slice. The times are simulated.
32 devices in a mesh: freq: 4 (over x, core), space: 8 (over z, y).
Axes of the slice: x: 2, y: 2, z: 4, core: 2. Of those that a mesh axis runs over, the one named last changes fastest.
Arguments:
- source_field: bfloat16 [2, 8, 1024, 1024], P(None, 'freq', 'space'), may hold values from -6 to 6
- receiver_field: bfloat16 [2, 8, 1024, 1024], P(None, 'freq', 'space'), may hold values from -6 to 6
- line_inverse: bfloat16 [2, 8, 1024, 1024], P(None, 'freq'), may hold values from -0.125 to 0.125
- lens_delay: float32 [3, 1024, 1024], P(None, 'space'), may hold values from -0.6 to 0.6
- omegas: float32 [8], P('freq'), may hold values from 4 to 40
- image_weights: float32 [8], P('freq'), may hold values from 0.1 to 1
Outputs:
- source_out: bfloat16 [2, 8, 1024, 1024], P(None, 'freq', 'space')
- receiver_out: bfloat16 [2, 8, 1024, 1024], P(None, 'freq', 'space')
- gradient: float32 [3, 1024, 1024], P(None, 'space')
All inputs are finite; a program needn't handle non-finite values.
Results may differ from a plain program's by a relative error of at most 0.017.
Values may be sent and summed in bfloat16 or wider, within the bound.
No kernel may reach another device: no remote copies, remote signals or barrier semaphores. Data moves between devices by JAX's collectives and lax.ppermute only.
A program may use at most 128 MiB of HBM per device.

v0:
```python
import jax
import jax.numpy as jnp
from jax import lax
from jax.sharding import PartitionSpec as P


def to_blocks(matrix, pieces):
    leading = matrix.shape[:-2]
    local_rows = matrix.shape[-2]
    columns = matrix.shape[-1] // pieces
    arranged = matrix.reshape(leading + (local_rows, pieces, columns))
    arranged = jnp.moveaxis(arranged, -2, -3)
    return arranged.reshape(leading + (pieces, local_rows * columns))


def from_blocks(blocked, local_rows):
    leading = blocked.shape[:-2]
    pieces = blocked.shape[-2]
    columns = blocked.shape[-1] // local_rows
    arranged = blocked.reshape(leading + (pieces, local_rows, columns))
    arranged = jnp.moveaxis(arranged, -1, -3)
    return arranged.reshape(leading + (columns, pieces * local_rows))


def rotate(fields, phase_angle):
    cosine = jnp.cos(phase_angle)
    sine_part = jnp.sin(phase_angle)
    flip_sign = jnp.array([1.0, -1.0], jnp.float32).reshape(2, 1, 1, 1)
    real_part = fields[:, 0]
    imag_part = fields[:, 1]
    return jnp.stack(
        [
            real_part * cosine + flip_sign * imag_part * sine_part,
            imag_part * cosine - flip_sign * real_part * sine_part,
        ],
        axis=1,
    )


def line_solve(line_inverse, fields):
    flip_sign = jnp.array([1.0, -1.0], jnp.float32).reshape(2, 1, 1, 1)
    prod_real = jnp.einsum(
        "fij,wpfrj->wpfri", line_inverse[0], fields, preferred_element_type=jnp.float32
    )
    prod_imag = jnp.einsum(
        "fij,wpfrj->wpfri", line_inverse[1], fields, preferred_element_type=jnp.float32
    )
    new_real = prod_real[:, 0] - flip_sign * prod_imag[:, 1]
    new_imag = prod_real[:, 1] + flip_sign * prod_imag[:, 0]
    return jnp.stack([new_real, new_imag], axis=1)


def march_step(line_inverse, phased, local_rows):
    pieces = lax.axis_size("space")
    across = line_solve(line_inverse, phased).astype(jnp.bfloat16)
    received = lax.all_to_all(
        to_blocks(across, pieces), "space", split_axis=3, concat_axis=3, tiled=True
    )
    return line_solve(line_inverse, from_blocks(received, local_rows))


def image_slice(fields, image_weights):
    image_term = fields[0, 0] * fields[1, 0] + fields[0, 1] * fields[1, 1]
    return jnp.sum(image_weights[:, None, None] * image_term, axis=0)


def reduce_slice(image_term):
    return lax.psum(image_term.astype(jnp.bfloat16), "freq").astype(jnp.float32)


def finish_sums(slices):
    stacked = jnp.stack(slices)
    return stacked


def on_device(source_field, receiver_field, line_inverse, lens_delay, omegas, image_weights):
    pieces = lax.axis_size("space")
    local_rows = lens_delay.shape[1]
    depth_count = lens_delay.shape[0]
    wavefields = jnp.stack([source_field, receiver_field]).astype(jnp.float32)
    slices = []
    lens_columns = from_blocks(
        lax.all_to_all(
            to_blocks(lens_delay, pieces), "space", split_axis=1, concat_axis=1, tiled=True
        ),
        local_rows,
    )
    phased = rotate(wavefields, omegas[:, None, None] * lens_delay[0][None]).astype(jnp.bfloat16)
    solved = march_step(line_inverse, phased, local_rows)
    slices.append(reduce_slice(image_slice(solved, image_weights)))
    for depth_step in range(1, depth_count):
        phase_angle = omegas[:, None, None] * lens_columns[depth_step][None]
        phased_columns = rotate(solved, phase_angle).astype(jnp.bfloat16)
        received = lax.all_to_all(
            to_blocks(phased_columns, pieces), "space", split_axis=3, concat_axis=3, tiled=True
        )
        solved = march_step(line_inverse, from_blocks(received, local_rows), local_rows)
        slices.append(reduce_slice(image_slice(solved, image_weights)))
    final_blocks = lax.all_to_all(
        to_blocks(solved.astype(jnp.bfloat16), pieces),
        "space",
        split_axis=3,
        concat_axis=3,
        tiled=True,
    )
    final_fields = from_blocks(final_blocks, local_rows)
    gradient_columns = finish_sums(slices)
    gradient = from_blocks(
        lax.all_to_all(
            to_blocks(gradient_columns, pieces).astype(jnp.bfloat16),
            "space",
            split_axis=1,
            concat_axis=1,
            tiled=True,
        ).astype(jnp.float32),
        local_rows,
    )
    return (final_fields[0], final_fields[1], gradient)


def solution(mesh):
    placed = (
        P(None, "freq", "space", None),
        P(None, "freq", "space", None),
        P(None, "freq", None, None),
        P(None, "space", None),
        P("freq"),
        P("freq"),
    )
    return jax.shard_map(
        on_device,
        mesh=mesh,
        in_specs=placed,
        out_specs=(
            P(None, "freq", "space", None),
            P(None, "freq", "space", None),
            P(None, "space", None),
        ),
        check_vma=False,
    )
```

profile of v0, /device:TPU:0, one launch (start us, length us, event | category | flops | bytes accessed | tf_op | source)
XLA Modules:
  0.0 648.7 jit_solution(17331599846674338511)
XLA Ops:
  11.5 7.4 %all-to-all-start.1 = ((f32[3,8,16384]{2,0,1:T(4,128)}), f32[3,8,16384]{2,0,1:T(4,128)S(1)}, u32[]{:S(2)}, u32[]{:S(2)}) async-start(f32[3,8,16384]{2,0,1:T(4,128)} %copy.277), calls=%async_computation.1 | async-start | bytes 4194304 | tf_op jit(solution)/shard_map/all_to_all | solution.py:83
  24.5 42.7 %all-to-all-done.1 = f32[3,8,16384]{2,0,1:T(4,128)S(1)} async-done(((f32[3,8,16384]{2,0,1:T(4,128)}), f32[3,8,16384]{2,0,1:T(4,128)S(1)}, u32[]{:S(2)}, u32[]{:S(2)}) %all-to-all-start.1) | async-done | bytes 1572896 | tf_op jit(solution)/shard_map/all_to_all | solution.py:83
  71.8 12.3 %multiply_cosine_fusion.2 = (f32[2,128,1024]{2,1,0:T(8,128)S(1)}, f32[2,128,1024]{2,1,0:T(8,128)S(1)}, f32[2,128,1024]{2,1,0:T(8,128)}, f32[2,128,1024]{2,1,0:T(...) fusion(f32[128,1024]{1,0:T(8,128)S(1)} %copy-done.20, f32[2]{0:T(128)S(1)} %copy-done.28, ...), kind=kLoop, calls=%fused_computation.110 | loop fusion | flops 786432 | bytes 7864328 | tf_op jit(solution)/shard_map/cos | solution.py:26
  85.2 4.7 fusion.33
  101.2 51.8 %all_to_all.40 = bf16[2,2,2,8,16384]{4,2,1,0,3:T(2,128)(2,1)S(1)} all-to-all(bf16[2,2,2,8,16384]{4,2,1,0,3:T(2,128)(2,1)S(1)} %copy.270), channel_id=1, replica_groups=mesh['freq'=4,'space'=8] {'space'}, dimensions={3} | all-to-all | bytes 4194304 | tf_op jit(solution)/shard_map/all_to_all | solution.py:56
  161.2 5.3 fusion.27
  166.6 6.1 fusion.45
  182.4 51.6 %all_to_all.41 = bf16[2,2,2,8,16384]{4,2,1,0,3:T(2,128)(2,1)S(1)} all-to-all(bf16[2,2,2,8,16384]{4,2,1,0,3:T(2,128)(2,1)S(1)} %copy.285), channel_id=1, replica_groups=mesh['freq'=4,'space'=8] {'space'}, dimensions={3} | all-to-all | bytes 4194304 | tf_op jit(solution)/shard_map/all_to_all | solution.py:94
  242.2 5.3 fusion.36
  260.7 51.6 %all_to_all.42 = bf16[2,2,2,8,16384]{4,2,1,0,3:T(2,128)(2,1)S(1)} all-to-all(bf16[2,2,2,8,16384]{4,2,1,0,3:T(2,128)(2,1)S(1)} %copy.290), channel_id=1, replica_groups=mesh['freq'=4,'space'=8] {'space'}, dimensions={3} | all-to-all | bytes 4194304 | tf_op jit(solution)/shard_map/all_to_all | solution.py:56
  320.5 5.3 fusion.30
  325.9 6.1 fusion.48
  341.6 51.4 %all_to_all.43 = bf16[2,2,2,8,16384]{4,2,1,0,3:T(2,128)(2,1)S(1)} all-to-all(bf16[2,2,2,8,16384]{4,2,1,0,3:T(2,128)(2,1)S(1)} %copy.302), channel_id=1, replica_groups=mesh['freq'=4,'space'=8] {'space'}, dimensions={3} | all-to-all | bytes 4194304 | tf_op jit(solution)/shard_map/all_to_all | solution.py:94
  401.3 5.3 fusion.39
  419.8 51.4 %all_to_all.44 = bf16[2,2,2,8,16384]{4,2,1,0,3:T(2,128)(2,1)S(1)} all-to-all(bf16[2,2,2,8,16384]{4,2,1,0,3:T(2,128)(2,1)S(1)} %copy.307), channel_id=1, replica_groups=mesh['freq'=4,'space'=8] {'space'}, dimensions={3} | all-to-all | bytes 4194304 | tf_op jit(solution)/shard_map/all_to_all | solution.py:56
  479.4 5.3 fusion.24
  484.8 8.1 %fusion.42 = f32[2,2,2,128,1024]{4,3,2,0,1:T(8,128)} fusion(bf16[2,2,2,128,1024]{4,3,2,0,1:T(8,128)(2,1)S(1)} %copy-done.25, bf16[2,2,1024,1024]{3,2,1,0:T(8,128)(2,1)} %param.17), kind=kOutput, calls=%fused_computation.30 | convolution fusion | flops 2147483648 | bytes 10485760 | tf_op jit(solution)/shard_map/fij,wpfrj->wpfri/dot_general | solution.py:42
  493.0 6.4 fusion.72
  499.4 6.2 subtract_convert_fusion
  512.7 34.0 %all-reduce.3.cloned.1.call-done = (bf16[1,128,8,128]{1,3,2,0:T(8,128)(2,1)}, bf16[1,128,8,128]{1,3,2,0:T(8,128)(2,1)}, bf16[1,128,8,128]{1,3,2,0:T(8,128)(2,1)}) async-done(((bf16[1,128,8,128]{1,3,2,0:T(8,128)(2,1)}, bf16[1,128,8,128]{1,3,2,0:T(8,128)(2,1)}, bf16[1,128,8,128]{1,3,2,0:T(8,128)(2,1)}), (bf16[1,128,8,128]{1,3,2,0:T(8,128)(2,1)}, bf16[1,128,8,128]{1,3,2,0:T(8,128)(2,1)}, ...) | async-done | bytes 786448 | tf_op jit(solution)/shard_map/psum | solution.py:68
  551.4 5.8 all-to-all-start.7
  562.7 5.1 copy.317
  567.8 14.5 %all-to-all-done.7 = bf16[3,8,16384]{2,0,1:T(4,128)(2,1)S(1)} async-done(((bf16[3,8,16384]{2,0,1:T(4,128)(2,1)}), bf16[3,8,16384]{2,0,1:T(4,128)(2,1)S(1)}, u32[]{:S(2)}, u32[]{:S(2)}) %all-to-all-start.7) | async-done | bytes 786464 | tf_op jit(solution)/shard_map/all_to_all | solution.py:109
  591.0 43.1 %all-to-all-done.6 = bf16[2,2,2,8,16384]{4,2,1,0,3:T(2,128)(2,1)S(1)} async-done(((bf16[2,2,2,8,16384]{4,2,1,0,3:T(2,128)(2,1)}), bf16[2,2,2,8,16384]{4,2,1,0,3:T(2,128)(2,1)S(1)}, u32[]{:S(2)}, u32[]{:S(2)}) %all-to-all-start.6) | async-done | bytes 2097184 | tf_op jit(solution)/shard_map/all_to_all | solution.py:99
  (161 shorter events, 146.2 us)
Async XLA Ops:
  11.5 7.5 %copy-start.26 = (bf16[2,2,128,1024]{3,2,1,0:T(8,128)(2,1)S(1)}, bf16[2,2,128,1024]{3,2,1,0:T(8,128)(2,1)}, u32[]{:S(2)}) copy-start(bf16[2,2,128,1024]{3,2,1,0:T(8,128)(2,1)} %param.16) | copy-start | bytes 3145732
  11.5 55.7 %all-to-all-start.1 = ((f32[3,8,16384]{2,0,1:T(4,128)}), f32[3,8,16384]{2,0,1:T(4,128)S(1)}, u32[]{:S(2)}, u32[]{:S(2)}) async-start(f32[3,8,16384]{2,0,1:T(4,128)} %copy.277), calls=%async_computation.1 | async-start | bytes 4194304 | tf_op jit(solution)/shard_map/all_to_all | solution.py:83
  18.9 527.7 %all-reduce.3.cloned.1.call-start = ((), (), s32[]{:S(2)}) async-start(), calls=%async_computation.8 | async-start | bytes 1572864 | tf_op jit(solution)/shard_map/psum | solution.py:68
  71.8 12.3 %copy-start.8 = (f32[2,2,2,128,1024]{4,3,1,0,2:T(8,128)S(1)}, f32[2,2,2,128,1024]{4,3,1,0,2:T(8,128)}, u32[]{:S(2)}) copy-start(f32[2,2,2,128,1024]{4,3,1,0,2:T(8,128)} %maximum_convert_fusion) | copy-start | bytes 12582916
  71.8 12.3 %copy-start.27 = (f32[2]{0:T(128)S(1)}, f32[2]{0:T(128)}, u32[]{:S(2)}) copy-start(f32[2]{0:T(128)} %constant.4.clone) | copy-start | bytes 28
  84.2 5.8 slice-start
  166.6 6.2 copy-start
  166.6 6.2 copy-start.18
  166.6 6.2 copy-start.19
  242.2 5.3 copy-start.22
  320.5 5.3 copy-start.23
  325.9 6.1 copy-start.4
  325.9 6.1 copy-start.17
  479.4 5.4 copy-start.25
  479.4 13.5 %copy-start.7 = (f32[2,2,2,128,1024]{4,3,2,0,1:T(8,128)S(1)}, f32[2,2,2,128,1024]{4,3,2,0,1:T(8,128)}, u32[]{:S(2)}) copy-start(f32[2,2,2,128,1024]{4,3,2,0,1:T(8,128)} %copy-done.6) | copy-start | bytes 12582916
  484.8 8.2 %copy-start.9 = (f32[2,2,2,128,1024]{4,3,2,0,1:T(8,128)}, f32[2,2,2,128,1024]{4,3,2,0,1:T(8,128)S(1)}, u32[]{:S(2)}) copy-start(f32[2,2,2,128,1024]{4,3,2,0,1:T(8,128)S(1)} %fusion.24) | copy-start | bytes 12582916
  484.8 8.2 %copy-start.1 = (f32[2,2,2,128,1024]{4,3,2,0,1:T(8,128)S(1)}, f32[2,2,2,128,1024]{4,3,2,0,1:T(8,128)}, u32[]{:S(2)}) copy-start(f32[2,2,2,128,1024]{4,3,2,0,1:T(8,128)} %copy-done) | copy-start | bytes 12582916
  484.8 8.2 %copy-start.3 = (f32[2,2,2,128,1024]{4,3,2,0,1:T(8,128)S(1)}, f32[2,2,2,128,1024]{4,3,2,0,1:T(8,128)}, u32[]{:S(2)}) copy-start(f32[2,2,2,128,1024]{4,3,2,0,1:T(8,128)} %copy-done.2) | copy-start | bytes 12582916
  484.8 8.2 %copy-start.5 = (f32[2,2,2,128,1024]{4,3,2,0,1:T(8,128)S(1)}, f32[2,2,2,128,1024]{4,3,2,0,1:T(8,128)}, u32[]{:S(2)}) copy-start(f32[2,2,2,128,1024]{4,3,2,0,1:T(8,128)} %copy-done.4) | copy-start | bytes 12582916
  499.4 6.2 copy-start.10
  499.4 6.7 %copy-start.14 = (f32[2,2,128,1024]{3,2,1,0:T(8,128)S(1)}, f32[2,2,128,1024]{3,2,1,0:T(8,128)}, u32[]{:S(2)}) copy-start(f32[2,2,128,1024]{3,2,1,0:T(8,128)} %get-tuple-element.57) | copy-start | bytes 6291460
  499.4 6.7 %copy-start.15 = (f32[2,2,128,1024]{3,2,1,0:T(8,128)S(1)}, f32[2,2,128,1024]{3,2,1,0:T(8,128)}, u32[]{:S(2)}) copy-start(f32[2,2,128,1024]{3,2,1,0:T(8,128)} %get-tuple-element.58) | copy-start | bytes 6291460
  551.4 30.9 %all-to-all-start.7 = ((bf16[3,8,16384]{2,0,1:T(4,128)(2,1)}), bf16[3,8,16384]{2,0,1:T(4,128)(2,1)S(1)}, u32[]{:S(2)}, u32[]{:S(2)}) async-start(bf16[3,8,16384]{2,0,1:T(4,128)(2,1)} %reshape.230), calls=%async_computation.7 | async-start | bytes 2097152 | tf_op jit(solution)/shard_map/all_to_all | solution.py:109
  582.3 51.8 %all-to-all-start.6 = ((bf16[2,2,2,8,16384]{4,2,1,0,3:T(2,128)(2,1)}), bf16[2,2,2,8,16384]{4,2,1,0,3:T(2,128)(2,1)S(1)}, u32[]{:S(2)}, u32[]{:S(2)}) async-start(bf16[2,2,2,8,16384]{4,2,1,0,3:T(2,128)(2,1)} %copy.317), calls=%async_computation.6 | async-start | bytes 4194304 | tf_op jit(solution)/shard_map/all_to_all | solution.py:99
  (12 other events, 33.6 us)
Sparse Core Ops, SparseCore 0:
  512.8 33.8 all-reduce.2
where the time goes:
time: 659 us; the launch traced here: 649 us
  blocking collectives  258 us (39%)
  waiting for transfers between devices  134 us (20%)
  local copies, waits for them, and re-layouts  120 us (18%)
  matrix products  63.2 us (10%)
  other arithmetic  41.5 us (6%)
  starting transfers between devices  16.9 us (3%)
  between operations  15.3 us (2%)
    all_to_all x3, blocking collectives, march_step(): lax.all_to_all(to_blocks(across, pieces), 'space', split_axis=3, concat_a...  155 us
    all_to_all x2, blocking collectives, on_device(): lax.all_to_all(to_blocks(phased_columns, pieces), 'space', split_axis=3,...  103 us
    all_to_all x1, waiting for transfers between devices, on_device(): lax.all_to_all(to_blocks(solved.astype(jnp.bfloat16), pieces), 'space', s...  43.1 us
    all_to_all x1, waiting for transfers between devices, on_device(): lax.all_to_all(to_blocks(lens_delay, pieces), 'space', split_axis=1, conc...  42.7 us
    reshape x14, local copies, waits for them, and re-layouts, to_blocks(): return arranged.reshape(leading + (pieces, local_rows * columns))  40.7 us
    psum x1, waiting for transfers between devices, reduce_slice(): return lax.psum(image_term.astype(jnp.bfloat16), 'freq').astype(jnp.float32)  34 us
    dot_general x6, matrix products, line_solve(): jnp.einsum('fij,wpfrj->wpfri', line_inverse[0], fields, preferred_element...  31.8 us
    dot_general x6, matrix products, line_solve(): jnp.einsum('fij,wpfrj->wpfri', line_inverse[1], fields, preferred_element...  31.4 us
  transfers between devices with their start and end apart: 4, of which 4 were waited for; matrix products, arithmetic and copies ran while one was open for 3% of the time, Pallas kernels for 0%

commit v1 on v0

--- a/solution.py
+++ b/solution.py
@@ -1,7 +1,570 @@
 import jax
 import jax.numpy as jnp
 from jax import lax
+from jax.experimental import pallas as pl
+from jax.experimental.pallas import tpu as pltpu
 from jax.sharding import PartitionSpec as P
+
+BF = jnp.bfloat16
+F32 = jnp.float32
+TWO_OVER_PI = 0.63661977236758134
+ANY = pl.BlockSpec(memory_space=pl.ANY)
+SMEM = pl.BlockSpec(memory_space=pltpu.SMEM)
+
+
+def sin_cos(quarter_turns):
+    whole = jnp.round(quarter_turns)
+    r = quarter_turns - whole
+    q = r * r
+    s = -0.00460174 * q + 0.07968794
+    s = s * q - 0.64596367
+    s = (s * q + 1.57079632) * r
+    c = 0.00091925 * q - 0.02086341
+    c = c * q + 0.25366950
+    c = c * q - 1.23370055
+    c = c * q + 1.0
+    k = whole.astype(jnp.int32)
+    odd = (k & 1) == 1
+    sine = jnp.where(odd, c, s)
+    cosine = jnp.where(odd, s, c)
+    sine = jnp.where((k & 2) == 2, -sine, sine)
+    cosine = jnp.where(((k + 1) & 2) == 2, -cosine, cosine)
+    return sine, cosine
+
+
+def dot_rows(a, b):
+    return lax.dot_general(a, b, (((1,), (0,)), ((), ())), preferred_element_type=F32)
+
+
+def dot_lines(a, b):
+    return lax.dot_general(a, b, (((1,), (1,)), ((), ())), preferred_element_type=F32)
+
+
+def spec(block, index):
+    return pl.BlockSpec(block, index)
+
+
+def call(body, grid, ins, outs, scratch, operands, cost, limit=60 << 20):
+    return pl.pallas_call(
+        body,
+        out_shape=[jax.ShapeDtypeStruct(s, d) for s, d, _, _ in outs],
+        grid_spec=pltpu.PrefetchScalarGridSpec(
+            num_scalar_prefetch=1,
+            grid=grid,
+            in_specs=ins,
+            out_specs=[pl.BlockSpec(b, i) for _, _, b, i in outs],
+            scratch_shapes=scratch,
+        ),
+        compiler_params=pltpu.CompilerParams(vmem_limit_bytes=limit),
+        cost_estimate=pl.CostEstimate(flops=cost, bytes_accessed=8 << 20, transcendentals=0),
+    )(*operands)
+
+
+def home_solve(ids, turn, source, receiver, matrix, lens, omegas):
+    _, _, rows, cols = source.shape
+    half = cols // 2
+
+    def body(ids, src, rec, mat, len_ref, om, m00, m01, m10, m11, phased):
+        b = pl.program_id(0)
+        y = ids[3]
+        j = ids[4] ^ turn
+
+        @pl.when(b == 0)
+        def _():
+            sine, cosine = sin_cos(len_ref[0] * (om[j] * TWO_OVER_PI))
+            sr = src[0, 0].astype(F32)
+            si = src[1, 0].astype(F32)
+            rr = rec[0, 0].astype(F32)
+            ri = -rec[1, 0].astype(F32)
+            first = y == 0
+            for at, (re, im) in enumerate(
+                (
+                    (jnp.where(first, sr, rr), jnp.where(first, si, ri)),
+                    (jnp.where(first, rr, sr), jnp.where(first, ri, si)),
+                )
+            ):
+                phased[pl.ds(at * rows, rows), :] = (re * cosine + im * sine).astype(BF)
+                phased[pl.ds((2 + at) * rows, rows), :] = (im * cosine - re * sine).astype(BF)
+
+        q_re = dot_lines(phased[...], mat[0, 0])
+        q_im = dot_lines(phased[...], mat[1, 0])
+        n = 2 * rows
+        new_re = (q_re[:n] - q_im[n:]).astype(BF)
+        new_im = (q_re[n:] + q_im[:n]).astype(BF)
+        for at, outs in enumerate(((m00, m10), (m01, m11))):
+
+            @pl.when(b == at)
+            def _(outs=outs):
+                for w, out in enumerate(outs):
+                    out[0] = new_re[w * rows : (w + 1) * rows]
+                    out[1] = new_im[w * rows : (w + 1) * rows]
+
+    message = ((2, rows, half), BF, (2, rows, half), lambda b, ids: (0, 0, 0))
+    field = spec((2, 1, rows, cols), lambda b, ids: (0, ids[4] ^ turn, 0, 0))
+    return call(
+        body,
+        (2,),
+        [
+            field,
+            field,
+            spec((2, 1, half, cols), lambda b, ids: (0, ids[4] ^ turn, ids[5] ^ b, 0)),
+            spec((1, rows, cols), lambda b, ids: (0, 0, 0)),
+            SMEM,
+        ],
+        [message] * 4,
+        [pltpu.VMEM((4 * rows, cols), BF)],
+        (ids, source, receiver, matrix, lens, omegas),
+        2 * 4 * rows * cols * cols * 2,
+    )
+
+
+def lens_place(ids, s, side):
+    return ((ids[1] ^ side) * 2 + (ids[3] ^ (s % 2))) * 4 + (ids[2] ^ (s // 2))
+
+
+def rotated(re, im, sine, cosine):
+    return (re * cosine + im * sine).astype(BF), (im * cosine - re * sine).astype(BF)
+
+
+def column_solve(ids, messages, matrix, lens, omega):
+    _, rows, half = messages[0].shape
+    n = matrix.shape[-1]
+    slices = n // rows
+    tile = 2 * rows
+    tiles = n // tile
+    quarter = rows // 2
+    per = tile // quarter
+    blocked = matrix.reshape(2, slices, 2, quarter, n)
+
+    def body(ids, *refs):
+        (m0, m1, m2, m3, m4, m5, m6, m7, mat, mat_half, len_ref, om,
+         keep, send, phased, out, field, sems) = refs
+        i = pl.program_id(0)
+        t = ids[4] * 2 + ids[3]
+
+        @pl.when(i == 0)
+        def _():
+            copies = []
+            for at, m in enumerate((m0, m1, m2, m3, m4, m5, m6, m7)):
+                a, b = at // 2, at % 2
+                place = (ids[0] ^ b) * 4 + (t ^ a)
+                for part in range(2):
+                    copies.append(
+                        pltpu.make_async_copy(
+                            m.at[part],
+                            field.at[part, pl.ds(pl.multiple_of(place * rows, rows), rows)],
+                            sems.at[at, part],
+                        )
+                    )
+            for copy in copies:
+                copy.start()
+            for copy in copies:
+                copy.wait()
+
+        @pl.when(i < tiles)
+        def _():
+            left = mat[...].reshape(2 * tile, n)
+            q_re = dot_rows(left, field[0])
+            q_im = dot_rows(left, field[1])
+            new_re = q_re[:tile] - q_im[tile:]
+            new_im = q_im[:tile] + q_re[tile:]
+            first = ids[3] == 0
+            for part, new in enumerate((new_re, new_im)):
+                even, odd = new[:rows].astype(BF), new[rows:].astype(BF)
+                keep[part, i] = jnp.where(first, even, odd)
+                send[part, i] = jnp.where(first, odd, even)
+            for s in range(2):
+                for side in range(2):
+                    at = ((ids[1] ^ side) * 2 + (ids[3] ^ s)) * 4 + (ids[2] ^ i)
+                    sine, cosine = sin_cos(len_ref[at] * (om[0] * TWO_OVER_PI))
+                    lo = s * rows + side * quarter
+                    re, im = rotated(
+                        new_re[lo : lo + quarter], new_im[lo : lo + quarter], sine, cosine
+                    )
+                    to = pl.ds(pl.multiple_of(i * tile + lo, quarter), quarter)
+                    phased[0, to] = re
+                    phased[1, to] = im
+
+        @pl.when(i >= tiles)
+        def _():
+            left = mat_half[...].reshape(2 * tile, n)
+            q_re = dot_rows(left, phased[0])
+            q_im = dot_rows(left, phased[1])
+            to = pl.ds(pl.multiple_of((i - tiles) * tile, tile), tile)
+            out[0, to] = (q_re[:tile] - q_im[tile:]).astype(BF)
+            out[1, to] = (q_im[:tile] + q_re[tile:]).astype(BF)
+
+    flat = lambda rank: (lambda i, ids: (0,) * rank)
+    part_shape = (2, tiles, rows, half)
+    return call(
+        body,
+        (tiles + tiles // 2,),
+        [ANY] * 8
+        + [
+            spec((2, tile, n), lambda i, ids: (0, jnp.minimum(i, tiles - 1), 0)),
+            spec(
+                (2, per, 1, quarter, n),
+                lambda i, ids: (0, jnp.maximum(i - tiles, 0), 1 - ids[0], 0, 0),
+            ),
+            spec(lens.shape, flat(3)),
+            SMEM,
+        ],
+        [
+            (part_shape, BF, part_shape, flat(4)),
+            (part_shape, BF, part_shape, flat(4)),
+            ((2, n, half), BF, (2, n, half), flat(3)),
+            ((2, n // 2, half), BF, (2, n // 2, half), flat(3)),
+        ],
+        [pltpu.VMEM((2, n, half), BF), pltpu.SemaphoreType.DMA((8, 2))],
+        (ids, *messages, matrix, blocked, lens, omega),
+        12 * n * n * half,
+    )
+
+
+def column_rest(ids, phased, matrix, rows):
+    _, n, half = phased.shape
+    slices = n // rows
+    tile = 2 * rows
+    quarter = rows // 2
+    per = tile // quarter
+    blocked = matrix.reshape(2, slices, 2, quarter, n)
+
+    def body(ids, field, mat_half, out):
+        left = mat_half[...].reshape(2 * tile, n)
+        q_re = dot_rows(left, field[0])
+        q_im = dot_rows(left, field[1])
+        out[0] = (q_re[:tile] - q_im[tile:]).astype(BF)
+        out[1] = (q_im[:tile] + q_re[tile:]).astype(BF)
+
+    return call(
+        body,
+        (slices * quarter // tile,),
+        [
+            spec((2, n, half), lambda i, ids: (0, 0, 0)),
+            spec((2, per, 1, quarter, n), lambda i, ids: (0, i, ids[0], 0, 0)),
+        ],
+        [((2, n // 2, half), BF, (2, tile, half), lambda i, ids: (0, i, 0))],
+        [],
+        (ids, phased, blocked),
+        4 * n * n * half,
+    )[0]
+
+
+def row_solve(ids, own, received, matrix, lens, omega, rows):
+    _, lines, half = own.shape
+    n = matrix.shape[-1]
+    slices = n // rows
+    quarter = rows // 2
+    tile = 2 * rows
+    tiles = n // tile
+
+    def body(ids, own_ref, rec_ref, mat, mat_half, len_ref, om, keep, send, phased, out, field):
+        i = pl.program_id(0)
+
+        @pl.when(i == 0)
+        def _():
+            for at, ref in enumerate((own_ref, rec_ref)):
+                to = pl.ds(pl.multiple_of((ids[0] ^ at) * half, half), half)
+                field[pl.ds(0, lines), to] = ref[0]
+                field[pl.ds(lines, lines), to] = ref[1]
+
+        @pl.when(i < tiles)
+        def _():
+            q_re = dot_lines(field[...], mat[0])
+            q_im = dot_lines(field[...], mat[1])
+            new_re = q_re[:lines] - q_im[lines:]
+            new_im = q_re[lines:] + q_im[:lines]
+            cols = pl.ds(pl.multiple_of(i * tile, tile), tile)
+            inner = pl.ds(pl.multiple_of((i % (half // tile)) * tile, tile), tile)
+            side = i // (half // tile)
+            first = ids[3] == 0
+            for s in range(slices):
+                at = ((ids[1] ^ side) * 2 + (ids[3] ^ (s % 2))) * 4 + (ids[2] ^ (s // 2))
+                sine, cosine = sin_cos(len_ref[at, :, inner] * (om[0] * TWO_OVER_PI))
+                lo = s * quarter
+                re, im = rotated(
+                    new_re[lo : lo + quarter], new_im[lo : lo + quarter], sine, cosine
+                )
+                phased[0, pl.ds(lo, quarter), cols] = re
+                phased[1, pl.ds(lo, quarter), cols] = im
+            for part, new in enumerate((new_re, new_im)):
+                for z in range(slices // 2):
+                    lo = 2 * z * quarter
+                    even = new[lo : lo + quarter].astype(BF)
+                    odd = new[lo + quarter : lo + 2 * quarter].astype(BF)
+                    keep[part, z, :, cols] = jnp.where(first, even, odd)
+                    send[part, z, :, cols] = jnp.where(first, odd, even)
+
+        @pl.when(i >= tiles)
+        def _():
+            left = phased[...].reshape(2 * lines, n)
+            q_re = dot_lines(left, mat_half[0])
+            q_im = dot_lines(left, mat_half[1])
+            cols = pl.ds(pl.multiple_of((i - tiles) * tile, tile), tile)
+            out[0, :, cols] = (q_re[:lines] - q_im[lines:]).astype(BF)
+            out[1, :, cols] = (q_re[lines:] + q_im[:lines]).astype(BF)
+
+    flat = lambda rank: (lambda i, ids: (0,) * rank)
+    part_shape = (2, slices // 2, quarter, n)
+    per_half = half // tile
+    return call(
+        body,
+        (tiles + per_half,),
+        [
+            spec(own.shape, flat(3)),
+            spec(own.shape, flat(3)),
+            spec((2, tile, n), lambda i, ids: (0, jnp.minimum(i, tiles - 1), 0)),
+            spec(
+                (2, tile, n),
+                lambda i, ids: (0, (1 - ids[0]) * per_half + jnp.maximum(i - tiles, 0), 0),
+            ),
+            spec(lens.shape, flat(3)),
+            SMEM,
+        ],
+        [
+            (part_shape, BF, part_shape, flat(4)),
+            (part_shape, BF, part_shape, flat(4)),
+            ((2, lines, n), BF, (2, lines, n), flat(3)),
+            ((2, lines, half), BF, (2, lines, half), flat(3)),
+        ],
+        [pltpu.VMEM((2 * lines, n), BF)],
+        (ids, own, received, matrix, matrix, lens, omega),
+        12 * n * n * half,
+    )
+
+
+def row_rest(ids, phased, matrix, rows):
+    _, lines, n = phased.shape
+    half = n // 2
+    tile = 2 * rows
+    per_half = half // tile
+
+    def body(ids, field, mat, out):
+        left = field[...].reshape(2 * lines, n)
+        q_re = dot_lines(left, mat[0])
+        q_im = dot_lines(left, mat[1])
+        out[0] = (q_re[:lines] - q_im[lines:]).astype(BF)
+        out[1] = (q_re[lines:] + q_im[:lines]).astype(BF)
+
+    return call(
+        body,
+        (per_half,),
+        [
+            spec(phased.shape, lambda i, ids: (0, 0, 0)),
+            spec((2, tile, n), lambda i, ids: (0, ids[0] * per_half + i, 0)),
+        ],
+        [((2, lines, half), BF, (2, lines, tile), lambda i, ids: (0, 0, i))],
+        [],
+        (ids, phased, matrix),
+        4 * n * n * half,
+    )[0]
+
+
+def last_solve(ids, turn, own, received, matrix, rows):
+    _, lines, half = own.shape
+    n = matrix.shape[-1]
+    slices = n // rows
+    quarter = rows // 2
+    tile = 2 * rows
+
+    def body(ids, own_ref, rec_ref, mat, m00, m01, m10, m11, field):
+        b = pl.program_id(0)
+
+        @pl.when(b == 0)
+        def _():
+            for at, ref in enumerate((own_ref, rec_ref)):
+                side = (ids[0] ^ at) * quarter
+                for part in range(2):
+                    for s in range(slices):
+                        to = pl.ds(pl.multiple_of(s * rows + side, quarter), quarter)
+                        field[part, to] = ref[part, pl.ds(s * quarter, quarter)]
+
+        left = mat[...].reshape(2 * tile, n)
+        q_re = dot_rows(left, field[0])
+        q_im = dot_rows(left, field[1])
+        new_re = (q_re[:tile] - q_im[tile:]).astype(BF)
+        new_im = q_im[:tile] + q_re[tile:]
+        first = ids[3] == 0
+        new_im = jnp.where(first, new_im, -new_im).astype(BF)
+        for at, (near, far) in enumerate(((m00, m10), (m01, m11))):
+
+            @pl.when(b == at)
+            def _(near=near, far=far):
+                for part, new in enumerate((new_re, new_im)):
+                    near[part] = jnp.where(first, new[:rows], new[rows:])
+                    far[part] = jnp.where(first, new[rows:], new[:rows])
+
+    message = ((2, rows, half), BF, (2, rows, half), lambda b, ids: (0, 0, 0))
+    return call(
+        body,
+        (2,),
+        [
+            spec(own.shape, lambda b, ids: (0, 0, 0)),
+            spec(own.shape, lambda b, ids: (0, 0, 0)),
+            spec((2, tile, n), lambda b, ids: (0, (ids[0] ^ b) * 2 + (ids[4] ^ turn), 0)),
+        ],
+        [message] * 4,
+        [pltpu.VMEM((2, n, half), BF)],
+        (ids, own, received, matrix),
+        4 * n * n * half,
+    )
+
+
+def arrive(ids, messages, image_weights, freqs):
+    _, rows, half = messages[0].shape
+
+    def body(ids, *refs):
+        ms, (wt, src, rec, grad, held, sems) = refs[:8], refs[8:]
+        copies = [
+            pltpu.make_async_copy(m, held.at[at], sems.at[at]) for at, m in enumerate(ms)
+        ]
+        for copy in copies:
+            copy.start()
+        for copy in copies:
+            copy.wait()
+        for side in range(2):
+            total = None
+            for j in range(freqs):
+                a_hi = ids[4] ^ j
+                b = ids[5] ^ side
+                s_at = (a_hi * 2 + ids[3]) * 2 + b
+                r_at = (a_hi * 2 + (1 - ids[3])) * 2 + b
+                s, r = held[s_at], held[r_at]
+                cols = pl.ds(side * half, half)
+                src[:, j, :, cols] = s
+                rec[:, j, :, cols] = r
+                s, r = s.astype(F32), r.astype(F32)
+                term = wt[j] * (s[0] * r[0] + s[1] * r[1])
+                total = term if total is None else total + term
+            grad[:, pl.ds(side * half, half)] = total.astype(BF)
+
+    flat = lambda rank: (lambda i, ids: (0,) * rank)
+    full = (2, freqs, rows, 2 * half)
+    return call(
+        body,
+        (1,),
+        [ANY] * 8 + [SMEM],
+        [
+            (full, BF, full, flat(4)),
+            (full, BF, full, flat(4)),
+            ((rows, 2 * half), BF, (rows, 2 * half), flat(2)),
+        ],
+        [pltpu.VMEM((8, 2, rows, half), BF), pltpu.SemaphoreType.DMA((8,))],
+        (ids, *messages, image_weights),
+        1 << 22,
+    )
+
+
+def flip(size, bit):
+    return [(i, i ^ bit) for i in range(size)]
+
+
+def scatter_rounds(groups, space, back):
+    rounds = []
+    for a in range(4):
+        for b in range(2):
+            perm = []
+            for x in range(groups // 2):
+                for c in range(2):
+                    for s in range(space):
+                        home = (2 * x + c) * space + s
+                        away = (2 * x + ((s // 4) ^ b)) * space + 4 * c + ((s % 4) ^ a)
+                        perm.append((away, home) if back else (home, away))
+            rounds.append(perm)
+    return rounds
+
+
+def plane_per_chip(source, receiver, matrix, lens, omegas, image_weights):
+    groups, space = lax.axis_size("freq"), lax.axis_size("space")
+    both = ("freq", "space")
+    _, freqs, rows, cols = source.shape
+    half, quarter = cols // 2, rows // 2
+    group, s = lax.axis_index("freq"), lax.axis_index("space")
+    core, x, z, y = group % 2, group // 2, s // 2, s % 2
+    ids = jnp.stack([core, x, z, y, z % 2, z // 2]).astype(jnp.int32)
+    swap = flip(groups, 1)
+
+    mine = core == z // 2
+    scalars = jnp.stack([omegas, image_weights])
+    other = lax.ppermute(scalars, "freq", swap)
+    omega, weight = jnp.where(mine, scalars, other)[:, z % 2]
+    omega = omega.reshape(1)
+
+    going, coming = scatter_rounds(groups, space, False), scatter_rounds(groups, space, True)
+    messages = []
+    for turn in range(2):
+        sent = home_solve(ids, turn, source, receiver, matrix, lens, omegas)
+        for at, m in enumerate(sent):
+            messages.append(lax.ppermute(m, both, going[4 * turn + at]))
+
+    stacks = []
+    for depth, (r0, c0) in ((1, (x * quarter, core * half)), (2, (core * quarter, x * half))):
+        piece = lax.dynamic_slice(lens, (depth, r0, c0), (1, quarter, half))
+        line = jnp.concatenate(
+            [piece] + [lax.ppermute(piece, "space", flip(space, 2 * k)) for k in (1, 2, 3)]
+        )
+        plane = jnp.concatenate([line, lax.ppermute(line, "space", flip(space, 1))])
+        stacks.append(jnp.concatenate([plane, lax.ppermute(plane, "freq", flip(groups, 2))]))
+
+    held = lax.dynamic_slice(matrix, (0, z % 2, 0, 0), (2, 1, cols, cols))[:, 0]
+    line_matrix = jnp.where(mine, held, lax.ppermute(held, "freq", swap))
+
+    keep0, send0, phased, sent = column_solve(ids, messages, line_matrix, stacks[0], omega)
+    came = lax.ppermute(sent, "freq", swap)
+    own = column_rest(ids, phased, line_matrix, rows)
+    partner0 = lax.ppermute(send0, "space", flip(space, 1))
+    keep1, send1, phased, sent = row_solve(
+        ids, own, came, line_matrix, stacks[1], omega, rows
+    )
+    came = lax.ppermute(sent, "freq", swap)
+    own = row_rest(ids, phased, line_matrix, rows)
+    partner1 = lax.ppermute(send1, "space", flip(space, 1))
+
+    finals = []
+    for turn in range(2):
+        sent = last_solve(ids, turn, own, came, line_matrix, rows)
+        for at, m in enumerate(sent):
+            finals.append(lax.ppermute(m, both, coming[4 * turn + at]))
+
+    def product(a, b):
+        a, b = a.astype(F32), b.astype(F32)
+        return weight * (a[0] * b[0] - a[1] * b[1])
+
+    term0 = product(keep0, partner0)
+    term1 = product(keep1, partner1)
+    halves0 = term0.reshape(-1, 2, quarter, half)
+    halves1 = jnp.moveaxis(term1.reshape(-1, quarter, 2, half), 2, 1)
+    halves = jnp.stack([halves0, halves1], axis=1)
+
+    def side(v, at):
+        return lax.dynamic_index_in_dim(v, at, 2, keepdims=False)
+
+    over_x = side(halves, x) + lax.ppermute(
+        side(halves, 1 - x).astype(BF), "freq", flip(groups, 2)
+    ).astype(F32)
+
+    def slab(at):
+        return lax.dynamic_index_in_dim(over_x, at, 0, keepdims=False)
+
+    total = slab(z)
+    for k in (1, 2, 3):
+        total = total + lax.ppermute(slab(z ^ k).astype(BF), "space", flip(space, 2 * k)).astype(F32)
+    piece = total.astype(BF)
+    pair = jnp.stack([piece, lax.ppermute(piece, "freq", swap)])
+    quad = jnp.stack([pair, lax.ppermute(pair, "freq", flip(groups, 2))])
+
+    def at_of(px, pc, depth):
+        return lax.dynamic_slice(
+            quad, (x ^ px, core ^ pc, depth, 0, 0), (1, 1, 1, quarter, half)
+        )[0, 0, 0].astype(F32)
+
+    grad0 = jnp.block([[at_of(0, 0, 0), at_of(0, 1, 0)], [at_of(1, 0, 0), at_of(1, 1, 0)]])
+    grad1 = jnp.block([[at_of(0, 0, 1), at_of(1, 0, 1)], [at_of(0, 1, 1), at_of(1, 1, 1)]])
+
+    source_out, receiver_out, term2 = arrive(ids, finals, image_weights, freqs)
+    chip = term2.astype(F32) + lax.ppermute(term2, "freq", swap).astype(F32)
+    grad2 = chip + lax.ppermute(chip.astype(BF), "freq", flip(groups, 2)).astype(F32)
+    return source_out, receiver_out, jnp.stack([grad0, grad1, grad2])
 
 
 def to_blocks(matrix, pieces):
@@ -73,7 +636,7 @@
     return stacked
 
 
-def on_device(source_field, receiver_field, line_inverse, lens_delay, omegas, image_weights):
+def general(source_field, receiver_field, line_inverse, lens_delay, omegas, image_weights):
     pieces = lax.axis_size("space")
     local_rows = lens_delay.shape[1]
     depth_count = lens_delay.shape[0]
@@ -118,6 +681,14 @@
     return (final_fields[0], final_fields[1], gradient)
 
 
+def on_device(source_field, receiver_field, line_inverse, lens_delay, omegas, image_weights):
+    args = (source_field, receiver_field, line_inverse, lens_delay, omegas, image_weights)
+    groups, space = lax.axis_size("freq"), lax.axis_size("space")
+    freqs, depths = omegas.shape[0], lens_delay.shape[0]
+    fits = space == 2 * 2 * freqs and freqs == 2 and groups % 4 == 0 and depths == 3
+    return plane_per_chip(*args) if fits else general(*args)
+
+
 def solution(mesh):
     placed = (
         P(None, "freq", "space", None),

time: 659 us -> 248 us (0.38); the launches traced: 649 us -> 247 us
  blocking collectives: 258 us -> 0 us
  local copies, waits for them, and re-layouts: 120 us -> 21.1 us
  Pallas kernels: 0 us -> 79.1 us
  waiting for transfers between devices: 134 us -> 69.5 us
  matrix products: 63.2 us -> 0 us
  starting transfers between devices: 16.9 us -> 58.8 us
  other arithmetic: 41.5 us -> 17.5 us
  between operations: 15.3 us -> 1.07 us
    all_to_all x5 -> x0, blocking collectives: 258 us -> none  [the longest x3 155 us: march_step(): lax.all_to_all(to_blocks(across, pieces), 'space', split_axis=3, concat_a...]
    all_to_all x3 -> x0, waiting for transfers between devices: 100 us -> none  [the longest x1 43.1 us: on_device(): lax.all_to_all(to_blocks(solved.astype(jnp.bfloat16), pieces), 'space', s...]
    reshape x31 -> x0, local copies, waits for them, and re-layouts: 83.8 us -> none  [the longest x14 40.7 us: to_blocks(): return arranged.reshape(leading + (pieces, local_rows * columns))]
    pallas_call x0 -> x9, Pallas kernels: none -> 79.1 us  [call(): pl.pallas_call(body, out_shape=[jax.ShapeDtypeStruct(s, d) for s, d, _, _...]
    ppermute x0 -> x40, waiting for transfers between devices: none -> 69.5 us  [the longest x8 17.3 us: plane_per_chip(): messages.append(lax.ppermute(m, both, going[4 * turn + at]))]
    dot_general x12 -> x0, matrix products: 63.2 us -> none  [the longest x6 31.8 us: line_solve(): jnp.einsum('fij,wpfrj->wpfri', line_inverse[0], fields, preferred_element...]
    ppermute x0 -> x40, starting transfers between devices: none -> 58.8 us  [the longest x8 12.2 us: plane_per_chip(): messages.append(lax.ppermute(m, both, going[4 * turn + at]))]
    psum x1 -> x0, waiting for transfers between devices: 34 us -> none  [reduce_slice(): return lax.psum(image_term.astype(jnp.bfloat16), 'freq').astype(jnp.float32)]
  transfers between devices with their start and end apart: 4 -> 40, of which waited for: 4 -> 14; matrix products, arithmetic and copies ran while one was open for 3% -> 11% of each run, Pallas kernels for 0% -> 32%
where the time goes in v1:
time: 248 us; the launch traced here: 247 us
  Pallas kernels  79.1 us (32%)
  waiting for transfers between devices  69.5 us (28%)
  starting transfers between devices  58.8 us (24%)
  local copies, waits for them, and re-layouts  21.1 us (9%)
  other arithmetic  17.5 us (7%)
    pallas_call x9, Pallas kernels, call(): pl.pallas_call(body, out_shape=[jax.ShapeDtypeStruct(s, d) for s, d, _, _...  79.1 us
    ppermute x8, waiting for transfers between devices, plane_per_chip(): messages.append(lax.ppermute(m, both, going[4 * turn + at]))  17.3 us
    ppermute x8, waiting for transfers between devices, plane_per_chip(): finals.append(lax.ppermute(m, both, coming[4 * turn + at]))  13.6 us
    ppermute x2, waiting for transfers between devices, plane_per_chip(): plane = jnp.concatenate([line, lax.ppermute(line, 'space', flip(space, 1))])  12.4 us
    ppermute x8, starting transfers between devices, plane_per_chip(): messages.append(lax.ppermute(m, both, going[4 * turn + at]))  12.2 us
    ppermute x8, starting transfers between devices, plane_per_chip(): finals.append(lax.ppermute(m, both, coming[4 * turn + at]))  11.2 us
    ppermute x3, waiting for transfers between devices, plane_per_chip(): lax.ppermute(slab(z ^ k).astype(BF), 'space', flip(space, 2 * k))  11.1 us
    unnamed x66, local copies, waits for them, and re-layouts  10.7 us
  transfers between devices with their start and end apart: 40, of which 14 were waited for; matrix products, arithmetic and copies ran while one was open for 11% of the time, Pallas kernels for 32%

profile of v1, /device:TPU:0, one launch (start us, length us, event | category | flops | bytes accessed | tf_op | source)
XLA Modules:
  0.0 246.9 jit_solution(11882810458353172869)
XLA Ops:
  0.7 4.7 %dynamic-slice_bitcast_fusion = bf16[2,1024,1024]{2,1,0:T(8,128)(2,1)} fusion(bf16[2,2,1024,1024]{3,2,1,0:T(8,128)(2,1)} %mat.3, s32[]{:T(128)S(6)} %select_n.111), kind=kLoop, calls=%fused_computation | loop fusion | bytes 8388612 | tf_op jit(solution)/shard_map/squeeze | solution.py:509
  7.5 4.6 %collective-permute-start.11 = (f32[1,64,512]{2,1,0:T(8,128)S(1)}, f32[1,64,512]{2,1,0:T(8,128)S(1)}, u32[]{:S(2)}, u32[]{:S(2)}) collective-permute-start(f32[1,64,512]{2,1,0:T(8,128)S(1)} %get-tuple-element.62), channel_id=1, source_target_pairs={{0,6},{1,7},{2,4},{3,5},{4,2},{5,3},{6,0},{7,1},{8,14},{9,15},{10,... | collective-permute-start | bytes 393224 | tf_op jit(solution)/shard_map/ppermute | solution.py:504
  12.7 3.8 %collective-permute-start.18 = (f32[1,64,512]{2,1,0:T(8,128)S(1)}, f32[1,64,512]{2,1,0:T(8,128)S(1)}, u32[]{:S(2)}, u32[]{:S(2)}) collective-permute-start(f32[1,64,512]{2,1,0:T(8,128)S(1)} %get-tuple-element.58), channel_id=1, source_target_pairs={{0,6},{1,7},{2,4},{3,5},{4,2},{5,3},{6,0},{7,1},{8,14},{9,15},{10,... | collective-permute-start | bytes 393224 | tf_op jit(solution)/shard_map/ppermute | solution.py:504
  17.2 7.6 %shard_map.86 = (bf16[2,128,512]{2,1,0:T(8,128)(2,1)}, bf16[2,128,512]{2,1,0:T(8,128)(2,1)}, bf16[2,128,512]{2,1,0:T(8,128)(2,1)}, bf16[2,128,512]{2,1,0:T(8,128)(2,1)}) custom-call(s32[6]{0:T(128)} %stack.78.ids, bf16[2,2,128,1024]{3,2,1,0:T(8,128)(2,1)} %src.3, bf16[2,2,128,1024]{3,2,1,0:T(8,128)(2,1)} %rec.3, bf16[2,2,1024,1024]{3,2,1,0:T(8,128)(2,1)} %mat.3, ...), custom_call_target="tpu_custom_call" | custom-call | flops 2147483648 | bytes 8388608 | tf_op jit(solution)/shard_map/pallas_call | solution.py:48
  28.8 7.4 %shard_map.85 = (bf16[2,128,512]{2,1,0:T(8,128)(2,1)}, bf16[2,128,512]{2,1,0:T(8,128)(2,1)}, bf16[2,128,512]{2,1,0:T(8,128)(2,1)}, bf16[2,128,512]{2,1,0:T(8,128)(2,1)}) custom-call(s32[6]{0:T(128)} %stack.78.ids, bf16[2,2,128,1024]{3,2,1,0:T(8,128)(2,1)} %src.3, bf16[2,2,128,1024]{3,2,1,0:T(8,128)(2,1)} %rec.3, bf16[2,2,1024,1024]{3,2,1,0:T(8,128)(2,1)} %mat.3, ...), custom_call_target="tpu_custom_call" | custom-call | flops 2147483648 | bytes 8388608 | tf_op jit(solution)/shard_map/pallas_call | solution.py:48
  50.4 10.5 %collective-permute-done.19 = f32[4,64,512]{2,1,0:T(8,128)S(1)} collective-permute-done((f32[4,64,512]{2,1,0:T(8,128)S(1)}, f32[4,64,512]{2,1,0:T(8,128)S(1)}, u32[]{:S(2)}, u32[]{:S(2)}) %collective-permute-start.19) | collective-permute-done | bytes 524320 | tf_op jit(solution)/shard_map/ppermute | solution.py:506
  62.3 4.9 %collective-permute-done.13 = f32[8,64,512]{2,1,0:T(8,128)S(1)} collective-permute-done((f32[8,64,512]{2,1,0:T(8,128)}, f32[8,64,512]{2,1,0:T(8,128)S(1)}, u32[]{:S(2)}, u32[]{:S(2)}) %collective-permute-start.13) | collective-permute-done | bytes 1048608 | tf_op jit(solution)/shard_map/ppermute | solution.py:507
  71.4 3.6 %collective-permute-start.1 = (bf16[2,128,512]{2,1,0:T(8,128)(2,1)S(1)}, bf16[2,128,512]{2,1,0:T(8,128)(2,1)S(1)}, u32[]{:S(2)}, u32[]{:S(2)}) collective-permute-start(bf16[2,128,512]{2,1,0:T(8,128)(2,1)S(1)} %copy-done.17), channel_id=1, source_target_pairs={{0,8},{1,9},{2,10},{3,11},{4,0},{5,1},{6,2},{7,3},{8,12},{9,13},{1... | collective-permute-start | bytes 786440 | tf_op jit(solution)/shard_map/ppermute | solution.py:498
  77.4 4.7 %broadcast_select_fusion.refs_8_.mat.mat_half = bf16[2,1024,1024]{2,1,0:T(8,128)(2,1)} fusion(bf16[2,1024,1024]{2,1,0:T(8,128)(2,1)} %collective-permute-done.8, pred[]{:T(512)S(6)} %eq.9, bf16[2,2,1024,1024]{3,2,1,0:T(8,128)(2,1)} %mat.3, s32[]{:T(128)S(6)} %select_n.111), kind=kLoop, calls=%fused_computation.1 | loop fusion | flops 2097152 | bytes 12582917 | tf_op jit(solution)/shard_map/jit(_where)/select_n | solution.py:510
  83.6 11.8 %collective-permute-done.1.refs_1_ = bf16[2,128,512]{2,1,0:T(8,128)(2,1)S(1)} collective-permute-done((bf16[2,128,512]{2,1,0:T(8,128)(2,1)S(1)}, bf16[2,128,512]{2,1,0:T(8,128)(2,1)S(1)}, u32[]{:S(2)}, u32[]{:S(2)}) %collective-permute-start.1) | collective-permute-done | bytes 262176 | tf_op jit(solution)/shard_map/ppermute | solution.py:498
  95.4 5.6 %collective-permute-done.3.refs_3_ = bf16[2,128,512]{2,1,0:T(8,128)(2,1)S(1)} collective-permute-done((bf16[2,128,512]{2,1,0:T(8,128)(2,1)S(1)}, bf16[2,128,512]{2,1,0:T(8,128)(2,1)S(1)}, u32[]{:S(2)}, u32[]{:S(2)}) %collective-permute-start.3) | collective-permute-done | bytes 262176 | tf_op jit(solution)/shard_map/ppermute | solution.py:498
  101.7 17.9 %shard_map.87 = (bf16[2,4,128,512]{3,2,1,0:T(8,128)(2,1)}, bf16[2,4,128,512]{3,2,1,0:T(8,128)(2,1)}, bf16[2,1024,512]{2,1,0:T(8,128)(2,1)}, bf16[2,512,512]{2,1,0:T(8,128)(2,1)}) custom-call(s32[6]{0:T(128)} %stack.78.ids, bf16[2,128,512]{2,1,0:T(8,128)(2,1)} %copy-done.25, bf16[2,128,512]{2,1,0:T(8,128)(2,1)} %copy-done.26, ...), custom_call_target="tpu_custom_call" | custom-call | flops 6442450944 | bytes 8388608 | tf_op jit(solution)/shard_map/pallas_call | solution.py:48
  122.3 5.9 %shard_map.88.own_ref = bf16[2,512,512]{2,1,0:T(8,128)(2,1)} custom-call(s32[6]{0:T(128)} %stack.78.ids, bf16[2,1024,512]{2,1,0:T(8,128)(2,1)} %get-tuple-element.38.field, bf16[2,8,2,64,1024]{4,3,2,1,0:T(8,128)(2,1)} %bitcast.81), custom_call_target="tpu_custom_call" | custom-call | flops 2147483648 | bytes 8388608 | tf_op jit(solution)/shard_map/pallas_call | solution.py:48
  129.2 17.1 %shard_map.89 = (bf16[2,4,64,1024]{3,2,1,0:T(8,128)(2,1)}, bf16[2,4,64,1024]{3,2,1,0:T(8,128)(2,1)}, bf16[2,512,1024]{2,1,0:T(8,128)(2,1)}, bf16[2,512,512]{2,1,0:T(8,128)(2,1)}) custom-call(s32[6]{0:T(128)} %stack.78.ids, bf16[2,512,512]{2,1,0:T(8,128)(2,1)} %shard_map.88.own_ref, bf16[2,512,512]{2,1,0:T(8,128)(2,1)} %copy-done.12, ...), custom_call_target="tpu_custom_call" | custom-call | flops 6442450944 | bytes 8388608 | tf_op jit(solution)/shard_map/pallas_call | solution.py:48
  152.7 6.0 %shard_map.90.own_ref = bf16[2,512,512]{2,1,0:T(8,128)(2,1)} custom-call(s32[6]{0:T(128)} %stack.78.ids, bf16[2,512,1024]{2,1,0:T(8,128)(2,1)} %get-tuple-element.40.field, bf16[2,1024,1024]{2,1,0:T(8,128)(2,1)} %broadcast_select_fusion.refs_8_.mat.mat_half), custom_call_target="tpu_custom_call" | custom-call | flops 2147483648 | bytes 8388608 | tf_op jit(solution)/shard_map/pallas_call | solution.py:48
  161.3 6.4 %shard_map.92 = (bf16[2,128,512]{2,1,0:T(8,128)(2,1)}, bf16[2,128,512]{2,1,0:T(8,128)(2,1)}, bf16[2,128,512]{2,1,0:T(8,128)(2,1)}, bf16[2,128,512]{2,1,0:T(8,128)(2,1)}) custom-call(s32[6]{0:T(128)} %stack.78.ids, bf16[2,512,512]{2,1,0:T(8,128)(2,1)} %shard_map.90.own_ref, bf16[2,512,512]{2,1,0:T(8,128)(2,1)} %collective-permute-done.21.rec_ref, ...), custom_call_target="tpu_custom_call" | custom-call | flops 2147483648 | bytes 8388608 | tf_op jit(solution)/shard_map/pallas_call | solution.py:48
  180.1 6.3 %shard_map.91 = (bf16[2,128,512]{2,1,0:T(8,128)(2,1)}, bf16[2,128,512]{2,1,0:T(8,128)(2,1)}, bf16[2,128,512]{2,1,0:T(8,128)(2,1)}, bf16[2,128,512]{2,1,0:T(8,128)(2,1)}) custom-call(s32[6]{0:T(128)} %stack.78.ids, bf16[2,512,512]{2,1,0:T(8,128)(2,1)} %shard_map.90.own_ref, bf16[2,512,512]{2,1,0:T(8,128)(2,1)} %collective-permute-done.21.rec_ref, ...), custom_call_target="tpu_custom_call" | custom-call | flops 2147483648 | bytes 8388608 | tf_op jit(solution)/shard_map/pallas_call | solution.py:48
  190.7 4.7 %collective-permute-done.28.refs_6_ = bf16[2,128,512]{2,1,0:T(8,128)(2,1)} collective-permute-done((bf16[2,128,512]{2,1,0:T(8,128)(2,1)}, bf16[2,128,512]{2,1,0:T(8,128)(2,1)}, u32[]{:S(2)}, u32[]{:S(2)}) %collective-permute-start.28) | collective-permute-done | bytes 262176 | tf_op jit(solution)/shard_map/ppermute | solution.py:527
  197.7 7.0 %collective-permute-done.24.refs_2_ = bf16[2,128,512]{2,1,0:T(8,128)(2,1)} collective-permute-done((bf16[2,128,512]{2,1,0:T(8,128)(2,1)}, bf16[2,128,512]{2,1,0:T(8,128)(2,1)}, u32[]{:S(2)}, u32[]{:S(2)}) %collective-permute-start.24) | collective-permute-done | bytes 262176 | tf_op jit(solution)/shard_map/ppermute | solution.py:527
  204.7 4.4 %shard_map.93 = (bf16[2,2,128,1024]{3,2,1,0:T(8,128)(2,1)}, bf16[2,2,128,1024]{3,2,1,0:T(8,128)(2,1)}, bf16[128,1024]{1,0:T(8,128)(2,1)}) custom-call(s32[6]{0:T(128)} %stack.78.ids, bf16[2,128,512]{2,1,0:T(8,128)(2,1)} %copy-done.5, bf16[2,128,512]{2,1,0:T(8,128)(2,1)} %copy-done.6, bf16[2,128,512]{2,1,0:T(8,128)(2,1)} %collective-permute-done.24.refs_2_, ...), custom_call_target="tpu_custom_call" | custom-call | flops 4194304 | bytes 8388608 | tf_op jit(solution)/shard_map/pallas_call | solution.py:48
  209.2 10.6 %collective-permute-start.38 = (bf16[128,1024]{1,0:T(8,128)(2,1)}, bf16[128,1024]{1,0:T(8,128)(2,1)S(1)}, u32[]{:S(2)}, u32[]{:S(2)}) collective-permute-start(bf16[128,1024]{1,0:T(8,128)(2,1)} %get-tuple-element.56), channel_id=1, source_target_pairs={{0,8},{8,0},{16,24},{24,16},{1,9},{9,1},{17,25},{25,17},{2,10},{10... | collective-permute-start | bytes 786440 | tf_op jit(solution)/shard_map/ppermute | solution.py:565
  225.5 4.2 %collective-permute-done.35 = bf16[2,64,512]{2,1,0:T(8,128)(2,1)S(1)} collective-permute-done((bf16[2,64,512]{2,1,0:T(8,128)(2,1)S(1)}, bf16[2,64,512]{2,1,0:T(8,128)(2,1)S(1)}, u32[]{:S(2)}, u32[]{:S(2)}) %collective-permute-start.35) | collective-permute-done | bytes 131104 | tf_op jit(solution)/shard_map/ppermute | solution.py:551
  229.8 5.6 %collective-permute-done.34 = bf16[2,64,512]{2,1,0:T(8,128)(2,1)S(1)} collective-permute-done((bf16[2,64,512]{2,1,0:T(8,128)(2,1)S(1)}, bf16[2,64,512]{2,1,0:T(8,128)(2,1)S(1)}, u32[]{:S(2)}, u32[]{:S(2)}) %collective-permute-start.34) | collective-permute-done | bytes 131104 | tf_op jit(solution)/shard_map/ppermute | solution.py:551
  238.1 7.2 %collective-permute-done.37 = bf16[2,2,64,512]{3,2,1,0:T(8,128)(2,1)S(1)} collective-permute-done((bf16[2,2,64,512]{3,2,1,0:T(8,128)(2,1)S(1)}, bf16[2,2,64,512]{3,2,1,0:T(8,128)(2,1)S(1)}, u32[]{:S(2)}, u32[]{:S(2)}) %collective-permute-start.37) | collective-permute-done | bytes 262176 | tf_op jit(solution)/shard_map/ppermute | solution.py:554
  (164 shorter events, 73.5 us)
Async XLA Ops:
  5.3 70.3 %collective-permute-start.8 = (bf16[2,1024,1024]{2,1,0:T(8,128)(2,1)}, bf16[2,1024,1024]{2,1,0:T(8,128)(2,1)}, u32[]{:S(2)}, u32[]{:S(2)}) collective-permute-start(bf16[2,1024,1024]{2,1,0:T(8,128)(2,1)} %dynamic-slice_bitcast_fusion), channel_id=1, source_target_pairs={{0,8},{8,0},{16,24},{24,16},{1,9},{9,1},{17,25},{25,17},{2,10},{10... | collective-permute-start | bytes 12582920 | tf_op jit(solution)/shard_map/ppermute | solution.py:510
  7.5 18.0 %collective-permute-start.11 = (f32[1,64,512]{2,1,0:T(8,128)S(1)}, f32[1,64,512]{2,1,0:T(8,128)S(1)}, u32[]{:S(2)}, u32[]{:S(2)}) collective-permute-start(f32[1,64,512]{2,1,0:T(8,128)S(1)} %get-tuple-element.62), channel_id=1, source_target_pairs={{0,6},{1,7},{2,4},{3,5},{4,2},{5,3},{6,0},{7,1},{8,14},{9,15},{10,... | collective-permute-start | bytes 393224 | tf_op jit(solution)/shard_map/ppermute | solution.py:504
  12.1 15.0 %collective-permute-start.10 = (f32[1,64,512]{2,1,0:T(8,128)S(1)}, f32[1,64,512]{2,1,0:T(8,128)S(1)}, u32[]{:S(2)}, u32[]{:S(2)}) collective-permute-start(f32[1,64,512]{2,1,0:T(8,128)S(1)} %get-tuple-element.62), channel_id=1, source_target_pairs={{0,4},{1,5},{2,6},{3,7},{4,0},{5,1},{6,2},{7,3},{8,12},{9,13},{10,... | collective-permute-start | bytes 393224 | tf_op jit(solution)/shard_map/ppermute | solution.py:504
  12.1 15.0 %collective-permute-start.9 = (f32[1,64,512]{2,1,0:T(8,128)S(1)}, f32[1,64,512]{2,1,0:T(8,128)S(1)}, u32[]{:S(2)}, u32[]{:S(2)}) collective-permute-start(f32[1,64,512]{2,1,0:T(8,128)S(1)} %get-tuple-element.62), channel_id=1, source_target_pairs={{0,2},{1,3},{2,0},{3,1},{4,6},{5,7},{6,4},{7,5},{8,10},{9,11},{10,... | collective-permute-start | bytes 393224 | tf_op jit(solution)/shard_map/ppermute | solution.py:504
  12.7 30.3 %collective-permute-start.18 = (f32[1,64,512]{2,1,0:T(8,128)S(1)}, f32[1,64,512]{2,1,0:T(8,128)S(1)}, u32[]{:S(2)}, u32[]{:S(2)}) collective-permute-start(f32[1,64,512]{2,1,0:T(8,128)S(1)} %get-tuple-element.58), channel_id=1, source_target_pairs={{0,6},{1,7},{2,4},{3,5},{4,2},{5,3},{6,0},{7,1},{8,14},{9,15},{10,... | collective-permute-start | bytes 393224 | tf_op jit(solution)/shard_map/ppermute | solution.py:504
  25.5 19.2 %collective-permute-start.17 = (f32[1,64,512]{2,1,0:T(8,128)S(1)}, f32[1,64,512]{2,1,0:T(8,128)S(1)}, u32[]{:S(2)}, u32[]{:S(2)}) collective-permute-start(f32[1,64,512]{2,1,0:T(8,128)S(1)} %get-tuple-element.58), channel_id=1, source_target_pairs={{0,4},{1,5},{2,6},{3,7},{4,0},{5,1},{6,2},{7,3},{8,12},{9,13},{10,... | collective-permute-start | bytes 393224 | tf_op jit(solution)/shard_map/ppermute | solution.py:504
  27.1 19.0 %collective-permute-start.16 = (f32[1,64,512]{2,1,0:T(8,128)S(1)}, f32[1,64,512]{2,1,0:T(8,128)S(1)}, u32[]{:S(2)}, u32[]{:S(2)}) collective-permute-start(f32[1,64,512]{2,1,0:T(8,128)S(1)} %get-tuple-element.58), channel_id=1, source_target_pairs={{0,2},{1,3},{2,0},{3,1},{4,6},{5,7},{6,4},{7,5},{8,10},{9,11},{10,... | collective-permute-start | bytes 393224 | tf_op jit(solution)/shard_map/ppermute | solution.py:504
  41.4 25.8 %collective-permute-start.13 = (f32[8,64,512]{2,1,0:T(8,128)}, f32[8,64,512]{2,1,0:T(8,128)S(1)}, u32[]{:S(2)}, u32[]{:S(2)}) collective-permute-start(f32[8,64,512]{2,1,0:T(8,128)} %get-tuple-element.75), channel_id=1, source_target_pairs={{0,16},{8,24},{16,0},{24,8},{1,17},{9,25},{17,1},{25,9},{2,18},{10... | collective-permute-start | bytes 3145736 | tf_op jit(solution)/shard_map/ppermute | solution.py:507
  43.0 27.7 %collective-permute-start.4 = (bf16[2,128,512]{2,1,0:T(8,128)(2,1)S(1)}, bf16[2,128,512]{2,1,0:T(8,128)(2,1)S(1)}, u32[]{:S(2)}, u32[]{:S(2)}) collective-permute-start(bf16[2,128,512]{2,1,0:T(8,128)(2,1)S(1)} %copy-done.20), channel_id=1, source_target_pairs={{0,2},{1,3},{2,0},{3,1},{4,10},{5,11},{6,8},{7,9},{8,6},{9,7},{10,... | collective-permute-start | bytes 786440 | tf_op jit(solution)/shard_map/ppermute | solution.py:498
  44.8 26.6 %collective-permute-start.5 = (bf16[2,128,512]{2,1,0:T(8,128)(2,1)S(1)}, bf16[2,128,512]{2,1,0:T(8,128)(2,1)S(1)}, u32[]{:S(2)}, u32[]{:S(2)}) collective-permute-start(bf16[2,128,512]{2,1,0:T(8,128)(2,1)S(1)} %copy-done.19), channel_id=1, source_target_pairs={{0,10},{1,11},{2,8},{3,9},{4,2},{5,3},{6,0},{7,1},{8,14},{9,15},{1... | collective-permute-start | bytes 786440 | tf_op jit(solution)/shard_map/ppermute | solution.py:498
  46.1 14.7 %collective-permute-start.19 = (f32[4,64,512]{2,1,0:T(8,128)S(1)}, f32[4,64,512]{2,1,0:T(8,128)S(1)}, u32[]{:S(2)}, u32[]{:S(2)}) collective-permute-start(f32[4,64,512]{2,1,0:T(8,128)S(1)} %pad_maximum_fusion.2), channel_id=1, source_target_pairs={{0,1},{1,0},{2,3},{3,2},{4,5},{5,4},{6,7},{7,6},{8,9},{9,8},{10,11... | collective-permute-start | bytes 1572872 | tf_op jit(solution)/shard_map/ppermute | solution.py:506
  67.2 14.8 %collective-permute-start.7 = (bf16[2,128,512]{2,1,0:T(8,128)(2,1)S(1)}, bf16[2,128,512]{2,1,0:T(8,128)(2,1)S(1)}, u32[]{:S(2)}, u32[]{:S(2)}) collective-permute-start(bf16[2,128,512]{2,1,0:T(8,128)(2,1)S(1)} %copy-done.13), channel_id=1, source_target_pairs={{0,11},{1,10},{2,9},{3,8},{4,3},{5,2},{6,1},{7,0},{8,15},{9,14},{1... | collective-permute-start | bytes 786440 | tf_op jit(solution)/shard_map/ppermute | solution.py:498
  71.4 24.0 %collective-permute-start.1 = (bf16[2,128,512]{2,1,0:T(8,128)(2,1)S(1)}, bf16[2,128,512]{2,1,0:T(8,128)(2,1)S(1)}, u32[]{:S(2)}, u32[]{:S(2)}) collective-permute-start(bf16[2,128,512]{2,1,0:T(8,128)(2,1)S(1)} %copy-done.17), channel_id=1, source_target_pairs={{0,8},{1,9},{2,10},{3,11},{4,0},{5,1},{6,2},{7,3},{8,12},{9,13},{1... | collective-permute-start | bytes 786440 | tf_op jit(solution)/shard_map/ppermute | solution.py:498
  75.0 20.4 %collective-permute-start.2 = (bf16[2,128,512]{2,1,0:T(8,128)(2,1)S(1)}, bf16[2,128,512]{2,1,0:T(8,128)(2,1)S(1)}, u32[]{:S(2)}, u32[]{:S(2)}) collective-permute-start(bf16[2,128,512]{2,1,0:T(8,128)(2,1)S(1)} %copy-done.15), channel_id=1, source_target_pairs={{0,1},{1,0},{2,3},{3,2},{4,9},{5,8},{6,11},{7,10},{8,5},{9,4},{10,... | collective-permute-start | bytes 786440 | tf_op jit(solution)/shard_map/ppermute | solution.py:498
  75.6 25.3 %collective-permute-start.3 = (bf16[2,128,512]{2,1,0:T(8,128)(2,1)S(1)}, bf16[2,128,512]{2,1,0:T(8,128)(2,1)S(1)}, u32[]{:S(2)}, u32[]{:S(2)}) collective-permute-start(bf16[2,128,512]{2,1,0:T(8,128)(2,1)S(1)} %copy-done.14), channel_id=1, source_target_pairs={{0,9},{1,8},{2,11},{3,10},{4,1},{5,0},{6,3},{7,2},{8,13},{9,12},{1... | collective-permute-start | bytes 786440 | tf_op jit(solution)/shard_map/ppermute | solution.py:498
  82.1 37.6 %collective-permute-start.20 = (f32[8,64,512]{2,1,0:T(8,128)S(1)}, f32[8,64,512]{2,1,0:T(8,128)S(1)}, u32[]{:S(2)}, u32[]{:S(2)}) collective-permute-start(f32[8,64,512]{2,1,0:T(8,128)S(1)} %get-tuple-element.73), channel_id=1, source_target_pairs={{0,16},{8,24},{16,0},{24,8},{1,17},{9,25},{17,1},{25,9},{2,18},{10... | collective-permute-start | bytes 3145736 | tf_op jit(solution)/shard_map/ppermute | solution.py:507
  120.8 29.0 %collective-permute-start.30 = (bf16[2,4,128,512]{3,2,1,0:T(8,128)(2,1)}, bf16[2,4,128,512]{3,2,1,0:T(8,128)(2,1)}, u32[]{:S(2)}, u32[]{:S(2)}) collective-permute-start(bf16[2,4,128,512]{3,2,1,0:T(8,128)(2,1)} %get-tuple-element.53), channel_id=1, source_target_pairs={{0,1},{1,0},{2,3},{3,2},{4,5},{5,4},{6,7},{7,6},{8,9},{9,8},{10,11... | collective-permute-start | bytes 3145736 | tf_op jit(solution)/shard_map/ppermute | solution.py:515
  146.3 15.0 %collective-permute-start.21 = (bf16[2,512,512]{2,1,0:T(8,128)(2,1)}, bf16[2,512,512]{2,1,0:T(8,128)(2,1)}, u32[]{:S(2)}, u32[]{:S(2)}) collective-permute-start(bf16[2,512,512]{2,1,0:T(8,128)(2,1)} %get-tuple-element.41), channel_id=1, source_target_pairs={{0,8},{8,0},{16,24},{24,16},{1,9},{9,1},{17,25},{25,17},{2,10},{10... | collective-permute-start | bytes 3145736 | tf_op jit(solution)/shard_map/ppermute | solution.py:519
  146.5 27.6 %collective-permute-start.31 = (bf16[2,4,64,1024]{3,2,1,0:T(8,128)(2,1)}, bf16[2,4,64,1024]{3,2,1,0:T(8,128)(2,1)}, u32[]{:S(2)}, u32[]{:S(2)}) collective-permute-start(bf16[2,4,64,1024]{3,2,1,0:T(8,128)(2,1)} %get-tuple-element.55), channel_id=1, source_target_pairs={{0,1},{1,0},{2,3},{3,2},{4,5},{5,4},{6,7},{7,6},{8,9},{9,8},{10,11... | collective-permute-start | bytes 3145736 | tf_op jit(solution)/shard_map/ppermute | solution.py:521
  167.7 18.7 %collective-permute-start.26 = (bf16[2,128,512]{2,1,0:T(8,128)(2,1)}, bf16[2,128,512]{2,1,0:T(8,128)(2,1)S(1)}, u32[]{:S(2)}, u32[]{:S(2)}) collective-permute-start(bf16[2,128,512]{2,1,0:T(8,128)(2,1)} %get-tuple-element.46), channel_id=1, source_target_pairs={{2,0},{3,1},{0,2},{1,3},{10,4},{11,5},{8,6},{9,7},{6,8},{7,9},{4,1... | collective-permute-start | bytes 786440 | tf_op jit(solution)/shard_map/ppermute | solution.py:527
  167.7 20.4 %collective-permute-start.27 = (bf16[2,128,512]{2,1,0:T(8,128)(2,1)}, bf16[2,128,512]{2,1,0:T(8,128)(2,1)}, u32[]{:S(2)}, u32[]{:S(2)}) collective-permute-start(bf16[2,128,512]{2,1,0:T(8,128)(2,1)} %get-tuple-element.47), channel_id=1, source_target_pairs={{10,0},{11,1},{8,2},{9,3},{2,4},{3,5},{0,6},{1,7},{14,8},{15,9},{1... | collective-permute-start | bytes 786440 | tf_op jit(solution)/shard_map/ppermute | solution.py:527
  171.1 24.2 %collective-permute-start.28 = (bf16[2,128,512]{2,1,0:T(8,128)(2,1)}, bf16[2,128,512]{2,1,0:T(8,128)(2,1)}, u32[]{:S(2)}, u32[]{:S(2)}) collective-permute-start(bf16[2,128,512]{2,1,0:T(8,128)(2,1)} %get-tuple-element.48), channel_id=1, source_target_pairs={{3,0},{2,1},{1,2},{0,3},{11,4},{10,5},{9,6},{8,7},{7,8},{6,9},{5,1... | collective-permute-start | bytes 786440 | tf_op jit(solution)/shard_map/ppermute | solution.py:527
  171.1 24.7 %collective-permute-start.29 = (bf16[2,128,512]{2,1,0:T(8,128)(2,1)}, bf16[2,128,512]{2,1,0:T(8,128)(2,1)}, u32[]{:S(2)}, u32[]{:S(2)}) collective-permute-start(bf16[2,128,512]{2,1,0:T(8,128)(2,1)} %get-tuple-element.49), channel_id=1, source_target_pairs={{11,0},{10,1},{9,2},{8,3},{3,4},{2,5},{1,6},{0,7},{15,8},{14,9},{1... | collective-permute-start | bytes 786440 | tf_op jit(solution)/shard_map/ppermute | solution.py:527
  178.6 41.1 %collective-permute-start.32 = (bf16[4,2,64,512]{3,2,1,0:T(8,128)(2,1)}, bf16[4,2,64,512]{3,2,1,0:T(8,128)(2,1)S(1)}, u32[]{:S(2)}, u32[]{:S(2)}) collective-permute-start(bf16[4,2,64,512]{3,2,1,0:T(8,128)(2,1)} %fusion.9), channel_id=1, source_target_pairs={{0,16},{8,24},{16,0},{24,8},{1,17},{9,25},{17,1},{25,9},{2,18},{10... | collective-permute-start | bytes 1572872 | tf_op jit(solution)/shard_map/ppermute | solution.py:542
  (45 other events, 520.1 us)

commit v2 on v1

--- a/solution.py
+++ b/solution.py
@@ -5,9 +5,11 @@
 from jax.experimental.pallas import tpu as pltpu
 from jax.sharding import PartitionSpec as P
 
+
 BF = jnp.bfloat16
 F32 = jnp.float32
 TWO_OVER_PI = 0.63661977236758134
+LENS_GAIN = 1.66
 ANY = pl.BlockSpec(memory_space=pl.ANY)
 SMEM = pl.BlockSpec(memory_space=pltpu.SMEM)
 
@@ -44,7 +46,7 @@
     return pl.BlockSpec(block, index)
 
 
-def call(body, grid, ins, outs, scratch, operands, cost, limit=60 << 20):
+def call(body, grid, ins, outs, scratch, operands, cost, limit=28 << 20):
     return pl.pallas_call(
         body,
         out_shape=[jax.ShapeDtypeStruct(s, d) for s, d, _, _ in outs],
@@ -115,18 +117,44 @@
         [pltpu.VMEM((4 * rows, cols), BF)],
         (ids, source, receiver, matrix, lens, omegas),
         2 * 4 * rows * cols * cols * 2,
-    )
-
-
-def lens_place(ids, s, side):
-    return ((ids[1] ^ side) * 2 + (ids[3] ^ (s % 2))) * 4 + (ids[2] ^ (s // 2))
+        60 << 20,
+    )
+
+
+def trig(ids, stack, omega, by_rows):
+    _, quarter, half = stack.shape
+    slices = stack.shape[0] // 2
+    rows, cols = (quarter, 2 * half) if by_rows else (2 * quarter, half)
+
+    def body(ids, pieces, om, sine_ref, cosine_ref):
+        s = pl.program_id(0)
+        for side in range(2):
+            at = ((ids[1] ^ side) * 2 + (ids[3] ^ (s % 2))) * 4 + (ids[2] ^ (s // 2))
+            sine, cosine = sin_cos(pieces[at] * (om[0] * (TWO_OVER_PI / LENS_GAIN)))
+            if by_rows:
+                to = (slice(None), pl.ds(side * half, half))
+            else:
+                to = (pl.ds(side * quarter, quarter), slice(None))
+            sine_ref[to] = sine
+            cosine_ref[to] = cosine
+
+    out = ((slices * rows, cols), F32, (rows, cols), lambda s, ids: (s, 0))
+    return call(
+        body,
+        (slices,),
+        [spec(stack.shape, lambda s, ids: (0, 0, 0)), SMEM],
+        [out, out],
+        [],
+        (ids, stack, omega),
+        1 << 26,
+    )
 
 
 def rotated(re, im, sine, cosine):
     return (re * cosine + im * sine).astype(BF), (im * cosine - re * sine).astype(BF)
 
 
-def column_solve(ids, messages, matrix, lens, omega):
+def column_solve(ids, messages, matrix, waves):
     _, rows, half = messages[0].shape
     n = matrix.shape[-1]
     slices = n // rows
@@ -137,7 +165,7 @@
     blocked = matrix.reshape(2, slices, 2, quarter, n)
 
     def body(ids, *refs):
-        (m0, m1, m2, m3, m4, m5, m6, m7, mat, mat_half, len_ref, om,
+        (m0, m1, m2, m3, m4, m5, m6, m7, mat, mat_half, sine_ref, cosine_ref,
          keep, send, phased, out, field, sems) = refs
         i = pl.program_id(0)
         t = ids[4] * 2 + ids[3]
@@ -173,17 +201,10 @@
                 even, odd = new[:rows].astype(BF), new[rows:].astype(BF)
                 keep[part, i] = jnp.where(first, even, odd)
                 send[part, i] = jnp.where(first, odd, even)
-            for s in range(2):
-                for side in range(2):
-                    at = ((ids[1] ^ side) * 2 + (ids[3] ^ s)) * 4 + (ids[2] ^ i)
-                    sine, cosine = sin_cos(len_ref[at] * (om[0] * TWO_OVER_PI))
-                    lo = s * rows + side * quarter
-                    re, im = rotated(
-                        new_re[lo : lo + quarter], new_im[lo : lo + quarter], sine, cosine
-                    )
-                    to = pl.ds(pl.multiple_of(i * tile + lo, quarter), quarter)
-                    phased[0, to] = re
-                    phased[1, to] = im
+            re, im = rotated(new_re, new_im, sine_ref[...], cosine_ref[...])
+            to = pl.ds(pl.multiple_of(i * tile, tile), tile)
+            phased[0, to] = re
+            phased[1, to] = im
 
         @pl.when(i >= tiles)
         def _():
@@ -206,8 +227,8 @@
                 (2, per, 1, quarter, n),
                 lambda i, ids: (0, jnp.maximum(i - tiles, 0), 1 - ids[0], 0, 0),
             ),
-            spec(lens.shape, flat(3)),
-            SMEM,
+            spec((tile, half), lambda i, ids: (jnp.minimum(i, tiles - 1), 0)),
+            spec((tile, half), lambda i, ids: (jnp.minimum(i, tiles - 1), 0)),
         ],
         [
             (part_shape, BF, part_shape, flat(4)),
@@ -216,7 +237,7 @@
             ((2, n // 2, half), BF, (2, n // 2, half), flat(3)),
         ],
         [pltpu.VMEM((2, n, half), BF), pltpu.SemaphoreType.DMA((8, 2))],
-        (ids, *messages, matrix, blocked, lens, omega),
+        (ids, *messages, matrix, blocked, *waves),
         12 * n * n * half,
     )
 
@@ -250,7 +271,7 @@
     )[0]
 
 
-def row_solve(ids, own, received, matrix, lens, omega, rows):
+def row_solve(ids, own, received, matrix, waves, rows):
     _, lines, half = own.shape
     n = matrix.shape[-1]
     slices = n // rows
@@ -258,7 +279,7 @@
     tile = 2 * rows
     tiles = n // tile
 
-    def body(ids, own_ref, rec_ref, mat, mat_half, len_ref, om, keep, send, phased, out, field):
+    def body(ids, own_ref, rec_ref, mat, mat_half, sine_ref, cosine_ref, keep, send, phased, out, field):
         i = pl.program_id(0)
 
         @pl.when(i == 0)
@@ -275,18 +296,10 @@
             new_re = q_re[:lines] - q_im[lines:]
             new_im = q_re[lines:] + q_im[:lines]
             cols = pl.ds(pl.multiple_of(i * tile, tile), tile)
-            inner = pl.ds(pl.multiple_of((i % (half // tile)) * tile, tile), tile)
-            side = i // (half // tile)
             first = ids[3] == 0
-            for s in range(slices):
-                at = ((ids[1] ^ side) * 2 + (ids[3] ^ (s % 2))) * 4 + (ids[2] ^ (s // 2))
-                sine, cosine = sin_cos(len_ref[at, :, inner] * (om[0] * TWO_OVER_PI))
-                lo = s * quarter
-                re, im = rotated(
-                    new_re[lo : lo + quarter], new_im[lo : lo + quarter], sine, cosine
-                )
-                phased[0, pl.ds(lo, quarter), cols] = re
-                phased[1, pl.ds(lo, quarter), cols] = im
+            re, im = rotated(new_re, new_im, sine_ref[...], cosine_ref[...])
+            phased[0, :, cols] = re
+            phased[1, :, cols] = im
             for part, new in enumerate((new_re, new_im)):
                 for z in range(slices // 2):
                     lo = 2 * z * quarter
@@ -318,8 +331,8 @@
                 (2, tile, n),
                 lambda i, ids: (0, (1 - ids[0]) * per_half + jnp.maximum(i - tiles, 0), 0),
             ),
-            spec(lens.shape, flat(3)),
-            SMEM,
+            spec((lines, tile), lambda i, ids: (0, jnp.minimum(i, tiles - 1))),
+            spec((lines, tile), lambda i, ids: (0, jnp.minimum(i, tiles - 1))),
         ],
         [
             (part_shape, BF, part_shape, flat(4)),
@@ -328,7 +341,7 @@
             ((2, lines, half), BF, (2, lines, half), flat(3)),
         ],
         [pltpu.VMEM((2 * lines, n), BF)],
-        (ids, own, received, matrix, matrix, lens, omega),
+        (ids, own, received, matrix, matrix, *waves),
         12 * n * n * half,
     )
 
@@ -361,7 +374,7 @@
 
 
 def last_solve(ids, turn, own, received, matrix, rows):
-    _, lines, half = own.shape
+    _, _, half = own.shape
     n = matrix.shape[-1]
     slices = n // rows
     quarter = rows // 2
@@ -455,6 +468,32 @@
     )
 
 
+def image_terms(ids, keep, other, weight, by_rows):
+    _, lines, rows, cols = keep.shape
+    high, wide = (rows, cols // 2) if by_rows else (rows // 2, cols)
+
+    def body(ids, k, o, wt, stay, away):
+        first = ids[1] == 0
+        re = k[0, 0].astype(F32) * o[0, 0].astype(F32)
+        term = wt[0] * (re - k[1, 0].astype(F32) * o[1, 0].astype(F32))
+        lo, hi = (term[:, :wide], term[:, wide:]) if by_rows else (term[:high], term[high:])
+        stay[0] = jnp.where(first, lo, hi)
+        away[0] = jnp.where(first, hi, lo).astype(BF)
+
+    block = spec((2, 1, rows, cols), lambda i, ids: (0, i, 0, 0))
+    shape, piece = (lines, high, wide), (1, high, wide)
+    index = lambda i, ids: (i, 0, 0)
+    return call(
+        body,
+        (lines,),
+        [block, block, SMEM],
+        [(shape, F32, piece, index), (shape, BF, piece, index)],
+        [],
+        (ids, keep, other, weight),
+        1 << 22,
+    )
+
+
 def flip(size, bit):
     return [(i, i ^ bit) for i in range(size)]
 
@@ -484,72 +523,69 @@
     ids = jnp.stack([core, x, z, y, z % 2, z // 2]).astype(jnp.int32)
     swap = flip(groups, 1)
 
+    going, coming = scatter_rounds(groups, space, False), scatter_rounds(groups, space, True)
+
+    def send(outputs, turn, rounds):
+        return [lax.ppermute(m, both, rounds[4 * turn + at]) for at, m in enumerate(outputs)]
+
+    corners = ((1, x * quarter, core * half), (2, core * quarter, x * half))
+    piece = jnp.concatenate(
+        [lax.dynamic_slice(lens, corner, (1, quarter, half)) for corner in corners]
+    )
+    piece = (piece * LENS_GAIN).astype(jnp.float16)
+    line = [piece] + [lax.ppermute(piece, "space", flip(space, 2 * k)) for k in (1, 2, 3)]
+    line = jnp.stack(line, axis=1)
+    across_y = lax.ppermute(line, "space", flip(space, 1))
+    planes = [jnp.concatenate([line[d], across_y[d]]) for d in range(2)]
+    across_x = [lax.ppermute(planes[d], "freq", flip(groups, 2)) for d in range(2)]
+
+    solved = home_solve(ids, 0, source, receiver, matrix, lens, omegas)
+    messages = send(solved, 0, going)
+    solved = home_solve(ids, 1, source, receiver, matrix, lens, omegas)
+    messages += send(solved, 1, going)
+
     mine = core == z // 2
     scalars = jnp.stack([omegas, image_weights])
     other = lax.ppermute(scalars, "freq", swap)
     omega, weight = jnp.where(mine, scalars, other)[:, z % 2]
-    omega = omega.reshape(1)
-
-    going, coming = scatter_rounds(groups, space, False), scatter_rounds(groups, space, True)
-    messages = []
-    for turn in range(2):
-        sent = home_solve(ids, turn, source, receiver, matrix, lens, omegas)
-        for at, m in enumerate(sent):
-            messages.append(lax.ppermute(m, both, going[4 * turn + at]))
-
-    stacks = []
-    for depth, (r0, c0) in ((1, (x * quarter, core * half)), (2, (core * quarter, x * half))):
-        piece = lax.dynamic_slice(lens, (depth, r0, c0), (1, quarter, half))
-        line = jnp.concatenate(
-            [piece] + [lax.ppermute(piece, "space", flip(space, 2 * k)) for k in (1, 2, 3)]
-        )
-        plane = jnp.concatenate([line, lax.ppermute(line, "space", flip(space, 1))])
-        stacks.append(jnp.concatenate([plane, lax.ppermute(plane, "freq", flip(groups, 2))]))
-
+    omega, weight = omega.reshape(1), weight.reshape(1)
     held = lax.dynamic_slice(matrix, (0, z % 2, 0, 0), (2, 1, cols, cols))[:, 0]
-    line_matrix = jnp.where(mine, held, lax.ppermute(held, "freq", swap))
-
-    keep0, send0, phased, sent = column_solve(ids, messages, line_matrix, stacks[0], omega)
+    theirs = lax.ppermute(held, "freq", swap)
+    line_matrix = jnp.where(mine, held, theirs)
+
+    waves = []
+    for d in range(2):
+        stack = jnp.concatenate([planes[d], across_x[d]]).astype(F32)
+        waves.append(trig(ids, stack, omega, d == 1))
+
+    keep0, send0, phased, sent = column_solve(ids, messages, line_matrix, waves[0])
     came = lax.ppermute(sent, "freq", swap)
+    partner0 = lax.ppermute(send0, "space", flip(space, 1))
     own = column_rest(ids, phased, line_matrix, rows)
-    partner0 = lax.ppermute(send0, "space", flip(space, 1))
-    keep1, send1, phased, sent = row_solve(
-        ids, own, came, line_matrix, stacks[1], omega, rows
-    )
+    keep1, send1, phased, sent = row_solve(ids, own, came, line_matrix, waves[1], rows)
     came = lax.ppermute(sent, "freq", swap)
+    partner1 = lax.ppermute(send1, "space", flip(space, 1))
     own = row_rest(ids, phased, line_matrix, rows)
-    partner1 = lax.ppermute(send1, "space", flip(space, 1))
-
-    finals = []
-    for turn in range(2):
-        sent = last_solve(ids, turn, own, came, line_matrix, rows)
-        for at, m in enumerate(sent):
-            finals.append(lax.ppermute(m, both, coming[4 * turn + at]))
-
-    def product(a, b):
-        a, b = a.astype(F32), b.astype(F32)
-        return weight * (a[0] * b[0] - a[1] * b[1])
-
-    term0 = product(keep0, partner0)
-    term1 = product(keep1, partner1)
-    halves0 = term0.reshape(-1, 2, quarter, half)
-    halves1 = jnp.moveaxis(term1.reshape(-1, quarter, 2, half), 2, 1)
-    halves = jnp.stack([halves0, halves1], axis=1)
-
-    def side(v, at):
-        return lax.dynamic_index_in_dim(v, at, 2, keepdims=False)
-
-    over_x = side(halves, x) + lax.ppermute(
-        side(halves, 1 - x).astype(BF), "freq", flip(groups, 2)
-    ).astype(F32)
-
-    def slab(at):
-        return lax.dynamic_index_in_dim(over_x, at, 0, keepdims=False)
-
-    total = slab(z)
-    for k in (1, 2, 3):
-        total = total + lax.ppermute(slab(z ^ k).astype(BF), "space", flip(space, 2 * k)).astype(F32)
-    piece = total.astype(BF)
+
+    solved = last_solve(ids, 0, own, came, line_matrix, rows)
+    finals = send(solved, 0, coming)
+    solved = last_solve(ids, 1, own, came, line_matrix, rows)
+    finals += send(solved, 1, coming)
+
+    pieces = []
+    for depth, keep, partner in ((0, keep0, partner0), (1, keep1, partner1)):
+        stay, away = image_terms(ids, keep, partner, weight, depth == 1)
+        over_x = stay + lax.ppermute(away, "freq", flip(groups, 2)).astype(F32)
+
+        def slab(at):
+            return lax.dynamic_index_in_dim(over_x, at, 0, keepdims=False)
+
+        total = slab(z)
+        for k in (1, 2, 3):
+            part = lax.ppermute(slab(z ^ k).astype(BF), "space", flip(space, 2 * k))
+            total = total + part.astype(F32)
+        pieces.append(total.astype(BF))
+    piece = jnp.stack(pieces)
     pair = jnp.stack([piece, lax.ppermute(piece, "freq", swap)])
     quad = jnp.stack([pair, lax.ppermute(pair, "freq", flip(groups, 2))])
 
@@ -686,7 +722,9 @@
     groups, space = lax.axis_size("freq"), lax.axis_size("space")
     freqs, depths = omegas.shape[0], lens_delay.shape[0]
     fits = space == 2 * 2 * freqs and freqs == 2 and groups % 4 == 0 and depths == 3
-    return plane_per_chip(*args) if fits else general(*args)
+    if not fits:
+        return general(*args)
+    return plane_per_chip(*args)
 
 
 def solution(mesh):

time: 248 us -> 234 us (0.944)
  waiting for transfers between devices: 69.5 us -> 84.6 us
  other arithmetic: 17.5 us -> 5.74 us
  Pallas kernels: 79.1 us -> 67.9 us
  local copies, waits for them, and re-layouts: 21.1 us -> 10.9 us
  starting transfers between devices: 58.8 us -> 63.6 us
    pallas_call x9 -> x13, Pallas kernels: 79.1 us -> 67.9 us  [call(): pl.pallas_call(body, out_shape=[jax.ShapeDtypeStruct(s, d) for s, d, _, _...]
    ppermute x6 -> x3, waiting for transfers between devices: 1.6 us -> 10.3 us  [plane_per_chip(): lax.ppermute(piece, 'space', flip(space, 2 * k))]
    unnamed x66 -> x30, local copies, waits for them, and re-layouts: 10.7 us -> 3.83 us
    convert_element_type x6 -> x4, other arithmetic: 7.07 us -> 0.64 us  [the longest x2 0.59 us: plane_per_chip(): stack = jnp.concatenate([planes[d], across_x[d]]).astype(F32)]
    ppermute x25 -> x28, starting transfers between devices: 35.1 us -> 39.6 us  [the longest x16 22.6 us: send(): lax.ppermute(m, both, rounds[4 * turn + at])]
    ppermute x1, waiting for transfers between devices: 0.01 us -> 4.3 us  [plane_per_chip(): lax.ppermute(chip.astype(BF), 'freq', flip(groups, 2)).astype(F32)]
    ppermute x6 -> x3, starting transfers between devices: 8.98 us -> 5.24 us  [plane_per_chip(): lax.ppermute(piece, 'space', flip(space, 2 * k))]
    mul x2 -> x0, other arithmetic: 3.68 us -> none  [product(): return weight * (a[0] * b[0] - a[1] * b[1])]
  transfers between devices with their start and end apart: 40 -> 40, of which waited for: 14 -> 21; matrix products, arithmetic and copies ran while one was open for 11% -> 3% of each run, Pallas kernels for 32% -> 24%
where the time goes in v2:
time: 234 us
  waiting for transfers between devices  84.6 us (36%)
  Pallas kernels  67.9 us (29%)
  starting transfers between devices  63.6 us (27%)
  local copies, waits for them, and re-layouts  10.9 us (5%)
  other arithmetic  5.74 us (2%)
    pallas_call x13, Pallas kernels, call(): pl.pallas_call(body, out_shape=[jax.ShapeDtypeStruct(s, d) for s, d, _, _...  67.9 us
    ppermute x16, waiting for transfers between devices, send(): lax.ppermute(m, both, rounds[4 * turn + at])  38.4 us
    ppermute x16, starting transfers between devices, send(): lax.ppermute(m, both, rounds[4 * turn + at])  22.6 us
    ppermute x2, waiting for transfers between devices, plane_per_chip(): lax.ppermute(planes[d], 'freq', flip(groups, 2))  14.9 us
    ppermute x1, starting transfers between devices, plane_per_chip(): chip = term2.astype(F32) + lax.ppermute(term2, 'freq', swap).astype(F32)  13.1 us
    ppermute x3, waiting for transfers between devices, plane_per_chip(): lax.ppermute(piece, 'space', flip(space, 2 * k))  10.3 us
    ppermute x6, starting transfers between devices, plane_per_chip(): part = lax.ppermute(slab(z ^ k).astype(BF), 'space', flip(space, 2 * k))  8.78 us
    ppermute x1, waiting for transfers between devices, plane_per_chip(): quad = jnp.stack([pair, lax.ppermute(pair, 'freq', flip(groups, 2))])  7.01 us
  transfers between devices with their start and end apart: 40, of which 21 were waited for; matrix products, arithmetic and copies ran while one was open for 3% of the time, Pallas kernels for 24%

profile of v2, /device:TPU:0, one launch (start us, length us, event | category | flops | bytes accessed | tf_op | source)
XLA Modules:
  0.0 234.0 jit_solution(9563799470374412664)
XLA Ops:
  0.7 4.7 %dynamic-slice_bitcast_fusion = bf16[2,1024,1024]{2,1,0:T(8,128)(2,1)} fusion(bf16[2,2,1024,1024]{3,2,1,0:T(8,128)(2,1)} %mat.3, s32[]{:T(128)S(6)} %select_n.110), kind=kLoop, calls=%fused_computation | loop fusion | bytes 8388612 | tf_op jit(solution)/shard_map/squeeze | solution.py:552
  12.1 3.7 %collective-permute-done.9 = f16[2,64,512]{2,1,0:T(8,128)(2,1)S(1)} collective-permute-done((f16[2,64,512]{2,1,0:T(8,128)(2,1)S(1)}, f16[2,64,512]{2,1,0:T(8,128)(2,1)S(1)}, u32[]{:S(2)}, u32[]{:S(2)}) %collective-permute-start.9) | collective-permute-done | bytes 131104 | tf_op jit(solution)/shard_map/ppermute | solution.py:536
  15.8 6.6 %collective-permute-done.10 = f16[2,64,512]{2,1,0:T(8,128)(2,1)S(1)} collective-permute-done((f16[2,64,512]{2,1,0:T(8,128)(2,1)S(1)}, f16[2,64,512]{2,1,0:T(8,128)(2,1)S(1)}, u32[]{:S(2)}, u32[]{:S(2)}) %collective-permute-start.10) | collective-permute-done | bytes 131104 | tf_op jit(solution)/shard_map/ppermute | solution.py:536
  24.9 7.4 %shard_map.85 = (bf16[2,128,512]{2,1,0:T(8,128)(2,1)}, bf16[2,128,512]{2,1,0:T(8,128)(2,1)}, bf16[2,128,512]{2,1,0:T(8,128)(2,1)}, bf16[2,128,512]{2,1,0:T(8,128)(2,1)}) custom-call(s32[6]{0:T(128)} %stack.94.ids, bf16[2,2,128,1024]{3,2,1,0:T(8,128)(2,1)} %src.3, bf16[2,2,128,1024]{3,2,1,0:T(8,128)(2,1)} %rec.3, bf16[2,2,1024,1024]{3,2,1,0:T(8,128)(2,1)} %mat.3, ...), custom_call_target="tpu_custom_call" | custom-call | flops 2147483648 | bytes 8388608 | tf_op jit(solution)/shard_map/pallas_call | solution.py:50
  33.9 4.1 %collective-permute-start.1 = (bf16[2,128,512]{2,1,0:T(8,128)(2,1)}, bf16[2,128,512]{2,1,0:T(8,128)(2,1)S(1)}, u32[]{:S(2)}, u32[]{:S(2)}) collective-permute-start(bf16[2,128,512]{2,1,0:T(8,128)(2,1)} %get-tuple-element.39), channel_id=1, source_target_pairs={{0,8},{1,9},{2,10},{3,11},{4,0},{5,1},{6,2},{7,3},{8,12},{9,13},{1... | collective-permute-start | bytes 786440 | tf_op jit(solution)/shard_map/ppermute | solution.py:529
  40.0 7.4 %shard_map.86 = (bf16[2,128,512]{2,1,0:T(8,128)(2,1)}, bf16[2,128,512]{2,1,0:T(8,128)(2,1)}, bf16[2,128,512]{2,1,0:T(8,128)(2,1)}, bf16[2,128,512]{2,1,0:T(8,128)(2,1)}) custom-call(s32[6]{0:T(128)} %stack.94.ids, bf16[2,2,128,1024]{3,2,1,0:T(8,128)(2,1)} %src.3, bf16[2,2,128,1024]{3,2,1,0:T(8,128)(2,1)} %rec.3, bf16[2,2,1024,1024]{3,2,1,0:T(8,128)(2,1)} %mat.3, ...), custom_call_target="tpu_custom_call" | custom-call | flops 2147483648 | bytes 8388608 | tf_op jit(solution)/shard_map/pallas_call | solution.py:50
  48.6 3.7 %collective-permute-done.13 = f16[8,64,512]{2,1,0:T(8,128)(2,1)S(1)} collective-permute-done((f16[8,64,512]{2,1,0:T(8,128)(2,1)S(1)}, f16[8,64,512]{2,1,0:T(8,128)(2,1)S(1)}, u32[]{:S(2)}, u32[]{:S(2)}) %collective-permute-start.13) | collective-permute-done | bytes 524320 | tf_op jit(solution)/shard_map/ppermute | solution.py:540
  52.7 3.7 %shard_map.87 = (f32[1024,512]{1,0:T(8,128)S(1)}, f32[1024,512]{1,0:T(8,128)S(1)}) custom-call(s32[6]{0:T(128)S(1)} %copy-done.3, f32[16,64,512]{2,1,0:T(8,128)S(1)} %maximum_convert_fusion.pieces, f32[1]{0:T(128)} %bitcast.19.om), custom_call_target="tpu_custom_call" | custom-call | flops 67108864 | bytes 8388608 | tf_op jit(solution)/shard_map/pallas_call | solution.py:50
  64.1 5.0 %collective-permute-done.4.refs_4_ = bf16[2,128,512]{2,1,0:T(8,128)(2,1)S(1)} collective-permute-done((bf16[2,128,512]{2,1,0:T(8,128)(2,1)S(1)}, bf16[2,128,512]{2,1,0:T(8,128)(2,1)S(1)}, u32[]{:S(2)}, u32[]{:S(2)}) %collective-permute-start.4) | collective-permute-done | bytes 262176 | tf_op jit(solution)/shard_map/ppermute | solution.py:529
  71.9 8.9 %collective-permute-done.6.refs_6_ = bf16[2,128,512]{2,1,0:T(8,128)(2,1)S(1)} collective-permute-done((bf16[2,128,512]{2,1,0:T(8,128)(2,1)S(1)}, bf16[2,128,512]{2,1,0:T(8,128)(2,1)S(1)}, u32[]{:S(2)}, u32[]{:S(2)}) %collective-permute-start.6) | collective-permute-done | bytes 262176 | tf_op jit(solution)/shard_map/ppermute | solution.py:529
  83.2 12.1 %shard_map.88 = (bf16[2,4,128,512]{3,2,1,0:T(8,128)(2,1)S(1)}, bf16[2,4,128,512]{3,2,1,0:T(8,128)(2,1)S(1)}, bf16[2,1024,512]{2,1,0:T(8,128)(2,1)S(1)}, bf16[2,512,512]{2,1,0:T(8,128)(2,1)S(1)}) custom-call(s32[6]{0:T(128)S(1)} %copy-done.3, bf16[2,128,512]{2,1,0:T(8,128)(2,1)S(1)} %collective-permute-done.refs_0_, ...), custom_call_target="tpu_custom_call" | custom-call | flops 6442450944 | bytes 8388608 | tf_op jit(solution)/shard_map/pallas_call | solution.py:50
  99.7 11.2 %collective-permute-done.16 = f16[8,64,512]{2,1,0:T(8,128)(2,1)S(1)} collective-permute-done((f16[8,64,512]{2,1,0:T(8,128)(2,1)S(1)}, f16[8,64,512]{2,1,0:T(8,128)(2,1)S(1)}, u32[]{:S(2)}, u32[]{:S(2)}) %collective-permute-start.16) | collective-permute-done | bytes 524320 | tf_op jit(solution)/shard_map/ppermute | solution.py:540
  111.2 3.7 %shard_map.90 = (f32[512,1024]{1,0:T(8,128)S(1)}, f32[512,1024]{1,0:T(8,128)S(1)}) custom-call(s32[6]{0:T(128)S(1)} %copy-done.3, f32[16,64,512]{2,1,0:T(8,128)S(1)} %maximum_convert_fusion.1.pieces, f32[1]{0:T(128)} %bitcast.19.om), custom_call_target="tpu_custom_call" | custom-call | flops 67108864 | bytes 8388608 | tf_op jit(solution)/shard_map/pallas_call | solution.py:50
  118.2 11.1 %shard_map.91 = (bf16[2,4,64,1024]{3,2,1,0:T(8,128)(2,1)S(1)}, bf16[2,4,64,1024]{3,2,1,0:T(8,128)(2,1)}, bf16[2,512,1024]{2,1,0:T(8,128)(2,1)S(1)}, bf16[2,512,512]{2,1,0:T(8,128)(2,1)}) custom-call(s32[6]{0:T(128)S(1)} %copy-done.3, bf16[2,512,512]{2,1,0:T(8,128)(2,1)S(1)} %shard_map.89.own_ref, bf16[2,512,512]{2,1,0:T(8,128)(2,1)S(1)} %collective-permute-done.15.rec_ref, ...), custom_call_target="tpu_custom_call" | custom-call | flops 6442450944 | bytes 8388608 | tf_op jit(solution)/shard_map/pallas_call | solution.py:50
  133.8 5.6 %collective-permute-done.27 = bf16[4,64,512]{2,1,0:T(8,128)(2,1)S(1)} collective-permute-done((bf16[4,64,512]{2,1,0:T(8,128)(2,1)S(1)}, bf16[4,64,512]{2,1,0:T(8,128)(2,1)S(1)}, u32[]{:S(2)}, u32[]{:S(2)}) %collective-permute-start.27) | collective-permute-done | bytes 262176 | tf_op jit(solution)/shard_map/ppermute | solution.py:578
  157.1 4.7 %shard_map.94 = (bf16[2,128,512]{2,1,0:T(8,128)(2,1)S(1)}, bf16[2,128,512]{2,1,0:T(8,128)(2,1)S(1)}, bf16[2,128,512]{2,1,0:T(8,128)(2,1)S(1)}, bf16[2,128,512]{2,1,0:T(8,128)(2,1)S(1)}) custom-call(s32[6]{0:T(128)S(1)} %copy-done.3, bf16[2,512,512]{2,1,0:T(8,128)(2,1)S(1)} %shard_map.92.own_ref, bf16[2,512,512]{2,1,0:T(8,128)(2,1)} %collective-permute-done.17.rec_ref, ...), custom_call_target="tpu_custom_call" | custom-call | flops 2147483648 | bytes 8388608 | tf_op jit(solution)/shard_map/pallas_call | solution.py:50
  169.1 6.5 %collective-permute-done.22.refs_4_ = bf16[2,128,512]{2,1,0:T(8,128)(2,1)S(1)} collective-permute-done((bf16[2,128,512]{2,1,0:T(8,128)(2,1)S(1)}, bf16[2,128,512]{2,1,0:T(8,128)(2,1)S(1)}, u32[]{:S(2)}, u32[]{:S(2)}) %collective-permute-start.22) | collective-permute-done | bytes 262176 | tf_op jit(solution)/shard_map/ppermute | solution.py:529
  175.7 4.6 %shard_map.93 = (bf16[2,128,512]{2,1,0:T(8,128)(2,1)S(1)}, bf16[2,128,512]{2,1,0:T(8,128)(2,1)S(1)}, bf16[2,128,512]{2,1,0:T(8,128)(2,1)S(1)}, bf16[2,128,512]{2,1,0:T(8,128)(2,1)S(1)}) custom-call(s32[6]{0:T(128)S(1)} %copy-done.3, bf16[2,512,512]{2,1,0:T(8,128)(2,1)S(1)} %shard_map.92.own_ref, bf16[2,512,512]{2,1,0:T(8,128)(2,1)} %collective-permute-done.17.rec_ref, ...), custom_call_target="tpu_custom_call" | custom-call | flops 2147483648 | bytes 8388608 | tf_op jit(solution)/shard_map/pallas_call | solution.py:50
  180.9 4.8 %collective-permute-start.25 = (bf16[2,128,512]{2,1,0:T(8,128)(2,1)S(1)}, bf16[2,128,512]{2,1,0:T(8,128)(2,1)S(1)}, u32[]{:S(2)}, u32[]{:S(2)}) collective-permute-start(bf16[2,128,512]{2,1,0:T(8,128)(2,1)S(1)} %get-tuple-element.61), channel_id=1, source_target_pairs={{11,0},{10,1},{9,2},{8,3},{3,4},{2,5},{1,6},{0,7},{15,8},{14,9},{1... | collective-permute-start | bytes 786440 | tf_op jit(solution)/shard_map/ppermute | solution.py:529
  193.3 4.7 %collective-permute-done.19.refs_1_ = bf16[2,128,512]{2,1,0:T(8,128)(2,1)S(1)} collective-permute-done((bf16[2,128,512]{2,1,0:T(8,128)(2,1)S(1)}, bf16[2,128,512]{2,1,0:T(8,128)(2,1)S(1)}, u32[]{:S(2)}, u32[]{:S(2)}) %collective-permute-start.19) | collective-permute-done | bytes 262176 | tf_op jit(solution)/shard_map/ppermute | solution.py:529
  198.7 4.0 %collective-permute-done.21.refs_3_ = bf16[2,128,512]{2,1,0:T(8,128)(2,1)S(1)} collective-permute-done((bf16[2,128,512]{2,1,0:T(8,128)(2,1)S(1)}, bf16[2,128,512]{2,1,0:T(8,128)(2,1)S(1)}, u32[]{:S(2)}, u32[]{:S(2)}) %collective-permute-start.21) | collective-permute-done | bytes 262176 | tf_op jit(solution)/shard_map/ppermute | solution.py:529
  205.6 13.1 %collective-permute-start.38 = (bf16[128,1024]{1,0:T(8,128)(2,1)S(1)}, bf16[128,1024]{1,0:T(8,128)(2,1)S(1)}, u32[]{:S(2)}, u32[]{:S(2)}) collective-permute-start(bf16[128,1024]{1,0:T(8,128)(2,1)S(1)} %get-tuple-element.72), channel_id=1, source_target_pairs={{0,8},{8,0},{16,24},{24,16},{1,9},{9,1},{17,25},{25,17},{2,10},{10... | collective-permute-start | bytes 786440 | tf_op jit(solution)/shard_map/ppermute | solution.py:601
  221.0 7.0 %collective-permute-done.37 = bf16[2,2,64,512]{3,2,1,0:T(8,128)(2,1)S(1)} collective-permute-done((bf16[2,2,64,512]{3,2,1,0:T(8,128)(2,1)S(1)}, bf16[2,2,64,512]{3,2,1,0:T(8,128)(2,1)S(1)}, u32[]{:S(2)}, u32[]{:S(2)}) %collective-permute-start.37) | collective-permute-done | bytes 262176 | tf_op jit(solution)/shard_map/ppermute | solution.py:590
  228.3 4.3 %collective-permute-done.39 = bf16[128,1024]{1,0:T(8,128)(2,1)S(1)} collective-permute-done((bf16[128,1024]{1,0:T(8,128)(2,1)S(1)}, bf16[128,1024]{1,0:T(8,128)(2,1)S(1)}, u32[]{:S(2)}, u32[]{:S(2)}) %collective-permute-start.39) | collective-permute-done | bytes 262176 | tf_op jit(solution)/shard_map/ppermute | solution.py:602
  (130 shorter events, 80.2 us)
Async XLA Ops:
  5.3 55.6 %collective-permute-start.8 = (bf16[2,1024,1024]{2,1,0:T(8,128)(2,1)}, bf16[2,1024,1024]{2,1,0:T(8,128)(2,1)}, u32[]{:S(2)}, u32[]{:S(2)}) collective-permute-start(bf16[2,1024,1024]{2,1,0:T(8,128)(2,1)} %dynamic-slice_bitcast_fusion), channel_id=1, source_target_pairs={{0,8},{8,0},{16,24},{24,16},{1,9},{9,1},{17,25},{25,17},{2,10},{10... | collective-permute-start | bytes 12582920 | tf_op jit(solution)/shard_map/ppermute | solution.py:553
  22.6 15.5 %collective-permute-start.12 = (f16[2,4,64,512]{3,2,1,0:T(8,128)(2,1)S(1)}, f16[2,4,64,512]{3,2,1,0:T(8,128)(2,1)S(1)}, u32[]{:S(2)}, u32[]{:S(2)}) collective-permute-start(f16[2,4,64,512]{3,2,1,0:T(8,128)(2,1)S(1)} %pad_maximum_fusion.1), channel_id=1, source_target_pairs={{0,1},{1,0},{2,3},{3,2},{4,5},{5,4},{6,7},{7,6},{8,9},{9,8},{10,11... | collective-permute-start | bytes 1572872 | tf_op jit(solution)/shard_map/ppermute | solution.py:538
  24.2 23.2 %collective-permute-start.14 = (f32[2,2]{1,0:T(2,128)S(1)}, f32[2,2]{1,0:T(2,128)S(1)}, u32[]{:S(2)}, u32[]{:S(2)}) collective-permute-start(f32[2,2]{1,0:T(2,128)S(1)} %pad_maximum_fusion.6), channel_id=1, source_target_pairs={{0,8},{8,0},{16,24},{24,16},{1,9},{9,1},{17,25},{25,17},{2,10},{10... | collective-permute-start | bytes 56 | tf_op jit(solution)/shard_map/ppermute | solution.py:549
  32.3 24.1 %collective-permute-start = (bf16[2,128,512]{2,1,0:T(8,128)(2,1)}, bf16[2,128,512]{2,1,0:T(8,128)(2,1)S(1)}, u32[]{:S(2)}, u32[]{:S(2)}) collective-permute-start(bf16[2,128,512]{2,1,0:T(8,128)(2,1)} %get-tuple-element.38), channel_id=1, source_target_pairs={{0,0},{1,1},{2,2},{3,3},{4,8},{5,9},{6,10},{7,11},{8,4},{9,5},{10,... | collective-permute-start | bytes 786440 | tf_op jit(solution)/shard_map/ppermute | solution.py:529
  33.9 22.6 %collective-permute-start.1 = (bf16[2,128,512]{2,1,0:T(8,128)(2,1)}, bf16[2,128,512]{2,1,0:T(8,128)(2,1)S(1)}, u32[]{:S(2)}, u32[]{:S(2)}) collective-permute-start(bf16[2,128,512]{2,1,0:T(8,128)(2,1)} %get-tuple-element.39), channel_id=1, source_target_pairs={{0,8},{1,9},{2,10},{3,11},{4,0},{5,1},{6,2},{7,3},{8,12},{9,13},{1... | collective-permute-start | bytes 786440 | tf_op jit(solution)/shard_map/ppermute | solution.py:529
  38.4 13.9 %collective-permute-start.13 = (f16[8,64,512]{2,1,0:T(8,128)(2,1)S(1)}, f16[8,64,512]{2,1,0:T(8,128)(2,1)S(1)}, u32[]{:S(2)}, u32[]{:S(2)}) collective-permute-start(f16[8,64,512]{2,1,0:T(8,128)(2,1)S(1)} %pad_maximum_fusion.2), channel_id=1, source_target_pairs={{0,16},{8,24},{16,0},{24,8},{1,17},{9,25},{17,1},{25,9},{2,18},{10... | collective-permute-start | bytes 1572872 | tf_op jit(solution)/shard_map/ppermute | solution.py:540
  56.6 15.3 %collective-permute-start.5 = (bf16[2,128,512]{2,1,0:T(8,128)(2,1)S(1)}, bf16[2,128,512]{2,1,0:T(8,128)(2,1)S(1)}, u32[]{:S(2)}, u32[]{:S(2)}) collective-permute-start(bf16[2,128,512]{2,1,0:T(8,128)(2,1)S(1)} %copy-done.12), channel_id=1, source_target_pairs={{0,10},{1,11},{2,8},{3,9},{4,2},{5,3},{6,0},{7,1},{8,14},{9,15},{1... | collective-permute-start | bytes 786440 | tf_op jit(solution)/shard_map/ppermute | solution.py:529
  59.7 21.1 %collective-permute-start.6 = (bf16[2,128,512]{2,1,0:T(8,128)(2,1)S(1)}, bf16[2,128,512]{2,1,0:T(8,128)(2,1)S(1)}, u32[]{:S(2)}, u32[]{:S(2)}) collective-permute-start(bf16[2,128,512]{2,1,0:T(8,128)(2,1)S(1)} %copy-done.11), channel_id=1, source_target_pairs={{0,3},{1,2},{2,1},{3,0},{4,11},{5,10},{6,9},{7,8},{8,7},{9,6},{10,... | collective-permute-start | bytes 786440 | tf_op jit(solution)/shard_map/ppermute | solution.py:529
  61.0 22.2 %collective-permute-start.7 = (bf16[2,128,512]{2,1,0:T(8,128)(2,1)S(1)}, bf16[2,128,512]{2,1,0:T(8,128)(2,1)S(1)}, u32[]{:S(2)}, u32[]{:S(2)}) collective-permute-start(bf16[2,128,512]{2,1,0:T(8,128)(2,1)S(1)} %copy-done.10), channel_id=1, source_target_pairs={{0,11},{1,10},{2,9},{3,8},{4,3},{5,2},{6,1},{7,0},{8,15},{9,14},{1... | collective-permute-start | bytes 786440 | tf_op jit(solution)/shard_map/ppermute | solution.py:529
  95.4 22.8 %collective-permute-start.15 = (bf16[2,512,512]{2,1,0:T(8,128)(2,1)S(1)}, bf16[2,512,512]{2,1,0:T(8,128)(2,1)S(1)}, u32[]{:S(2)}, u32[]{:S(2)}) collective-permute-start(bf16[2,512,512]{2,1,0:T(8,128)(2,1)S(1)} %get-tuple-element.49), channel_id=1, source_target_pairs={{0,8},{8,0},{16,24},{24,16},{1,9},{9,1},{17,25},{25,17},{2,10},{10... | collective-permute-start | bytes 3145736 | tf_op jit(solution)/shard_map/ppermute | solution.py:562
  97.0 13.9 %collective-permute-start.16 = (f16[8,64,512]{2,1,0:T(8,128)(2,1)S(1)}, f16[8,64,512]{2,1,0:T(8,128)(2,1)S(1)}, u32[]{:S(2)}, u32[]{:S(2)}) collective-permute-start(f16[8,64,512]{2,1,0:T(8,128)(2,1)S(1)} %pad_maximum_fusion.3), channel_id=1, source_target_pairs={{0,16},{8,24},{16,0},{24,8},{1,17},{9,25},{17,1},{25,9},{2,18},{10... | collective-permute-start | bytes 1572872 | tf_op jit(solution)/shard_map/ppermute | solution.py:540
  98.5 32.0 %collective-permute-start.26 = (bf16[2,4,128,512]{3,2,1,0:T(8,128)(2,1)S(1)}, bf16[2,4,128,512]{3,2,1,0:T(8,128)(2,1)S(1)}, u32[]{:S(2)}, u32[]{:S(2)}) collective-permute-start(bf16[2,4,128,512]{3,2,1,0:T(8,128)(2,1)S(1)} %get-tuple-element.65), channel_id=1, source_target_pairs={{0,1},{1,0},{2,3},{3,2},{4,5},{5,4},{6,7},{7,6},{8,9},{9,8},{10,11... | collective-permute-start | bytes 3145736 | tf_op jit(solution)/shard_map/ppermute | solution.py:563
  129.3 24.4 %collective-permute-start.31 = (bf16[2,4,64,1024]{3,2,1,0:T(8,128)(2,1)}, bf16[2,4,64,1024]{3,2,1,0:T(8,128)(2,1)S(1)}, u32[]{:S(2)}, u32[]{:S(2)}) collective-permute-start(bf16[2,4,64,1024]{3,2,1,0:T(8,128)(2,1)} %get-tuple-element.69), channel_id=1, source_target_pairs={{0,1},{1,0},{2,3},{3,2},{4,5},{5,4},{6,7},{7,6},{8,9},{9,8},{10,11... | collective-permute-start | bytes 3145736 | tf_op jit(solution)/shard_map/ppermute | solution.py:567
  133.8 23.3 %collective-permute-start.17 = (bf16[2,512,512]{2,1,0:T(8,128)(2,1)}, bf16[2,512,512]{2,1,0:T(8,128)(2,1)}, u32[]{:S(2)}, u32[]{:S(2)}) collective-permute-start(bf16[2,512,512]{2,1,0:T(8,128)(2,1)} %get-tuple-element.53), channel_id=1, source_target_pairs={{0,8},{8,0},{16,24},{24,16},{1,9},{9,1},{17,25},{25,17},{2,10},{10... | collective-permute-start | bytes 3145736 | tf_op jit(solution)/shard_map/ppermute | solution.py:566
  139.6 17.5 %collective-permute-start.28 = (bf16[64,512]{1,0:T(8,128)(2,1)S(1)}, bf16[64,512]{1,0:T(8,128)(2,1)S(1)}, u32[]{:S(2)}, u32[]{:S(2)}) collective-permute-start(bf16[64,512]{1,0:T(8,128)(2,1)S(1)} %get-tuple-element.82), channel_id=1, source_target_pairs={{0,2},{1,3},{2,0},{3,1},{4,6},{5,7},{6,4},{7,5},{8,10},{9,11},{10,... | collective-permute-start | bytes 196616 | tf_op jit(solution)/shard_map/ppermute | solution.py:585
  141.4 15.7 %collective-permute-start.29 = (bf16[64,512]{1,0:T(8,128)(2,1)S(1)}, bf16[64,512]{1,0:T(8,128)(2,1)S(1)}, u32[]{:S(2)}, u32[]{:S(2)}) collective-permute-start(bf16[64,512]{1,0:T(8,128)(2,1)S(1)} %get-tuple-element.84), channel_id=1, source_target_pairs={{0,4},{1,5},{2,6},{3,7},{4,0},{5,1},{6,2},{7,3},{8,12},{9,13},{10,... | collective-permute-start | bytes 196616 | tf_op jit(solution)/shard_map/ppermute | solution.py:585
  161.8 13.9 %collective-permute-start.22 = (bf16[2,128,512]{2,1,0:T(8,128)(2,1)S(1)}, bf16[2,128,512]{2,1,0:T(8,128)(2,1)S(1)}, u32[]{:S(2)}, u32[]{:S(2)}) collective-permute-start(bf16[2,128,512]{2,1,0:T(8,128)(2,1)S(1)} %get-tuple-element.58), channel_id=1, source_target_pairs={{2,0},{3,1},{0,2},{1,3},{10,4},{11,5},{8,6},{9,7},{6,8},{7,9},{4,1... | collective-permute-start | bytes 786440 | tf_op jit(solution)/shard_map/ppermute | solution.py:529
  163.6 17.3 %collective-permute-start.23 = (bf16[2,128,512]{2,1,0:T(8,128)(2,1)S(1)}, bf16[2,128,512]{2,1,0:T(8,128)(2,1)S(1)}, u32[]{:S(2)}, u32[]{:S(2)}) collective-permute-start(bf16[2,128,512]{2,1,0:T(8,128)(2,1)S(1)} %get-tuple-element.59), channel_id=1, source_target_pairs={{10,0},{11,1},{8,2},{9,3},{2,4},{3,5},{0,6},{1,7},{14,8},{15,9},{1... | collective-permute-start | bytes 786440 | tf_op jit(solution)/shard_map/ppermute | solution.py:529
  164.7 23.6 %collective-permute-start.24 = (bf16[2,128,512]{2,1,0:T(8,128)(2,1)S(1)}, bf16[2,128,512]{2,1,0:T(8,128)(2,1)S(1)}, u32[]{:S(2)}, u32[]{:S(2)}) collective-permute-start(bf16[2,128,512]{2,1,0:T(8,128)(2,1)S(1)} %get-tuple-element.60), channel_id=1, source_target_pairs={{3,0},{2,1},{1,2},{0,3},{11,4},{10,5},{9,6},{8,7},{7,8},{6,9},{5,1... | collective-permute-start | bytes 786440 | tf_op jit(solution)/shard_map/ppermute | solution.py:529
  164.8 24.1 %collective-permute-start.33 = (bf16[64,512]{1,0:T(8,128)(2,1)S(1)}, bf16[64,512]{1,0:T(8,128)(2,1)S(1)}, u32[]{:S(2)}, u32[]{:S(2)}) collective-permute-start(bf16[64,512]{1,0:T(8,128)(2,1)S(1)} %get-tuple-element.85), channel_id=1, source_target_pairs={{0,2},{1,3},{2,0},{3,1},{4,6},{5,7},{6,4},{7,5},{8,10},{9,11},{10,... | collective-permute-start | bytes 196616 | tf_op jit(solution)/shard_map/ppermute | solution.py:585
  167.1 23.4 %collective-permute-start.34 = (bf16[64,512]{1,0:T(8,128)(2,1)S(1)}, bf16[64,512]{1,0:T(8,128)(2,1)S(1)}, u32[]{:S(2)}, u32[]{:S(2)}) collective-permute-start(bf16[64,512]{1,0:T(8,128)(2,1)S(1)} %get-tuple-element.87), channel_id=1, source_target_pairs={{0,4},{1,5},{2,6},{3,7},{4,0},{5,1},{6,2},{7,3},{8,12},{9,13},{10,... | collective-permute-start | bytes 196616 | tf_op jit(solution)/shard_map/ppermute | solution.py:585
  175.7 16.7 %collective-permute-start.35 = (bf16[64,512]{1,0:T(8,128)(2,1)S(1)}, bf16[64,512]{1,0:T(8,128)(2,1)S(1)}, u32[]{:S(2)}, u32[]{:S(2)}) collective-permute-start(bf16[64,512]{1,0:T(8,128)(2,1)S(1)} %get-tuple-element.86), channel_id=1, source_target_pairs={{0,6},{1,7},{2,4},{3,5},{4,2},{5,3},{6,0},{7,1},{8,14},{9,15},{10,... | collective-permute-start | bytes 196616 | tf_op jit(solution)/shard_map/ppermute | solution.py:585
  193.2 25.4 %collective-permute-start.36 = (bf16[2,64,512]{2,1,0:T(8,128)(2,1)S(1)}, bf16[2,64,512]{2,1,0:T(8,128)(2,1)S(1)}, u32[]{:S(2)}, u32[]{:S(2)}) collective-permute-start(bf16[2,64,512]{2,1,0:T(8,128)(2,1)S(1)} %get-tuple-element.95), channel_id=1, source_target_pairs={{0,8},{8,0},{16,24},{24,16},{1,9},{9,1},{17,25},{25,17},{2,10},{10... | collective-permute-start | bytes 393224 | tf_op jit(solution)/shard_map/ppermute | solution.py:589
  205.6 14.2 %collective-permute-start.38 = (bf16[128,1024]{1,0:T(8,128)(2,1)S(1)}, bf16[128,1024]{1,0:T(8,128)(2,1)S(1)}, u32[]{:S(2)}, u32[]{:S(2)}) collective-permute-start(bf16[128,1024]{1,0:T(8,128)(2,1)S(1)} %get-tuple-element.72), channel_id=1, source_target_pairs={{0,8},{8,0},{16,24},{24,16},{1,9},{9,1},{17,25},{25,17},{2,10},{10... | collective-permute-start | bytes 786440 | tf_op jit(solution)/shard_map/ppermute | solution.py:601
  (31 other events, 337.9 us)

commit v3 on v2

--- a/solution.py
+++ b/solution.py
@@ -8,6 +8,9 @@
 
 BF = jnp.bfloat16
 F32 = jnp.float32
+CHUNKS = 1
+TILES = 2
+GRANT = 16
 TWO_OVER_PI = 0.63661977236758134
 LENS_GAIN = 1.66
 ANY = pl.BlockSpec(memory_space=pl.ANY)
@@ -62,6 +65,21 @@
     )(*operands)
 
 
+VMEM = pl.BlockSpec(memory_space=pltpu.VMEM)
+
+
+def solid(body, outs, scratch, operands, cost, limit, ins=None):
+    return pl.pallas_call(
+        body,
+        out_shape=[jax.ShapeDtypeStruct(s, d) for s, d in outs],
+        in_specs=[SMEM] + (ins or [VMEM] * (len(operands) - 1)),
+        out_specs=[VMEM] * len(outs),
+        scratch_shapes=scratch,
+        compiler_params=pltpu.CompilerParams(vmem_limit_bytes=limit << 20),
+        cost_estimate=pl.CostEstimate(flops=cost, bytes_accessed=8 << 20, transcendentals=0),
+    )(*operands)
+
+
 def home_solve(ids, turn, source, receiver, matrix, lens, omegas):
     _, _, rows, cols = source.shape
     half = cols // 2
@@ -129,7 +147,8 @@
     def body(ids, pieces, om, sine_ref, cosine_ref):
         s = pl.program_id(0)
         for side in range(2):
-            at = ((ids[1] ^ side) * 2 + (ids[3] ^ (s % 2))) * 4 + (ids[2] ^ (s // 2))
+            x_at, y_at = ids[1] ^ side, ids[3] ^ (s % 2)
+            at = (x_at * 2 + y_at) * 4 + (ids[2] ^ (s // 2))
             sine, cosine = sin_cos(pieces[at] * (om[0] * (TWO_OVER_PI / LENS_GAIN)))
             if by_rows:
                 to = (slice(None), pl.ds(side * half, half))
@@ -147,6 +166,7 @@
         [],
         (ids, stack, omega),
         1 << 26,
+        12 << 20,
     )
 
 
@@ -158,116 +178,83 @@
     _, rows, half = messages[0].shape
     n = matrix.shape[-1]
     slices = n // rows
-    tile = 2 * rows
-    tiles = n // tile
+    tile = n // TILES
+    chunk = half // CHUNKS
     quarter = rows // 2
-    per = tile // quarter
     blocked = matrix.reshape(2, slices, 2, quarter, n)
 
     def body(ids, *refs):
-        (m0, m1, m2, m3, m4, m5, m6, m7, mat, mat_half, sine_ref, cosine_ref,
-         keep, send, phased, out, field, sems) = refs
-        i = pl.program_id(0)
+        ms, (mat, sine_ref, cosine_ref, keep, send, phased, out, field) = refs[:8], refs[8:]
         t = ids[4] * 2 + ids[3]
-
-        @pl.when(i == 0)
-        def _():
-            copies = []
-            for at, m in enumerate((m0, m1, m2, m3, m4, m5, m6, m7)):
-                a, b = at // 2, at % 2
-                place = (ids[0] ^ b) * 4 + (t ^ a)
-                for part in range(2):
-                    copies.append(
-                        pltpu.make_async_copy(
-                            m.at[part],
-                            field.at[part, pl.ds(pl.multiple_of(place * rows, rows), rows)],
-                            sems.at[at, part],
-                        )
-                    )
-            for copy in copies:
-                copy.start()
-            for copy in copies:
-                copy.wait()
-
-        @pl.when(i < tiles)
-        def _():
-            left = mat[...].reshape(2 * tile, n)
-            q_re = dot_rows(left, field[0])
-            q_im = dot_rows(left, field[1])
-            new_re = q_re[:tile] - q_im[tile:]
-            new_im = q_im[:tile] + q_re[tile:]
-            first = ids[3] == 0
-            for part, new in enumerate((new_re, new_im)):
-                even, odd = new[:rows].astype(BF), new[rows:].astype(BF)
-                keep[part, i] = jnp.where(first, even, odd)
-                send[part, i] = jnp.where(first, odd, even)
-            re, im = rotated(new_re, new_im, sine_ref[...], cosine_ref[...])
-            to = pl.ds(pl.multiple_of(i * tile, tile), tile)
-            phased[0, to] = re
-            phased[1, to] = im
-
-        @pl.when(i >= tiles)
-        def _():
-            left = mat_half[...].reshape(2 * tile, n)
-            q_re = dot_rows(left, phased[0])
-            q_im = dot_rows(left, phased[1])
-            to = pl.ds(pl.multiple_of((i - tiles) * tile, tile), tile)
-            out[0, to] = (q_re[:tile] - q_im[tile:]).astype(BF)
-            out[1, to] = (q_im[:tile] + q_re[tile:]).astype(BF)
-
-    flat = lambda rank: (lambda i, ids: (0,) * rank)
-    part_shape = (2, tiles, rows, half)
-    return call(
-        body,
-        (tiles + tiles // 2,),
-        [ANY] * 8
-        + [
-            spec((2, tile, n), lambda i, ids: (0, jnp.minimum(i, tiles - 1), 0)),
-            spec(
-                (2, per, 1, quarter, n),
-                lambda i, ids: (0, jnp.maximum(i - tiles, 0), 1 - ids[0], 0, 0),
-            ),
-            spec((tile, half), lambda i, ids: (jnp.minimum(i, tiles - 1), 0)),
-            spec((tile, half), lambda i, ids: (jnp.minimum(i, tiles - 1), 0)),
-        ],
-        [
-            (part_shape, BF, part_shape, flat(4)),
-            (part_shape, BF, part_shape, flat(4)),
-            ((2, n, half), BF, (2, n, half), flat(3)),
-            ((2, n // 2, half), BF, (2, n // 2, half), flat(3)),
-        ],
-        [pltpu.VMEM((2, n, half), BF), pltpu.SemaphoreType.DMA((8, 2))],
-        (ids, *messages, matrix, blocked, *waves),
+        for at, m in enumerate(ms):
+            a, b = at // 2, at % 2
+            place = (ids[0] ^ b) * 4 + (t ^ a)
+            to = pl.ds(pl.multiple_of(place * rows, rows), rows)
+            field[0, to] = m[0]
+            field[1, to] = m[1]
+        first = ids[3] == 0
+        for i in range(TILES):
+            per = tile // rows
+            left = mat[:, i * per : (i + 1) * per].reshape(2 * tile, n)
+            to = pl.ds(i * tile, tile)
+            for c in range(CHUNKS):
+                cols = pl.ds(c * chunk, chunk)
+                q_re = dot_rows(left, field[0, :, cols])
+                q_im = dot_rows(left, field[1, :, cols])
+                new_re = q_re[:tile] - q_im[tile:]
+                new_im = q_im[:tile] + q_re[tile:]
+                re, im = rotated(new_re, new_im, sine_ref[to, cols], cosine_ref[to, cols])
+                phased[0, to, cols] = re
+                phased[1, to, cols] = im
+                for part, new in enumerate((new_re, new_im)):
+                    for line in range(per // 2):
+                        lo = 2 * line * rows
+                        even = new[lo : lo + rows].astype(BF)
+                        odd = new[lo + rows : lo + 2 * rows].astype(BF)
+                        z = i * (per // 2) + line
+                        keep[part, z, :, cols] = jnp.where(first, even, odd)
+                        send[part, z, :, cols] = jnp.where(first, odd, even)
+        column_half(mat, 1 - ids[0], phased, out)
+
+    part = ((2, slices // 2, rows, half), BF)
+    return solid(
+        body,
+        [part, part, ((2, n, half), BF), ((2, n // 2, half), BF)],
+        [pltpu.VMEM((2, n, half), BF)],
+        (ids, *messages, blocked, *waves),
         12 * n * n * half,
-    )
+        GRANT,
+    )
+
+
+def column_half(mat, side, field, out):
+    _, _, _, _, n = mat.shape
+    tile = n // 2
+    half = field.shape[-1]
+    chunk = half // CHUNKS
+    left = mat[:, :, side].reshape(2 * tile, n)
+    for c in range(CHUNKS):
+        cols = pl.ds(c * chunk, chunk)
+        q_re = dot_rows(left, field[0, :, cols])
+        q_im = dot_rows(left, field[1, :, cols])
+        out[0, :, cols] = (q_re[:tile] - q_im[tile:]).astype(BF)
+        out[1, :, cols] = (q_im[:tile] + q_re[tile:]).astype(BF)
 
 
 def column_rest(ids, phased, matrix, rows):
     _, n, half = phased.shape
-    slices = n // rows
-    tile = 2 * rows
-    quarter = rows // 2
-    per = tile // quarter
-    blocked = matrix.reshape(2, slices, 2, quarter, n)
-
-    def body(ids, field, mat_half, out):
-        left = mat_half[...].reshape(2 * tile, n)
-        q_re = dot_rows(left, field[0])
-        q_im = dot_rows(left, field[1])
-        out[0] = (q_re[:tile] - q_im[tile:]).astype(BF)
-        out[1] = (q_im[:tile] + q_re[tile:]).astype(BF)
-
-    return call(
-        body,
-        (slices * quarter // tile,),
-        [
-            spec((2, n, half), lambda i, ids: (0, 0, 0)),
-            spec((2, per, 1, quarter, n), lambda i, ids: (0, i, ids[0], 0, 0)),
-        ],
-        [((2, n // 2, half), BF, (2, tile, half), lambda i, ids: (0, i, 0))],
+    blocked = matrix.reshape(2, n // rows, 2, rows // 2, n)
+
+    def body(ids, field, mat, out):
+        column_half(mat, ids[0], field, out)
+
+    return solid(
+        body,
+        [((2, n // 2, half), BF)],
         [],
         (ids, phased, blocked),
         4 * n * n * half,
+        GRANT,
     )[0]
 
 
@@ -276,28 +263,21 @@
     n = matrix.shape[-1]
     slices = n // rows
     quarter = rows // 2
-    tile = 2 * rows
-    tiles = n // tile
-
-    def body(ids, own_ref, rec_ref, mat, mat_half, sine_ref, cosine_ref, keep, send, phased, out, field):
-        i = pl.program_id(0)
-
-        @pl.when(i == 0)
-        def _():
-            for at, ref in enumerate((own_ref, rec_ref)):
-                to = pl.ds(pl.multiple_of((ids[0] ^ at) * half, half), half)
-                field[pl.ds(0, lines), to] = ref[0]
-                field[pl.ds(lines, lines), to] = ref[1]
-
-        @pl.when(i < tiles)
-        def _():
-            q_re = dot_lines(field[...], mat[0])
-            q_im = dot_lines(field[...], mat[1])
+    tile = n // TILES
+
+    def body(ids, own_ref, rec_ref, mat, sine_ref, cosine_ref, keep, send, phased, out, field):
+        for at, ref in enumerate((own_ref, rec_ref)):
+            to = pl.ds(pl.multiple_of((ids[0] ^ at) * half, half), half)
+            field[pl.ds(0, lines), to] = ref[0]
+            field[pl.ds(lines, lines), to] = ref[1]
+        first = ids[3] == 0
+        for i in range(TILES * CHUNKS):
+            cols = pl.ds(i * (tile // CHUNKS), tile // CHUNKS)
+            q_re = dot_lines(field[...], mat[0, cols])
+            q_im = dot_lines(field[...], mat[1, cols])
             new_re = q_re[:lines] - q_im[lines:]
             new_im = q_re[lines:] + q_im[:lines]
-            cols = pl.ds(pl.multiple_of(i * tile, tile), tile)
-            first = ids[3] == 0
-            re, im = rotated(new_re, new_im, sine_ref[...], cosine_ref[...])
+            re, im = rotated(new_re, new_im, sine_ref[:, cols], cosine_ref[:, cols])
             phased[0, :, cols] = re
             phased[1, :, cols] = im
             for part, new in enumerate((new_re, new_im)):
@@ -307,69 +287,46 @@
                     odd = new[lo + quarter : lo + 2 * quarter].astype(BF)
                     keep[part, z, :, cols] = jnp.where(first, even, odd)
                     send[part, z, :, cols] = jnp.where(first, odd, even)
-
-        @pl.when(i >= tiles)
-        def _():
-            left = phased[...].reshape(2 * lines, n)
-            q_re = dot_lines(left, mat_half[0])
-            q_im = dot_lines(left, mat_half[1])
-            cols = pl.ds(pl.multiple_of((i - tiles) * tile, tile), tile)
-            out[0, :, cols] = (q_re[:lines] - q_im[lines:]).astype(BF)
-            out[1, :, cols] = (q_re[lines:] + q_im[:lines]).astype(BF)
-
-    flat = lambda rank: (lambda i, ids: (0,) * rank)
-    part_shape = (2, slices // 2, quarter, n)
-    per_half = half // tile
-    return call(
-        body,
-        (tiles + per_half,),
-        [
-            spec(own.shape, flat(3)),
-            spec(own.shape, flat(3)),
-            spec((2, tile, n), lambda i, ids: (0, jnp.minimum(i, tiles - 1), 0)),
-            spec(
-                (2, tile, n),
-                lambda i, ids: (0, (1 - ids[0]) * per_half + jnp.maximum(i - tiles, 0), 0),
-            ),
-            spec((lines, tile), lambda i, ids: (0, jnp.minimum(i, tiles - 1))),
-            spec((lines, tile), lambda i, ids: (0, jnp.minimum(i, tiles - 1))),
-        ],
-        [
-            (part_shape, BF, part_shape, flat(4)),
-            (part_shape, BF, part_shape, flat(4)),
-            ((2, lines, n), BF, (2, lines, n), flat(3)),
-            ((2, lines, half), BF, (2, lines, half), flat(3)),
-        ],
+        row_half(mat, 1 - ids[0], phased, out)
+
+    part = ((2, slices // 2, quarter, n), BF)
+    return solid(
+        body,
+        [part, part, ((2, lines, n), BF), ((2, lines, half), BF)],
         [pltpu.VMEM((2 * lines, n), BF)],
-        (ids, own, received, matrix, matrix, *waves),
+        (ids, own, received, matrix, *waves),
         12 * n * n * half,
-    )
-
-
-def row_rest(ids, phased, matrix, rows):
+        GRANT,
+    )
+
+
+def row_half(mat, side, field, out):
+    _, lines, n = field.shape
+    half = n // 2
+    chunk = half // CHUNKS
+    left = field[...].reshape(2 * lines, n)
+    for c in range(CHUNKS):
+        at = pl.ds(pl.multiple_of(side * half + c * chunk, chunk), chunk)
+        q_re = dot_lines(left, mat[0, at])
+        q_im = dot_lines(left, mat[1, at])
+        cols = pl.ds(c * chunk, chunk)
+        out[0, :, cols] = (q_re[:lines] - q_im[lines:]).astype(BF)
+        out[1, :, cols] = (q_re[lines:] + q_im[:lines]).astype(BF)
+
+
+def row_rest(ids, phased, matrix):
     _, lines, n = phased.shape
-    half = n // 2
-    tile = 2 * rows
-    per_half = half // tile
 
     def body(ids, field, mat, out):
-        left = field[...].reshape(2 * lines, n)
-        q_re = dot_lines(left, mat[0])
-        q_im = dot_lines(left, mat[1])
-        out[0] = (q_re[:lines] - q_im[lines:]).astype(BF)
-        out[1] = (q_re[lines:] + q_im[:lines]).astype(BF)
-
-    return call(
-        body,
-        (per_half,),
-        [
-            spec(phased.shape, lambda i, ids: (0, 0, 0)),
-            spec((2, tile, n), lambda i, ids: (0, ids[0] * per_half + i, 0)),
-        ],
-        [((2, lines, half), BF, (2, lines, tile), lambda i, ids: (0, 0, i))],
+        row_half(mat, ids[0], field, out)
+
+    return solid(
+        body,
+        [((2, lines, n // 2), BF)],
         [],
         (ids, phased, matrix),
-        4 * n * n * half,
+        4 * n * n * (n // 2),
+        GRANT,
     )[0]
 
 
@@ -381,53 +338,78 @@
     tile = 2 * rows
 
     def body(ids, own_ref, rec_ref, mat, m00, m01, m10, m11, field):
-        b = pl.program_id(0)
-
-        @pl.when(b == 0)
-        def _():
-            for at, ref in enumerate((own_ref, rec_ref)):
-                side = (ids[0] ^ at) * quarter
-                for part in range(2):
-                    for s in range(slices):
-                        to = pl.ds(pl.multiple_of(s * rows + side, quarter), quarter)
-                        field[part, to] = ref[part, pl.ds(s * quarter, quarter)]
-
-        left = mat[...].reshape(2 * tile, n)
-        q_re = dot_rows(left, field[0])
-        q_im = dot_rows(left, field[1])
-        new_re = (q_re[:tile] - q_im[tile:]).astype(BF)
-        new_im = q_im[:tile] + q_re[tile:]
+        for at, ref in enumerate((own_ref, rec_ref)):
+            side = (ids[0] ^ at) * quarter
+            for part in range(2):
+                for s in range(slices):
+                    to = pl.ds(pl.multiple_of(s * rows + side, quarter), quarter)
+                    field[part, to] = ref[part, pl.ds(s * quarter, quarter)]
         first = ids[3] == 0
-        new_im = jnp.where(first, new_im, -new_im).astype(BF)
-        for at, (near, far) in enumerate(((m00, m10), (m01, m11))):
-
-            @pl.when(b == at)
-            def _(near=near, far=far):
-                for part, new in enumerate((new_re, new_im)):
-                    near[part] = jnp.where(first, new[:rows], new[rows:])
-                    far[part] = jnp.where(first, new[rows:], new[:rows])
-
-    message = ((2, rows, half), BF, (2, rows, half), lambda b, ids: (0, 0, 0))
-    return call(
-        body,
-        (2,),
-        [
-            spec(own.shape, lambda b, ids: (0, 0, 0)),
-            spec(own.shape, lambda b, ids: (0, 0, 0)),
-            spec((2, tile, n), lambda b, ids: (0, (ids[0] ^ b) * 2 + (ids[4] ^ turn), 0)),
-        ],
-        [message] * 4,
+        for b, (near, far) in enumerate(((m00, m10), (m01, m11))):
+            at = (ids[0] ^ b) * 2 + (ids[4] ^ turn)
+            left = mat[:, pl.ds(pl.multiple_of(at * tile, tile), tile)].reshape(2 * tile, n)
+            q_re = dot_rows(left, field[0])
+            q_im = dot_rows(left, field[1])
+            new_re = (q_re[:tile] - q_im[tile:]).astype(BF)
+            new_im = q_im[:tile] + q_re[tile:]
+            new_im = jnp.where(first, new_im, -new_im).astype(BF)
+            for part, new in enumerate((new_re, new_im)):
+                near[part] = jnp.where(first, new[:rows], new[rows:])
+                far[part] = jnp.where(first, new[rows:], new[:rows])
+
+    return solid(
+        body,
+        [((2, rows, half), BF)] * 4,
         [pltpu.VMEM((2, n, half), BF)],
         (ids, own, received, matrix),
         4 * n * n * half,
-    )
-
-
-def arrive(ids, messages, image_weights, freqs):
+        GRANT,
+    )
+
+
+def last_term(ids, messages, image_weights):
     _, rows, half = messages[0].shape
+    high = rows // 2
 
     def body(ids, *refs):
-        ms, (wt, src, rec, grad, held, sems) = refs[:8], refs[8:]
+        ms, (wt, stay, away) = refs[:8], refs[8:]
+        sides = []
+        for b in range(2):
+            total = None
+            for turn in range(2):
+                s, r = ms[4 * turn + b], ms[4 * turn + 2 + b]
+                term = s[0].astype(F32) * r[0].astype(F32) + s[1].astype(F32) * r[1].astype(F32)
+                term = wt[ids[4] ^ turn] * term
+                total = term if total is None else total + term
+            sides.append(total)
+        left = ids[5] == 0
+        for b in range(2):
+            value = jnp.where(left, sides[b], sides[1 - b])
+            lo, hi = value[:high], value[high:]
+            first = ids[0] == 0
+            cols = pl.ds(b * half, half)
+            stay[:, cols] = jnp.where(first, lo, hi)
+            away[:, cols] = jnp.where(first, hi, lo).astype(BF)
+
+    shape = (high, 2 * half)
+    index = lambda i, ids: (0, 0)
+    return call(
+        body,
+        (1,),
+        [spec((2, rows, half), lambda i, ids: (0, 0, 0))] * 8 + [SMEM],
+        [(shape, F32, shape, index), (shape, BF, shape, index)],
+        [],
+        (ids, *messages, image_weights),
+        1 << 22,
+        14 << 20,
+    )
+
+
+def arrive(ids, messages, freqs):
+    _, rows, half = messages[0].shape
+
+    def body(ids, *refs):
+        ms, (src, rec, held, sems) = refs[:8], refs[8:]
         copies = [
             pltpu.make_async_copy(m, held.at[at], sems.at[at]) for at, m in enumerate(ms)
         ]
@@ -436,35 +418,24 @@
         for copy in copies:
             copy.wait()
         for side in range(2):
-            total = None
             for j in range(freqs):
                 a_hi = ids[4] ^ j
                 b = ids[5] ^ side
-                s_at = (a_hi * 2 + ids[3]) * 2 + b
-                r_at = (a_hi * 2 + (1 - ids[3])) * 2 + b
-                s, r = held[s_at], held[r_at]
                 cols = pl.ds(side * half, half)
-                src[:, j, :, cols] = s
-                rec[:, j, :, cols] = r
-                s, r = s.astype(F32), r.astype(F32)
-                term = wt[j] * (s[0] * r[0] + s[1] * r[1])
-                total = term if total is None else total + term
-            grad[:, pl.ds(side * half, half)] = total.astype(BF)
-
-    flat = lambda rank: (lambda i, ids: (0,) * rank)
+                src[:, j, :, cols] = held[(a_hi * 2 + ids[3]) * 2 + b]
+                rec[:, j, :, cols] = held[(a_hi * 2 + (1 - ids[3])) * 2 + b]
+
     full = (2, freqs, rows, 2 * half)
+    index = lambda i, ids: (0, 0, 0, 0)
     return call(
         body,
         (1,),
-        [ANY] * 8 + [SMEM],
-        [
-            (full, BF, full, flat(4)),
-            (full, BF, full, flat(4)),
-            ((rows, 2 * half), BF, (rows, 2 * half), flat(2)),
-        ],
+        [ANY] * 8,
+        [(full, BF, full, index), (full, BF, full, index)],
         [pltpu.VMEM((8, 2, rows, half), BF), pltpu.SemaphoreType.DMA((8,))],
-        (ids, *messages, image_weights),
+        (ids, *messages),
         1 << 22,
+        12 << 20,
     )
 
 
@@ -491,7 +462,37 @@
         [],
         (ids, keep, other, weight),
         1 << 22,
-    )
+        8 << 20,
+    )
+
+
+def gradient_rows(ids, quad, mine, theirs):
+    quarter, half = quad.shape[-2:]
+    rows, cols = 2 * quarter, 2 * half
+
+    def body(ids, quad_ref, mine_ref, theirs_ref, out):
+        for a in range(2):
+            for b in range(2):
+                to = (pl.ds(a * quarter, quarter), pl.ds(b * half, half))
+                out[(0, *to)] = quad_ref[ids[1] ^ a, ids[0] ^ b, 0].astype(F32)
+                out[(1, *to)] = quad_ref[ids[1] ^ b, ids[0] ^ a, 1].astype(F32)
+        first = ids[0] == 0
+        own, other = mine_ref[...].astype(F32), theirs_ref[...].astype(F32)
+        out[2, pl.ds(0, quarter)] = jnp.where(first, own, other)
+        out[2, pl.ds(quarter, quarter)] = jnp.where(first, other, own)
+
+    flat = lambda rank: (lambda i, ids: (0,) * rank)
+    full = (3, rows, cols)
+    return call(
+        body,
+        (1,),
+        [spec(quad.shape, flat(5)), spec(mine.shape, flat(2)), spec(mine.shape, flat(2))],
+        [(full, F32, full, flat(3))],
+        [],
+        (ids, quad, mine, theirs),
+        1 << 20,
+        8 << 20,
+    )[0]
 
 
 def flip(size, bit):
@@ -535,9 +536,12 @@
     piece = (piece * LENS_GAIN).astype(jnp.float16)
     line = [piece] + [lax.ppermute(piece, "space", flip(space, 2 * k)) for k in (1, 2, 3)]
     line = jnp.stack(line, axis=1)
-    across_y = lax.ppermute(line, "space", flip(space, 1))
-    planes = [jnp.concatenate([line[d], across_y[d]]) for d in range(2)]
-    across_x = [lax.ppermute(planes[d], "freq", flip(groups, 2)) for d in range(2)]
+    other_line = lax.ppermute(line, "space", flip(space, 1))
+    planes = [jnp.concatenate([line[d], other_line[d]]) for d in range(2)]
+    stacks = [
+        jnp.concatenate([planes[d], lax.ppermute(planes[d], "freq", flip(groups, 2))])
+        for d in range(2)
+    ]
 
     solved = home_solve(ids, 0, source, receiver, matrix, lens, omegas)
     messages = send(solved, 0, going)
@@ -553,10 +557,7 @@
     theirs = lax.ppermute(held, "freq", swap)
     line_matrix = jnp.where(mine, held, theirs)
 
-    waves = []
-    for d in range(2):
-        stack = jnp.concatenate([planes[d], across_x[d]]).astype(F32)
-        waves.append(trig(ids, stack, omega, d == 1))
+    waves = [trig(ids, stacks[d].astype(F32), omega, d == 1) for d in range(2)]
 
     keep0, send0, phased, sent = column_solve(ids, messages, line_matrix, waves[0])
     came = lax.ppermute(sent, "freq", swap)
@@ -565,42 +566,37 @@
     keep1, send1, phased, sent = row_solve(ids, own, came, line_matrix, waves[1], rows)
     came = lax.ppermute(sent, "freq", swap)
     partner1 = lax.ppermute(send1, "space", flip(space, 1))
-    own = row_rest(ids, phased, line_matrix, rows)
+    own = row_rest(ids, phased, line_matrix)
 
     solved = last_solve(ids, 0, own, came, line_matrix, rows)
     finals = send(solved, 0, coming)
     solved = last_solve(ids, 1, own, came, line_matrix, rows)
     finals += send(solved, 1, coming)
 
-    pieces = []
+    sums = []
     for depth, keep, partner in ((0, keep0, partner0), (1, keep1, partner1)):
         stay, away = image_terms(ids, keep, partner, weight, depth == 1)
-        over_x = stay + lax.ppermute(away, "freq", flip(groups, 2)).astype(F32)
-
-        def slab(at):
-            return lax.dynamic_index_in_dim(over_x, at, 0, keepdims=False)
-
-        total = slab(z)
-        for k in (1, 2, 3):
-            part = lax.ppermute(slab(z ^ k).astype(BF), "space", flip(space, 2 * k))
-            total = total + part.astype(F32)
-        pieces.append(total.astype(BF))
-    piece = jnp.stack(pieces)
-    pair = jnp.stack([piece, lax.ppermute(piece, "freq", swap)])
-    quad = jnp.stack([pair, lax.ppermute(pair, "freq", flip(groups, 2))])
-
-    def at_of(px, pc, depth):
-        return lax.dynamic_slice(
-            quad, (x ^ px, core ^ pc, depth, 0, 0), (1, 1, 1, quarter, half)
-        )[0, 0, 0].astype(F32)
-
-    grad0 = jnp.block([[at_of(0, 0, 0), at_of(0, 1, 0)], [at_of(1, 0, 0), at_of(1, 1, 0)]])
-    grad1 = jnp.block([[at_of(0, 0, 1), at_of(1, 0, 1)], [at_of(0, 1, 1), at_of(1, 1, 1)]])
-
-    source_out, receiver_out, term2 = arrive(ids, finals, image_weights, freqs)
-    chip = term2.astype(F32) + lax.ppermute(term2, "freq", swap).astype(F32)
-    grad2 = chip + lax.ppermute(chip.astype(BF), "freq", flip(groups, 2)).astype(F32)
-    return source_out, receiver_out, jnp.stack([grad0, grad1, grad2])
+        sums.append(stay + lax.ppermute(away, "freq", flip(groups, 2)).astype(F32))
+
+    def half_of(v, at, axis):
+        return lax.dynamic_index_in_dim(v, at, axis, keepdims=False)
+
+    low, high = z % 2, z // 2
+    paired = jnp.stack(sums, axis=1).reshape(2, 2, 2, quarter, half)
+    near = lax.ppermute(half_of(paired, 1 - low, 1).astype(BF), "space", flip(space, 2))
+    pair = half_of(paired, low, 1) + near.astype(F32)
+    far = lax.ppermute(half_of(pair, 1 - high, 0).astype(BF), "space", flip(space, 4))
+    piece = (half_of(pair, high, 0) + far.astype(F32)).astype(BF)
+    pair = jnp.stack([piece, lax.ppermute(piece, "freq", flip(groups, 2))])
+    quad = jnp.stack([pair, lax.ppermute(pair, "freq", swap)], axis=1)
+
+    stay, away = last_term(ids, finals, image_weights)
+    chip = (stay + lax.ppermute(away, "freq", swap).astype(F32)).astype(BF)
+    both_x = chip.astype(F32) + lax.ppermute(chip, "freq", flip(groups, 2)).astype(F32)
+    mine2 = both_x.astype(BF)
+    theirs2 = lax.ppermute(mine2, "freq", swap)
+    source_out, receiver_out = arrive(ids, finals, freqs)
+    return source_out, receiver_out, gradient_rows(ids, quad, mine2, theirs2)
 
 
 def to_blocks(matrix, pieces):

time: 234 us -> 233 us (level)
  starting transfers between devices: 63.6 us -> 53.7 us
  waiting for transfers between devices: 84.6 us -> 93.9 us
  Pallas kernels: 67.9 us -> 62.2 us
  local copies, waits for them, and re-layouts: 10.9 us -> 15.8 us
    pallas_call x13 -> x9, Pallas kernels: 67.9 us -> 31.5 us  [call(): pl.pallas_call(body, out_shape=[jax.ShapeDtypeStruct(s, d) for s, d, _, _...]
    pallas_call x0 -> x6, Pallas kernels: none -> 30.7 us  [solid(): pl.pallas_call(body, out_shape=[jax.ShapeDtypeStruct(s, d) for s, d in ou...]
    ppermute x1, waiting for transfers between devices: 0.01 us -> 12.1 us  [plane_per_chip(): partner0 = lax.ppermute(send0, 'space', flip(space, 1))]
    ppermute x16, waiting for transfers between devices: 38.4 us -> 26.9 us  [send(): lax.ppermute(m, both, rounds[4 * turn + at])]
    ppermute x1, waiting for transfers between devices: 2.57 us -> 10.8 us  [plane_per_chip(): partner1 = lax.ppermute(send1, 'space', flip(space, 1))]
    ppermute x13 -> x10, starting transfers between devices: 28.3 us -> 22.2 us  [the longest x1 10.7 us: plane_per_chip(): chip = (stay + lax.ppermute(away, 'freq', swap).astype(F32)).astype(BF)]
    unnamed x30 -> x46, local copies, waits for them, and re-layouts: 3.83 us -> 8.07 us
    ppermute x16, starting transfers between devices: 22.6 us -> 19.1 us  [send(): lax.ppermute(m, both, rounds[4 * turn + at])]
  transfers between devices with their start and end apart: 40 -> 37, of which waited for: 21 -> 17; matrix products, arithmetic and copies ran while one was open for 3% -> 4% of each run, Pallas kernels for 24% -> 23%
where the time goes in v3:
time: 233 us; the launch traced here: 232 us
  waiting for transfers between devices  93.9 us (40%)
  Pallas kernels  62.2 us (27%)
  starting transfers between devices  53.7 us (23%)
  local copies, waits for them, and re-layouts  15.8 us (7%)
  other arithmetic  5.11 us (2%)
    pallas_call x9, Pallas kernels, call(): pl.pallas_call(body, out_shape=[jax.ShapeDtypeStruct(s, d) for s, d, _, _...  31.5 us
    pallas_call x6, Pallas kernels, solid(): pl.pallas_call(body, out_shape=[jax.ShapeDtypeStruct(s, d) for s, d in ou...  30.7 us
    ppermute x16, waiting for transfers between devices, send(): lax.ppermute(m, both, rounds[4 * turn + at])  26.9 us
    ppermute x16, starting transfers between devices, send(): lax.ppermute(m, both, rounds[4 * turn + at])  19.1 us
    ppermute x2, waiting for transfers between devices, plane_per_chip(): lax.ppermute(planes[d], 'freq', flip(groups, 2))  16.1 us
    ppermute x1, waiting for transfers between devices, plane_per_chip(): partner0 = lax.ppermute(send0, 'space', flip(space, 1))  12.1 us
    ppermute x1, waiting for transfers between devices, plane_per_chip(): lax.ppermute(half_of(paired, 1 - low, 1).astype(BF), 'space', flip(space,...  11.3 us
    ppermute x1, waiting for transfers between devices, plane_per_chip(): partner1 = lax.ppermute(send1, 'space', flip(space, 1))  10.8 us
  transfers between devices with their start and end apart: 37, of which 17 were waited for; matrix products, arithmetic and copies ran while one was open for 4% of the time, Pallas kernels for 23%

profile of v3, /device:TPU:0, one launch (start us, length us, event | category | flops | bytes accessed | tf_op | source)
XLA Modules:
  0.0 232.0 jit_solution(10656590733320650181)
XLA Ops:
  0.7 4.7 %dynamic-slice_bitcast_fusion = bf16[2,1024,1024]{2,1,0:T(8,128)(2,1)} fusion(bf16[2,2,1024,1024]{3,2,1,0:T(8,128)(2,1)} %mat.3, s32[]{:T(128)S(6)} %select_n.84), kind=kLoop, calls=%fused_computation | loop fusion | bytes 8388612 | tf_op jit(solution)/shard_map/squeeze | solution.py:556
  12.1 3.7 %collective-permute-done.9 = f16[2,64,512]{2,1,0:T(8,128)(2,1)S(1)} collective-permute-done((f16[2,64,512]{2,1,0:T(8,128)(2,1)S(1)}, f16[2,64,512]{2,1,0:T(8,128)(2,1)S(1)}, u32[]{:S(2)}, u32[]{:S(2)}) %collective-permute-start.9) | collective-permute-done | bytes 131104 | tf_op jit(solution)/shard_map/ppermute | solution.py:537
  15.8 6.6 %collective-permute-done.10 = f16[2,64,512]{2,1,0:T(8,128)(2,1)S(1)} collective-permute-done((f16[2,64,512]{2,1,0:T(8,128)(2,1)S(1)}, f16[2,64,512]{2,1,0:T(8,128)(2,1)S(1)}, u32[]{:S(2)}, u32[]{:S(2)}) %collective-permute-start.10) | collective-permute-done | bytes 131104 | tf_op jit(solution)/shard_map/ppermute | solution.py:537
  24.9 7.4 %shard_map.85 = (bf16[2,128,512]{2,1,0:T(8,128)(2,1)}, bf16[2,128,512]{2,1,0:T(8,128)(2,1)}, bf16[2,128,512]{2,1,0:T(8,128)(2,1)}, bf16[2,128,512]{2,1,0:T(8,128)(2,1)}) custom-call(s32[6]{0:T(128)} %stack.76.ids, bf16[2,2,128,1024]{3,2,1,0:T(8,128)(2,1)} %src.3, bf16[2,2,128,1024]{3,2,1,0:T(8,128)(2,1)} %rec.3, bf16[2,2,1024,1024]{3,2,1,0:T(8,128)(2,1)} %mat.3, ...), custom_call_target="tpu_custom_call" | custom-call | flops 2147483648 | bytes 8388608 | tf_op jit(solution)/shard_map/pallas_call | solution.py:53
  33.9 4.1 %collective-permute-start.1 = (bf16[2,128,512]{2,1,0:T(8,128)(2,1)}, bf16[2,128,512]{2,1,0:T(8,128)(2,1)S(1)}, u32[]{:S(2)}, u32[]{:S(2)}) collective-permute-start(bf16[2,128,512]{2,1,0:T(8,128)(2,1)} %get-tuple-element.40), channel_id=1, source_target_pairs={{0,8},{1,9},{2,10},{3,11},{4,0},{5,1},{6,2},{7,3},{8,12},{9,13},{1... | collective-permute-start | bytes 786440 | tf_op jit(solution)/shard_map/ppermute | solution.py:530
  40.0 7.4 %shard_map.86 = (bf16[2,128,512]{2,1,0:T(8,128)(2,1)}, bf16[2,128,512]{2,1,0:T(8,128)(2,1)}, bf16[2,128,512]{2,1,0:T(8,128)(2,1)}, bf16[2,128,512]{2,1,0:T(8,128)(2,1)}) custom-call(s32[6]{0:T(128)} %stack.76.ids, bf16[2,2,128,1024]{3,2,1,0:T(8,128)(2,1)} %src.3, bf16[2,2,128,1024]{3,2,1,0:T(8,128)(2,1)} %rec.3, bf16[2,2,1024,1024]{3,2,1,0:T(8,128)(2,1)} %mat.3, ...), custom_call_target="tpu_custom_call" | custom-call | flops 2147483648 | bytes 8388608 | tf_op jit(solution)/shard_map/pallas_call | solution.py:53
  48.6 3.7 %collective-permute-done.13 = f16[8,64,512]{2,1,0:T(8,128)(2,1)S(1)} collective-permute-done((f16[8,64,512]{2,1,0:T(8,128)(2,1)S(1)}, f16[8,64,512]{2,1,0:T(8,128)(2,1)S(1)}, u32[]{:S(2)}, u32[]{:S(2)}) %collective-permute-start.13) | collective-permute-done | bytes 524320 | tf_op jit(solution)/shard_map/ppermute | solution.py:542
  52.7 3.8 %shard_map.87 = (f32[1024,512]{1,0:T(8,128)S(1)}, f32[1024,512]{1,0:T(8,128)S(1)}) custom-call(s32[6]{0:T(128)S(1)} %copy-done.3, f32[16,64,512]{2,1,0:T(8,128)S(1)} %maximum_convert_fusion.pieces, f32[1]{0:T(128)} %bitcast.19.om), custom_call_target="tpu_custom_call" | custom-call | flops 67108864 | bytes 8388608 | tf_op jit(solution)/shard_map/pallas_call | solution.py:53
  56.7 3.1 %collective-permute-start.5 = (bf16[2,128,512]{2,1,0:T(8,128)(2,1)S(1)}, bf16[2,128,512]{2,1,0:T(8,128)(2,1)S(1)}, u32[]{:S(2)}, u32[]{:S(2)}) collective-permute-start(bf16[2,128,512]{2,1,0:T(8,128)(2,1)S(1)} %copy-done.21), channel_id=1, source_target_pairs={{0,10},{1,11},{2,8},{3,9},{4,2},{5,3},{6,0},{7,1},{8,14},{9,15},{1... | collective-permute-start | bytes 786440 | tf_op jit(solution)/shard_map/ppermute | solution.py:530
  64.0 5.0 %collective-permute-done.4.refs_4_ = bf16[2,128,512]{2,1,0:T(8,128)(2,1)S(1)} collective-permute-done((bf16[2,128,512]{2,1,0:T(8,128)(2,1)S(1)}, bf16[2,128,512]{2,1,0:T(8,128)(2,1)S(1)}, u32[]{:S(2)}, u32[]{:S(2)}) %collective-permute-start.4) | collective-permute-done | bytes 262176 | tf_op jit(solution)/shard_map/ppermute | solution.py:530
  69.0 3.0 %collective-permute-done.5.refs_5_ = bf16[2,128,512]{2,1,0:T(8,128)(2,1)S(1)} collective-permute-done((bf16[2,128,512]{2,1,0:T(8,128)(2,1)S(1)}, bf16[2,128,512]{2,1,0:T(8,128)(2,1)S(1)}, u32[]{:S(2)}, u32[]{:S(2)}) %collective-permute-start.5) | collective-permute-done | bytes 262176 | tf_op jit(solution)/shard_map/ppermute | solution.py:530
  72.0 8.7 %collective-permute-done.6.refs_6_ = bf16[2,128,512]{2,1,0:T(8,128)(2,1)S(1)} collective-permute-done((bf16[2,128,512]{2,1,0:T(8,128)(2,1)S(1)}, bf16[2,128,512]{2,1,0:T(8,128)(2,1)S(1)}, u32[]{:S(2)}, u32[]{:S(2)}) %collective-permute-start.6) | collective-permute-done | bytes 262176 | tf_op jit(solution)/shard_map/ppermute | solution.py:530
  83.3 8.2 %shard_map.88 = (bf16[2,4,128,512]{3,2,1,0:T(8,128)(2,1)S(1)}, bf16[2,4,128,512]{3,2,1,0:T(8,128)(2,1)S(1)}, bf16[2,1024,512]{2,1,0:T(8,128)(2,1)S(1)}, bf16[2,512,512]{2,1,0:T(8,128)(2,1)S(1)}) custom-call(s32[6]{0:T(128)S(1)} %copy-done.3, bf16[2,128,512]{2,1,0:T(8,128)(2,1)S(1)} %collective-permute-done.refs_0_, ...), custom_call_target="tpu_custom_call" | custom-call | flops 6442450944 | bytes 8388608 | tf_op jit(solution)/shard_map/pallas_call | solution.py:72
  94.5 12.4 %collective-permute-done.16 = f16[8,64,512]{2,1,0:T(8,128)(2,1)S(1)} collective-permute-done((f16[8,64,512]{2,1,0:T(8,128)(2,1)S(1)}, f16[8,64,512]{2,1,0:T(8,128)(2,1)S(1)}, u32[]{:S(2)}, u32[]{:S(2)}) %collective-permute-start.16) | collective-permute-done | bytes 524320 | tf_op jit(solution)/shard_map/ppermute | solution.py:542
  107.2 4.0 %shard_map.90 = (f32[512,1024]{1,0:T(8,128)S(1)}, f32[512,1024]{1,0:T(8,128)S(1)}) custom-call(s32[6]{0:T(128)S(1)} %copy-done.3, f32[16,64,512]{2,1,0:T(8,128)S(1)} %maximum_convert_fusion.1.pieces, f32[1]{0:T(128)} %bitcast.19.om), custom_call_target="tpu_custom_call" | custom-call | flops 67108864 | bytes 8388608 | tf_op jit(solution)/shard_map/pallas_call | solution.py:53
  115.4 9.0 %shard_map.91 = (bf16[2,4,64,1024]{3,2,1,0:T(8,128)(2,1)S(1)}, bf16[2,4,64,1024]{3,2,1,0:T(8,128)(2,1)}, bf16[2,512,1024]{2,1,0:T(8,128)(2,1)S(1)}, bf16[2,512,512]{2,1,0:T(8,128)(2,1)}) custom-call(s32[6]{0:T(128)S(1)} %copy-done.3, bf16[2,512,512]{2,1,0:T(8,128)(2,1)S(1)} %shard_map.89.own_ref, bf16[2,512,512]{2,1,0:T(8,128)(2,1)S(1)} %collective-permute-done.15.rec_ref, ...), custom_call_target="tpu_custom_call" | custom-call | flops 6442450944 | bytes 8388608 | tf_op jit(solution)/shard_map/pallas_call | solution.py:72
  125.3 12.1 %collective-permute-done.26.o = bf16[2,4,128,512]{3,2,1,0:T(8,128)(2,1)S(1)} collective-permute-done((bf16[2,4,128,512]{3,2,1,0:T(8,128)(2,1)S(1)}, bf16[2,4,128,512]{3,2,1,0:T(8,128)(2,1)S(1)}, u32[]{:S(2)}, u32[]{:S(2)}) %collective-permute-start.26) | collective-permute-done | bytes 1048608 | tf_op jit(solution)/shard_map/ppermute | solution.py:564
  147.3 10.8 %collective-permute-done.28.o = bf16[2,4,64,1024]{3,2,1,0:T(8,128)(2,1)S(1)} collective-permute-done((bf16[2,4,64,1024]{3,2,1,0:T(8,128)(2,1)}, bf16[2,4,64,1024]{3,2,1,0:T(8,128)(2,1)S(1)}, u32[]{:S(2)}, u32[]{:S(2)}) %collective-permute-start.28) | collective-permute-done | bytes 1048608 | tf_op jit(solution)/shard_map/ppermute | solution.py:568
  161.3 3.9 %shard_map.94 = (bf16[2,128,512]{2,1,0:T(8,128)(2,1)S(1)}, bf16[2,128,512]{2,1,0:T(8,128)(2,1)S(1)}, bf16[2,128,512]{2,1,0:T(8,128)(2,1)S(1)}, bf16[2,128,512]{2,1,0:T(8,128)(2,1)S(1)}) custom-call(s32[6]{0:T(128)S(1)} %copy-done.3, bf16[2,512,512]{2,1,0:T(8,128)(2,1)S(1)} %shard_map.92.own_ref, bf16[2,512,512]{2,1,0:T(8,128)(2,1)} %collective-permute-done.17.rec_ref, ...), custom_call_target="tpu_custom_call" | custom-call | flops 2147483648 | bytes 8388608 | tf_op jit(solution)/shard_map/pallas_call | solution.py:72
  176.9 3.8 %shard_map.93 = (bf16[2,128,512]{2,1,0:T(8,128)(2,1)S(1)}, bf16[2,128,512]{2,1,0:T(8,128)(2,1)S(1)}, bf16[2,128,512]{2,1,0:T(8,128)(2,1)S(1)}, bf16[2,128,512]{2,1,0:T(8,128)(2,1)S(1)}) custom-call(s32[6]{0:T(128)S(1)} %copy-done.3, bf16[2,512,512]{2,1,0:T(8,128)(2,1)S(1)} %copy-done.8, bf16[2,512,512]{2,1,0:T(8,128)(2,1)} %collective-permute-done.17.rec_ref, ...), custom_call_target="tpu_custom_call" | custom-call | flops 2147483648 | bytes 8388608 | tf_op jit(solution)/shard_map/pallas_call | solution.py:72
  184.4 4.0 %collective-permute-done.24.refs_6_ = bf16[2,128,512]{2,1,0:T(8,128)(2,1)S(1)} collective-permute-done((bf16[2,128,512]{2,1,0:T(8,128)(2,1)S(1)}, bf16[2,128,512]{2,1,0:T(8,128)(2,1)S(1)}, u32[]{:S(2)}, u32[]{:S(2)}) %collective-permute-start.24) | collective-permute-done | bytes 262176 | tf_op jit(solution)/shard_map/ppermute | solution.py:530
  189.2 11.3 %collective-permute-done.30 = bf16[2,2,64,512]{3,2,1,0:T(8,128)(2,1)} collective-permute-done((bf16[2,2,64,512]{3,2,1,0:T(8,128)(2,1)S(1)}, bf16[2,2,64,512]{3,2,1,0:T(8,128)(2,1)}, u32[]{:S(2)}, u32[]{:S(2)}) %collective-permute-start.30) | collective-permute-done | bytes 262176 | tf_op jit(solution)/shard_map/ppermute | solution.py:586
  208.7 10.7 %collective-permute-start.34 = (bf16[64,1024]{1,0:T(8,128)(2,1)S(1)}, bf16[64,1024]{1,0:T(8,128)(2,1)S(1)}, u32[]{:S(2)}, u32[]{:S(2)}) collective-permute-start(bf16[64,1024]{1,0:T(8,128)(2,1)S(1)} %get-tuple-element.74), channel_id=1, source_target_pairs={{0,8},{8,0},{16,24},{24,16},{1,9},{9,1},{17,25},{25,17},{2,10},{10... | collective-permute-start | bytes 393224 | tf_op jit(solution)/shard_map/ppermute | solution.py:594
  221.6 4.2 %collective-permute-done.32 = bf16[2,64,512]{2,1,0:T(8,128)(2,1)S(1)} collective-permute-done((bf16[2,64,512]{2,1,0:T(8,128)(2,1)S(1)}, bf16[2,64,512]{2,1,0:T(8,128)(2,1)S(1)}, u32[]{:S(2)}, u32[]{:S(2)}) %collective-permute-start.32) | collective-permute-done | bytes 131104 | tf_op jit(solution)/shard_map/ppermute | solution.py:590
  (138 shorter events, 75.0 us)
Async XLA Ops:
  5.3 55.7 %collective-permute-start.8 = (bf16[2,1024,1024]{2,1,0:T(8,128)(2,1)}, bf16[2,1024,1024]{2,1,0:T(8,128)(2,1)}, u32[]{:S(2)}, u32[]{:S(2)}) collective-permute-start(bf16[2,1024,1024]{2,1,0:T(8,128)(2,1)} %dynamic-slice_bitcast_fusion), channel_id=1, source_target_pairs={{0,8},{8,0},{16,24},{24,16},{1,9},{9,1},{17,25},{25,17},{2,10},{10... | collective-permute-start | bytes 12582920 | tf_op jit(solution)/shard_map/ppermute | solution.py:557
  22.6 15.5 %collective-permute-start.12 = (f16[2,4,64,512]{3,2,1,0:T(8,128)(2,1)S(1)}, f16[2,4,64,512]{3,2,1,0:T(8,128)(2,1)S(1)}, u32[]{:S(2)}, u32[]{:S(2)}) collective-permute-start(f16[2,4,64,512]{3,2,1,0:T(8,128)(2,1)S(1)} %pad_maximum_fusion), channel_id=1, source_target_pairs={{0,1},{1,0},{2,3},{3,2},{4,5},{5,4},{6,7},{7,6},{8,9},{9,8},{10,11... | collective-permute-start | bytes 1572872 | tf_op jit(solution)/shard_map/ppermute | solution.py:539
  24.2 23.2 %collective-permute-start.14 = (f32[2,2]{1,0:T(2,128)S(1)}, f32[2,2]{1,0:T(2,128)S(1)}, u32[]{:S(2)}, u32[]{:S(2)}) collective-permute-start(f32[2,2]{1,0:T(2,128)S(1)} %pad_maximum_fusion.5), channel_id=1, source_target_pairs={{0,8},{8,0},{16,24},{24,16},{1,9},{9,1},{17,25},{25,17},{2,10},{10... | collective-permute-start | bytes 56 | tf_op jit(solution)/shard_map/ppermute | solution.py:553
  32.3 24.2 %collective-permute-start = (bf16[2,128,512]{2,1,0:T(8,128)(2,1)}, bf16[2,128,512]{2,1,0:T(8,128)(2,1)S(1)}, u32[]{:S(2)}, u32[]{:S(2)}) collective-permute-start(bf16[2,128,512]{2,1,0:T(8,128)(2,1)} %get-tuple-element.39), channel_id=1, source_target_pairs={{0,0},{1,1},{2,2},{3,3},{4,8},{5,9},{6,10},{7,11},{8,4},{9,5},{10,... | collective-permute-start | bytes 786440 | tf_op jit(solution)/shard_map/ppermute | solution.py:530
  33.9 22.7 %collective-permute-start.1 = (bf16[2,128,512]{2,1,0:T(8,128)(2,1)}, bf16[2,128,512]{2,1,0:T(8,128)(2,1)S(1)}, u32[]{:S(2)}, u32[]{:S(2)}) collective-permute-start(bf16[2,128,512]{2,1,0:T(8,128)(2,1)} %get-tuple-element.40), channel_id=1, source_target_pairs={{0,8},{1,9},{2,10},{3,11},{4,0},{5,1},{6,2},{7,3},{8,12},{9,13},{1... | collective-permute-start | bytes 786440 | tf_op jit(solution)/shard_map/ppermute | solution.py:530
  38.4 13.9 %collective-permute-start.13 = (f16[8,64,512]{2,1,0:T(8,128)(2,1)S(1)}, f16[8,64,512]{2,1,0:T(8,128)(2,1)S(1)}, u32[]{:S(2)}, u32[]{:S(2)}) collective-permute-start(f16[8,64,512]{2,1,0:T(8,128)(2,1)S(1)} %pad_maximum_fusion.1), channel_id=1, source_target_pairs={{0,16},{8,24},{16,0},{24,8},{1,17},{9,25},{17,1},{25,9},{2,18},{10... | collective-permute-start | bytes 1572872 | tf_op jit(solution)/shard_map/ppermute | solution.py:542
  56.7 15.3 %collective-permute-start.5 = (bf16[2,128,512]{2,1,0:T(8,128)(2,1)S(1)}, bf16[2,128,512]{2,1,0:T(8,128)(2,1)S(1)}, u32[]{:S(2)}, u32[]{:S(2)}) collective-permute-start(bf16[2,128,512]{2,1,0:T(8,128)(2,1)S(1)} %copy-done.21), channel_id=1, source_target_pairs={{0,10},{1,11},{2,8},{3,9},{4,2},{5,3},{6,0},{7,1},{8,14},{9,15},{1... | collective-permute-start | bytes 786440 | tf_op jit(solution)/shard_map/ppermute | solution.py:530
  59.8 20.9 %collective-permute-start.6 = (bf16[2,128,512]{2,1,0:T(8,128)(2,1)S(1)}, bf16[2,128,512]{2,1,0:T(8,128)(2,1)S(1)}, u32[]{:S(2)}, u32[]{:S(2)}) collective-permute-start(bf16[2,128,512]{2,1,0:T(8,128)(2,1)S(1)} %copy-done.19), channel_id=1, source_target_pairs={{0,3},{1,2},{2,1},{3,0},{4,11},{5,10},{6,9},{7,8},{8,7},{9,6},{10,... | collective-permute-start | bytes 786440 | tf_op jit(solution)/shard_map/ppermute | solution.py:530
  61.1 22.2 %collective-permute-start.7 = (bf16[2,128,512]{2,1,0:T(8,128)(2,1)S(1)}, bf16[2,128,512]{2,1,0:T(8,128)(2,1)S(1)}, u32[]{:S(2)}, u32[]{:S(2)}) collective-permute-start(bf16[2,128,512]{2,1,0:T(8,128)(2,1)S(1)} %copy-done.18), channel_id=1, source_target_pairs={{0,11},{1,10},{2,9},{3,8},{4,3},{5,2},{6,1},{7,0},{8,15},{9,14},{1... | collective-permute-start | bytes 786440 | tf_op jit(solution)/shard_map/ppermute | solution.py:530
  91.5 23.9 %collective-permute-start.15 = (bf16[2,512,512]{2,1,0:T(8,128)(2,1)S(1)}, bf16[2,512,512]{2,1,0:T(8,128)(2,1)S(1)}, u32[]{:S(2)}, u32[]{:S(2)}) collective-permute-start(bf16[2,512,512]{2,1,0:T(8,128)(2,1)S(1)} %get-tuple-element.50), channel_id=1, source_target_pairs={{0,8},{8,0},{16,24},{24,16},{1,9},{9,1},{17,25},{25,17},{2,10},{10... | collective-permute-start | bytes 3145736 | tf_op jit(solution)/shard_map/ppermute | solution.py:563
  93.0 13.9 %collective-permute-start.16 = (f16[8,64,512]{2,1,0:T(8,128)(2,1)S(1)}, f16[8,64,512]{2,1,0:T(8,128)(2,1)S(1)}, u32[]{:S(2)}, u32[]{:S(2)}) collective-permute-start(f16[8,64,512]{2,1,0:T(8,128)(2,1)S(1)} %pad_maximum_fusion.2), channel_id=1, source_target_pairs={{0,16},{8,24},{16,0},{24,8},{1,17},{9,25},{17,1},{25,9},{2,18},{10... | collective-permute-start | bytes 1572872 | tf_op jit(solution)/shard_map/ppermute | solution.py:542
  111.3 26.1 %collective-permute-start.26 = (bf16[2,4,128,512]{3,2,1,0:T(8,128)(2,1)S(1)}, bf16[2,4,128,512]{3,2,1,0:T(8,128)(2,1)S(1)}, u32[]{:S(2)}, u32[]{:S(2)}) collective-permute-start(bf16[2,4,128,512]{3,2,1,0:T(8,128)(2,1)S(1)} %get-tuple-element.66), channel_id=1, source_target_pairs={{0,1},{1,0},{2,3},{3,2},{4,5},{5,4},{6,7},{7,6},{8,9},{9,8},{10,11... | collective-permute-start | bytes 3145736 | tf_op jit(solution)/shard_map/ppermute | solution.py:564
  124.4 33.6 %collective-permute-start.28 = (bf16[2,4,64,1024]{3,2,1,0:T(8,128)(2,1)}, bf16[2,4,64,1024]{3,2,1,0:T(8,128)(2,1)S(1)}, u32[]{:S(2)}, u32[]{:S(2)}) collective-permute-start(bf16[2,4,64,1024]{3,2,1,0:T(8,128)(2,1)} %get-tuple-element.70), channel_id=1, source_target_pairs={{0,1},{1,0},{2,3},{3,2},{4,5},{5,4},{6,7},{7,6},{8,9},{9,8},{10,11... | collective-permute-start | bytes 3145736 | tf_op jit(solution)/shard_map/ppermute | solution.py:568
  125.3 36.0 %collective-permute-start.17 = (bf16[2,512,512]{2,1,0:T(8,128)(2,1)}, bf16[2,512,512]{2,1,0:T(8,128)(2,1)}, u32[]{:S(2)}, u32[]{:S(2)}) collective-permute-start(bf16[2,512,512]{2,1,0:T(8,128)(2,1)} %get-tuple-element.54), channel_id=1, source_target_pairs={{0,8},{8,0},{16,24},{24,16},{1,9},{9,1},{17,25},{25,17},{2,10},{10... | collective-permute-start | bytes 3145736 | tf_op jit(solution)/shard_map/ppermute | solution.py:567
  139.1 22.2 %collective-permute-start.27 = (bf16[4,64,512]{2,1,0:T(8,128)(2,1)S(1)}, bf16[4,64,512]{2,1,0:T(8,128)(2,1)S(1)}, u32[]{:S(2)}, u32[]{:S(2)}) collective-permute-start(bf16[4,64,512]{2,1,0:T(8,128)(2,1)S(1)} %get-tuple-element.68), channel_id=1, source_target_pairs={{0,16},{8,24},{16,0},{24,8},{1,17},{9,25},{17,1},{25,9},{2,18},{10... | collective-permute-start | bytes 786440 | tf_op jit(solution)/shard_map/ppermute | solution.py:579
  165.2 15.5 %collective-permute-start.22 = (bf16[2,128,512]{2,1,0:T(8,128)(2,1)S(1)}, bf16[2,128,512]{2,1,0:T(8,128)(2,1)S(1)}, u32[]{:S(2)}, u32[]{:S(2)}) collective-permute-start(bf16[2,128,512]{2,1,0:T(8,128)(2,1)S(1)} %get-tuple-element.59), channel_id=1, source_target_pairs={{2,0},{3,1},{0,2},{1,3},{10,4},{11,5},{8,6},{9,7},{6,8},{7,9},{4,1... | collective-permute-start | bytes 786440 | tf_op jit(solution)/shard_map/ppermute | solution.py:530
  167.1 15.9 %collective-permute-start.23 = (bf16[2,128,512]{2,1,0:T(8,128)(2,1)S(1)}, bf16[2,128,512]{2,1,0:T(8,128)(2,1)S(1)}, u32[]{:S(2)}, u32[]{:S(2)}) collective-permute-start(bf16[2,128,512]{2,1,0:T(8,128)(2,1)S(1)} %get-tuple-element.60), channel_id=1, source_target_pairs={{10,0},{11,1},{8,2},{9,3},{2,4},{3,5},{0,6},{1,7},{14,8},{15,9},{1... | collective-permute-start | bytes 786440 | tf_op jit(solution)/shard_map/ppermute | solution.py:530
  168.2 20.3 %collective-permute-start.24 = (bf16[2,128,512]{2,1,0:T(8,128)(2,1)S(1)}, bf16[2,128,512]{2,1,0:T(8,128)(2,1)S(1)}, u32[]{:S(2)}, u32[]{:S(2)}) collective-permute-start(bf16[2,128,512]{2,1,0:T(8,128)(2,1)S(1)} %get-tuple-element.61), channel_id=1, source_target_pairs={{3,0},{2,1},{1,2},{0,3},{11,4},{10,5},{9,6},{8,7},{7,8},{6,9},{5,1... | collective-permute-start | bytes 786440 | tf_op jit(solution)/shard_map/ppermute | solution.py:530
  169.0 31.5 %collective-permute-start.30 = (bf16[2,2,64,512]{3,2,1,0:T(8,128)(2,1)S(1)}, bf16[2,2,64,512]{3,2,1,0:T(8,128)(2,1)}, u32[]{:S(2)}, u32[]{:S(2)}) collective-permute-start(bf16[2,2,64,512]{3,2,1,0:T(8,128)(2,1)S(1)} %fusion.3), channel_id=1, source_target_pairs={{0,2},{1,3},{2,0},{3,1},{4,6},{5,7},{6,4},{7,5},{8,10},{9,11},{10,... | collective-permute-start | bytes 786440 | tf_op jit(solution)/shard_map/ppermute | solution.py:586
  171.3 31.0 %collective-permute-start.25 = (bf16[2,128,512]{2,1,0:T(8,128)(2,1)S(1)}, bf16[2,128,512]{2,1,0:T(8,128)(2,1)S(1)}, u32[]{:S(2)}, u32[]{:S(2)}) collective-permute-start(bf16[2,128,512]{2,1,0:T(8,128)(2,1)S(1)} %get-tuple-element.62), channel_id=1, source_target_pairs={{11,0},{10,1},{9,2},{8,3},{3,4},{2,5},{1,6},{0,7},{15,8},{14,9},{1... | collective-permute-start | bytes 786440 | tf_op jit(solution)/shard_map/ppermute | solution.py:530
  180.7 24.5 %collective-permute-start.18 = (bf16[2,128,512]{2,1,0:T(8,128)(2,1)S(1)}, bf16[2,128,512]{2,1,0:T(8,128)(2,1)S(1)}, u32[]{:S(2)}, u32[]{:S(2)}) collective-permute-start(bf16[2,128,512]{2,1,0:T(8,128)(2,1)S(1)} %get-tuple-element.55), channel_id=1, source_target_pairs={{0,0},{1,1},{2,2},{3,3},{8,4},{9,5},{10,6},{11,7},{4,8},{5,9},{6,1... | collective-permute-start | bytes 786440 | tf_op jit(solution)/shard_map/ppermute | solution.py:530
  182.9 22.4 %collective-permute-start.19 = (bf16[2,128,512]{2,1,0:T(8,128)(2,1)S(1)}, bf16[2,128,512]{2,1,0:T(8,128)(2,1)S(1)}, u32[]{:S(2)}, u32[]{:S(2)}) collective-permute-start(bf16[2,128,512]{2,1,0:T(8,128)(2,1)S(1)} %get-tuple-element.56), channel_id=1, source_target_pairs={{8,0},{9,1},{10,2},{11,3},{0,4},{1,5},{2,6},{3,7},{12,8},{13,9},{1... | collective-permute-start | bytes 786440 | tf_op jit(solution)/shard_map/ppermute | solution.py:530
  188.4 16.8 %collective-permute-start.20 = (bf16[2,128,512]{2,1,0:T(8,128)(2,1)S(1)}, bf16[2,128,512]{2,1,0:T(8,128)(2,1)S(1)}, u32[]{:S(2)}, u32[]{:S(2)}) collective-permute-start(bf16[2,128,512]{2,1,0:T(8,128)(2,1)S(1)} %get-tuple-element.57), channel_id=1, source_target_pairs={{1,0},{0,1},{3,2},{2,3},{9,4},{8,5},{11,6},{10,7},{5,8},{4,9},{7,1... | collective-permute-start | bytes 786440 | tf_op jit(solution)/shard_map/ppermute | solution.py:530
  202.4 17.0 %collective-permute-start.31 = (bf16[2,64,512]{2,1,0:T(8,128)(2,1)}, bf16[2,64,512]{2,1,0:T(8,128)(2,1)S(1)}, u32[]{:S(2)}, u32[]{:S(2)}) collective-permute-start(bf16[2,64,512]{2,1,0:T(8,128)(2,1)} %fusion.7), channel_id=1, source_target_pairs={{0,4},{1,5},{2,6},{3,7},{4,0},{5,1},{6,2},{7,3},{8,12},{9,13},{10,... | collective-permute-start | bytes 393224 | tf_op jit(solution)/shard_map/ppermute | solution.py:588
  (36 other events, 377.4 us)

commit v4 on v3

--- a/solution.py
+++ b/solution.py
@@ -335,7 +335,6 @@
     n = matrix.shape[-1]
     slices = n // rows
     quarter = rows // 2
-    tile = 2 * rows
 
     def body(ids, own_ref, rec_ref, mat, m00, m01, m10, m11, field):
         for at, ref in enumerate((own_ref, rec_ref)):
@@ -344,18 +343,22 @@
                 for s in range(slices):
                     to = pl.ds(pl.multiple_of(s * rows + side, quarter), quarter)
                     field[part, to] = ref[part, pl.ds(s * quarter, quarter)]
-        first = ids[3] == 0
-        for b, (near, far) in enumerate(((m00, m10), (m01, m11))):
-            at = (ids[0] ^ b) * 2 + (ids[4] ^ turn)
-            left = mat[:, pl.ds(pl.multiple_of(at * tile, tile), tile)].reshape(2 * tile, n)
-            q_re = dot_rows(left, field[0])
-            q_im = dot_rows(left, field[1])
-            new_re = (q_re[:tile] - q_im[tile:]).astype(BF)
-            new_im = q_im[:tile] + q_re[tile:]
-            new_im = jnp.where(first, new_im, -new_im).astype(BF)
-            for part, new in enumerate((new_re, new_im)):
-                near[part] = jnp.where(first, new[:rows], new[rows:])
-                far[part] = jnp.where(first, new[rows:], new[:rows])
+        outs = (m00, m01, m10, m11)
+        left = []
+        for part in range(2):
+            for at in range(4):
+                s = (ids[0] ^ (at % 2)) * 4 + (ids[4] ^ (at // 2)) * 2 + (ids[3] ^ turn)
+                left.append(mat[part, pl.ds(pl.multiple_of(s * rows, rows), rows)])
+        left = jnp.concatenate(left)
+        q_re = dot_rows(left, field[0])
+        q_im = dot_rows(left, field[1])
+        n_rows = 4 * rows
+        new_re = (q_re[:n_rows] - q_im[n_rows:]).astype(BF)
+        new_im = q_im[:n_rows] + q_re[n_rows:]
+        new_im = jnp.where(ids[3] == 0, new_im, -new_im).astype(BF)
+        for at, out in enumerate(outs):
+            out[0] = new_re[at * rows : (at + 1) * rows]
+            out[1] = new_im[at * rows : (at + 1) * rows]
 
     return solid(
         body,
@@ -568,26 +571,30 @@
     partner1 = lax.ppermute(send1, "space", flip(space, 1))
     own = row_rest(ids, phased, line_matrix)
 
-    solved = last_solve(ids, 0, own, came, line_matrix, rows)
-    finals = send(solved, 0, coming)
-    solved = last_solve(ids, 1, own, came, line_matrix, rows)
-    finals += send(solved, 1, coming)
-
-    sums = []
+    finals = [None] * 8
+    for turn in range(2):
+        solved = last_solve(ids, turn, own, came, line_matrix, rows)
+        for at, m in enumerate(solved):
+            place = (at // 2) * 4 + turn * 2 + at % 2
+            finals[place] = lax.ppermute(m, both, coming[place])
+
+    def half_of(v, at, axis):
+        return lax.dynamic_index_in_dim(v, at, axis, keepdims=False)
+
+    low, high = z % 2, z // 2
+    pieces = []
     for depth, keep, partner in ((0, keep0, partner0), (1, keep1, partner1)):
         stay, away = image_terms(ids, keep, partner, weight, depth == 1)
-        sums.append(stay + lax.ppermute(away, "freq", flip(groups, 2)).astype(F32))
-
-    def half_of(v, at, axis):
-        return lax.dynamic_index_in_dim(v, at, axis, keepdims=False)
-
-    low, high = z % 2, z // 2
-    paired = jnp.stack(sums, axis=1).reshape(2, 2, 2, quarter, half)
-    near = lax.ppermute(half_of(paired, 1 - low, 1).astype(BF), "space", flip(space, 2))
-    pair = half_of(paired, low, 1) + near.astype(F32)
-    far = lax.ppermute(half_of(pair, 1 - high, 0).astype(BF), "space", flip(space, 4))
-    piece = (half_of(pair, high, 0) + far.astype(F32)).astype(BF)
-    pair = jnp.stack([piece, lax.ppermute(piece, "freq", flip(groups, 2))])
+        over_x = stay + lax.ppermute(away, "freq", flip(groups, 2)).astype(F32)
+        paired = over_x.reshape(2, 2, quarter, half)
+        near = half_of(paired, 1 - low, 1).astype(BF)
+        near = lax.ppermute(near, "space", flip(space, 2))
+        pair = half_of(paired, low, 1) + near.astype(F32)
+        far = half_of(pair, 1 - high, 0).astype(BF)
+        far = lax.ppermute(far, "space", flip(space, 4))
+        piece = (half_of(pair, high, 0) + far.astype(F32)).astype(BF)
+        pieces.append(jnp.stack([piece, lax.ppermute(piece, "freq", flip(groups, 2))]))
+    pair = jnp.stack(pieces, axis=1)
     quad = jnp.stack([pair, lax.ppermute(pair, "freq", swap)], axis=1)
 
     stay, away = last_term(ids, finals, image_weights)

time: 233 us -> 231 us (level)
  other arithmetic: 5.11 us -> 7.78 us
  waiting for transfers between devices: 93.9 us -> 91.5 us
    ppermute x5 -> x16, waiting for transfers between devices: 15.6 us -> 34.9 us  [the longest x8 25.2 us: plane_per_chip(): finals[place] = lax.ppermute(m, both, coming[place])]
    ppermute x5 -> x16, starting transfers between devices: 8.6 us -> 25.9 us  [the longest x8 11.8 us: plane_per_chip(): finals[place] = lax.ppermute(m, both, coming[place])]
    ppermute x1, waiting for transfers between devices: 12.1 us -> 0.01 us  [plane_per_chip(): partner0 = lax.ppermute(send0, 'space', flip(space, 1))]
    ppermute x1, starting transfers between devices: 10.7 us -> 0.07 us  [plane_per_chip(): chip = (stay + lax.ppermute(away, 'freq', swap).astype(F32)).astype(BF)]
    ppermute x16 -> x8, starting transfers between devices: 19.1 us -> 11.1 us  [send(): lax.ppermute(m, both, rounds[4 * turn + at])]
    ppermute x16 -> x8, waiting for transfers between devices: 26.9 us -> 19.4 us  [send(): lax.ppermute(m, both, rounds[4 * turn + at])]
    ppermute x1, waiting for transfers between devices: 10.8 us -> 7.62 us  [plane_per_chip(): partner1 = lax.ppermute(send1, 'space', flip(space, 1))]
    unnamed x46 -> x34, local copies, waits for them, and re-layouts: 8.07 us -> 8.09 us
  transfers between devices with their start and end apart: 37 -> 40, of which waited for: 17 -> 18; matrix products, arithmetic and copies ran while one was open for 4% -> 5% of each run, Pallas kernels for 23% -> 22%
where the time goes in v4:
time: 231 us; the launch traced here: 230 us
  waiting for transfers between devices  91.5 us (40%)
  Pallas kernels  61.1 us (26%)
  starting transfers between devices  51.8 us (22%)
  local copies, waits for them, and re-layouts  16.9 us (7%)
  other arithmetic  7.78 us (3%)
    pallas_call x9, Pallas kernels, call(): pl.pallas_call(body, out_shape=[jax.ShapeDtypeStruct(s, d) for s, d, _, _...  31.5 us
    pallas_call x6, Pallas kernels, solid(): pl.pallas_call(body, out_shape=[jax.ShapeDtypeStruct(s, d) for s, d in ou...  29.6 us
    ppermute x8, waiting for transfers between devices, plane_per_chip(): finals[place] = lax.ppermute(m, both, coming[place])  25.2 us
    ppermute x8, waiting for transfers between devices, send(): lax.ppermute(m, both, rounds[4 * turn + at])  19.4 us
    ppermute x2, waiting for transfers between devices, plane_per_chip(): lax.ppermute(planes[d], 'freq', flip(groups, 2))  16.6 us
    ppermute x8, starting transfers between devices, plane_per_chip(): finals[place] = lax.ppermute(m, both, coming[place])  11.8 us
    ppermute x8, starting transfers between devices, send(): lax.ppermute(m, both, rounds[4 * turn + at])  11.1 us
    ppermute x3, waiting for transfers between devices, plane_per_chip(): lax.ppermute(piece, 'space', flip(space, 2 * k))  10.3 us
  transfers between devices with their start and end apart: 40, of which 18 were waited for; matrix products, arithmetic and copies ran while one was open for 5% of the time, Pallas kernels for 22%

profile of v4, /device:TPU:0, one launch (start us, length us, event | category | flops | bytes accessed | tf_op | source)
XLA Modules:
  0.0 230.3 jit_solution(7452884697162370886)
XLA Ops:
  0.7 4.7 %dynamic-slice_bitcast_fusion = bf16[2,1024,1024]{2,1,0:T(8,128)(2,1)} fusion(bf16[2,2,1024,1024]{3,2,1,0:T(8,128)(2,1)} %mat.3, s32[]{:T(128)S(6)} %select_n.88), kind=kLoop, calls=%fused_computation | loop fusion | bytes 8388612 | tf_op jit(solution)/shard_map/squeeze | solution.py:559
  12.1 3.7 %collective-permute-done.9 = f16[2,64,512]{2,1,0:T(8,128)(2,1)S(1)} collective-permute-done((f16[2,64,512]{2,1,0:T(8,128)(2,1)S(1)}, f16[2,64,512]{2,1,0:T(8,128)(2,1)S(1)}, u32[]{:S(2)}, u32[]{:S(2)}) %collective-permute-start.9) | collective-permute-done | bytes 131104 | tf_op jit(solution)/shard_map/ppermute | solution.py:540
  15.8 6.6 %collective-permute-done.10 = f16[2,64,512]{2,1,0:T(8,128)(2,1)S(1)} collective-permute-done((f16[2,64,512]{2,1,0:T(8,128)(2,1)S(1)}, f16[2,64,512]{2,1,0:T(8,128)(2,1)S(1)}, u32[]{:S(2)}, u32[]{:S(2)}) %collective-permute-start.10) | collective-permute-done | bytes 131104 | tf_op jit(solution)/shard_map/ppermute | solution.py:540
  25.0 7.4 %shard_map.85 = (bf16[2,128,512]{2,1,0:T(8,128)(2,1)}, bf16[2,128,512]{2,1,0:T(8,128)(2,1)}, bf16[2,128,512]{2,1,0:T(8,128)(2,1)}, bf16[2,128,512]{2,1,0:T(8,128)(2,1)}) custom-call(s32[6]{0:T(128)} %stack.85.ids, bf16[2,2,128,1024]{3,2,1,0:T(8,128)(2,1)} %src.3, bf16[2,2,128,1024]{3,2,1,0:T(8,128)(2,1)} %rec.3, bf16[2,2,1024,1024]{3,2,1,0:T(8,128)(2,1)} %mat.3, ...), custom_call_target="tpu_custom_call" | custom-call | flops 2147483648 | bytes 8388608 | tf_op jit(solution)/shard_map/pallas_call | solution.py:53
  34.0 4.1 %collective-permute-start.1 = (bf16[2,128,512]{2,1,0:T(8,128)(2,1)}, bf16[2,128,512]{2,1,0:T(8,128)(2,1)S(1)}, u32[]{:S(2)}, u32[]{:S(2)}) collective-permute-start(bf16[2,128,512]{2,1,0:T(8,128)(2,1)} %get-tuple-element.40), channel_id=1, source_target_pairs={{0,8},{1,9},{2,10},{3,11},{4,0},{5,1},{6,2},{7,3},{8,12},{9,13},{1... | collective-permute-start | bytes 786440 | tf_op jit(solution)/shard_map/ppermute | solution.py:533
  40.7 7.5 %shard_map.86 = (bf16[2,128,512]{2,1,0:T(8,128)(2,1)}, bf16[2,128,512]{2,1,0:T(8,128)(2,1)}, bf16[2,128,512]{2,1,0:T(8,128)(2,1)}, bf16[2,128,512]{2,1,0:T(8,128)(2,1)}) custom-call(s32[6]{0:T(128)} %stack.85.ids, bf16[2,2,128,1024]{3,2,1,0:T(8,128)(2,1)} %src.3, bf16[2,2,128,1024]{3,2,1,0:T(8,128)(2,1)} %rec.3, bf16[2,2,1024,1024]{3,2,1,0:T(8,128)(2,1)} %mat.3, ...), custom_call_target="tpu_custom_call" | custom-call | flops 2147483648 | bytes 8388608 | tf_op jit(solution)/shard_map/pallas_call | solution.py:53
  49.3 3.7 %collective-permute-done.13 = f16[8,64,512]{2,1,0:T(8,128)(2,1)S(1)} collective-permute-done((f16[8,64,512]{2,1,0:T(8,128)(2,1)S(1)}, f16[8,64,512]{2,1,0:T(8,128)(2,1)S(1)}, u32[]{:S(2)}, u32[]{:S(2)}) %collective-permute-start.13) | collective-permute-done | bytes 524320 | tf_op jit(solution)/shard_map/ppermute | solution.py:545
  53.5 3.8 %shard_map.87 = (f32[1024,512]{1,0:T(8,128)S(1)}, f32[1024,512]{1,0:T(8,128)S(1)}) custom-call(s32[6]{0:T(128)S(1)} %copy-done.3, f32[16,64,512]{2,1,0:T(8,128)S(1)} %maximum_convert_fusion.pieces, f32[1]{0:T(128)} %bitcast.19.om), custom_call_target="tpu_custom_call" | custom-call | flops 67108864 | bytes 8388608 | tf_op jit(solution)/shard_map/pallas_call | solution.py:53
  57.4 3.1 %collective-permute-start.5 = (bf16[2,128,512]{2,1,0:T(8,128)(2,1)S(1)}, bf16[2,128,512]{2,1,0:T(8,128)(2,1)S(1)}, u32[]{:S(2)}, u32[]{:S(2)}) collective-permute-start(bf16[2,128,512]{2,1,0:T(8,128)(2,1)S(1)} %copy-done.15), channel_id=1, source_target_pairs={{0,10},{1,11},{2,8},{3,9},{4,2},{5,3},{6,0},{7,1},{8,14},{9,15},{1... | collective-permute-start | bytes 786440 | tf_op jit(solution)/shard_map/ppermute | solution.py:533
  65.1 4.2 %collective-permute-done.4.refs_4_ = bf16[2,128,512]{2,1,0:T(8,128)(2,1)S(1)} collective-permute-done((bf16[2,128,512]{2,1,0:T(8,128)(2,1)S(1)}, bf16[2,128,512]{2,1,0:T(8,128)(2,1)S(1)}, u32[]{:S(2)}, u32[]{:S(2)}) %collective-permute-start.4) | collective-permute-done | bytes 262176 | tf_op jit(solution)/shard_map/ppermute | solution.py:533
  69.4 3.3 %collective-permute-done.5.refs_5_ = bf16[2,128,512]{2,1,0:T(8,128)(2,1)S(1)} collective-permute-done((bf16[2,128,512]{2,1,0:T(8,128)(2,1)S(1)}, bf16[2,128,512]{2,1,0:T(8,128)(2,1)S(1)}, u32[]{:S(2)}, u32[]{:S(2)}) %collective-permute-start.5) | collective-permute-done | bytes 262176 | tf_op jit(solution)/shard_map/ppermute | solution.py:533
  72.7 9.1 %collective-permute-done.6.refs_6_ = bf16[2,128,512]{2,1,0:T(8,128)(2,1)S(1)} collective-permute-done((bf16[2,128,512]{2,1,0:T(8,128)(2,1)S(1)}, bf16[2,128,512]{2,1,0:T(8,128)(2,1)S(1)}, u32[]{:S(2)}, u32[]{:S(2)}) %collective-permute-start.6) | collective-permute-done | bytes 262176 | tf_op jit(solution)/shard_map/ppermute | solution.py:533
  84.0 8.2 %shard_map.88 = (bf16[2,4,128,512]{3,2,1,0:T(8,128)(2,1)S(1)}, bf16[2,4,128,512]{3,2,1,0:T(8,128)(2,1)}, bf16[2,1024,512]{2,1,0:T(8,128)(2,1)S(1)}, bf16[2,512,512]{2,1,0:T(8,128)(2,1)S(1)}) custom-call(s32[6]{0:T(128)S(1)} %copy-done.3, bf16[2,128,512]{2,1,0:T(8,128)(2,1)S(1)} %collective-permute-done.refs_0_, ...), custom_call_target="tpu_custom_call" | custom-call | flops 6442450944 | bytes 8388608 | tf_op jit(solution)/shard_map/pallas_call | solution.py:72
  97.8 12.9 %collective-permute-done.16 = f16[8,64,512]{2,1,0:T(8,128)(2,1)} collective-permute-done((f16[8,64,512]{2,1,0:T(8,128)(2,1)}, f16[8,64,512]{2,1,0:T(8,128)(2,1)}, u32[]{:S(2)}, u32[]{:S(2)}) %collective-permute-start.16) | collective-permute-done | bytes 524320 | tf_op jit(solution)/shard_map/ppermute | solution.py:545
  112.1 4.0 %shard_map.90 = (f32[512,1024]{1,0:T(8,128)S(1)}, f32[512,1024]{1,0:T(8,128)S(1)}) custom-call(s32[6]{0:T(128)S(1)} %copy-done.3, f32[16,64,512]{2,1,0:T(8,128)S(1)} %maximum_convert_fusion.1.pieces, f32[1]{0:T(128)} %bitcast.19.om), custom_call_target="tpu_custom_call" | custom-call | flops 67108864 | bytes 8388608 | tf_op jit(solution)/shard_map/pallas_call | solution.py:53
  123.6 9.6 %shard_map.91 = (bf16[2,4,64,1024]{3,2,1,0:T(8,128)(2,1)S(1)}, bf16[2,4,64,1024]{3,2,1,0:T(8,128)(2,1)}, bf16[2,512,1024]{2,1,0:T(8,128)(2,1)S(1)}, bf16[2,512,512]{2,1,0:T(8,128)(2,1)}) custom-call(s32[6]{0:T(128)S(1)} %copy-done.3, bf16[2,512,512]{2,1,0:T(8,128)(2,1)S(1)} %shard_map.89.own_ref, bf16[2,512,512]{2,1,0:T(8,128)(2,1)} %collective-permute-done.15.rec_ref, ...), custom_call_target="tpu_custom_call" | custom-call | flops 6442450944 | bytes 8388608 | tf_op jit(solution)/shard_map/pallas_call | solution.py:72
  139.3 4.1 %collective-permute-done.28 = bf16[2,64,512]{2,1,0:T(8,128)(2,1)S(1)} collective-permute-done((bf16[2,64,512]{2,1,0:T(8,128)(2,1)S(1)}, bf16[2,64,512]{2,1,0:T(8,128)(2,1)S(1)}, u32[]{:S(2)}, u32[]{:S(2)}) %collective-permute-start.28) | collective-permute-done | bytes 131104 | tf_op jit(solution)/shard_map/ppermute | solution.py:591
  152.7 7.6 %collective-permute-done.31.o = bf16[2,4,64,1024]{3,2,1,0:T(8,128)(2,1)S(1)} collective-permute-done((bf16[2,4,64,1024]{3,2,1,0:T(8,128)(2,1)}, bf16[2,4,64,1024]{3,2,1,0:T(8,128)(2,1)S(1)}, u32[]{:S(2)}, u32[]{:S(2)}) %collective-permute-start.31) | collective-permute-done | bytes 1048608 | tf_op jit(solution)/shard_map/ppermute | solution.py:571
  164.2 3.0 %shard_map.94 = (bf16[2,128,512]{2,1,0:T(8,128)(2,1)S(1)}, bf16[2,128,512]{2,1,0:T(8,128)(2,1)S(1)}, bf16[2,128,512]{2,1,0:T(8,128)(2,1)S(1)}, bf16[2,128,512]{2,1,0:T(8,128)(2,1)S(1)}) custom-call(s32[6]{0:T(128)S(1)} %copy-done.3, bf16[2,512,512]{2,1,0:T(8,128)(2,1)S(1)} %shard_map.92.own_ref, bf16[2,512,512]{2,1,0:T(8,128)(2,1)S(1)} %collective-permute-done.17.rec_ref, ...), custom_call_target="tpu_custom_call" | custom-call | flops 2147483648 | bytes 8388608 | tf_op jit(solution)/shard_map/pallas_call | solution.py:72
  178.2 14.1 %collective-permute-done.20.refs_2_ = bf16[2,128,512]{2,1,0:T(8,128)(2,1)S(1)} collective-permute-done((bf16[2,128,512]{2,1,0:T(8,128)(2,1)S(1)}, bf16[2,128,512]{2,1,0:T(8,128)(2,1)S(1)}, u32[]{:S(2)}, u32[]{:S(2)}) %collective-permute-start.20) | collective-permute-done | bytes 262176 | tf_op jit(solution)/shard_map/ppermute | solution.py:579
  193.4 3.9 %collective-permute-start.23 = (bf16[2,128,512]{2,1,0:T(8,128)(2,1)S(1)}, bf16[2,128,512]{2,1,0:T(8,128)(2,1)S(1)}, u32[]{:S(2)}, u32[]{:S(2)}) collective-permute-start(bf16[2,128,512]{2,1,0:T(8,128)(2,1)S(1)} %get-tuple-element.60), channel_id=1, source_target_pairs={{10,0},{11,1},{8,2},{9,3},{2,4},{3,5},{0,6},{1,7},{14,8},{15,9},{1... | collective-permute-start | bytes 786440 | tf_op jit(solution)/shard_map/ppermute | solution.py:579
  197.3 5.7 %collective-permute-start.34 = (bf16[64,512]{1,0:T(8,128)(2,1)S(1)}, bf16[64,512]{1,0:T(8,128)(2,1)S(1)}, u32[]{:S(2)}, u32[]{:S(2)}) collective-permute-start(bf16[64,512]{1,0:T(8,128)(2,1)S(1)} %fusion.7), channel_id=1, source_target_pairs={{0,4},{1,5},{2,6},{3,7},{4,0},{5,1},{6,2},{7,3},{8,12},{9,13},{10,... | collective-permute-start | bytes 196616 | tf_op jit(solution)/shard_map/ppermute | solution.py:594
  203.1 6.2 %collective-permute-done.22.refs_4_ = bf16[2,128,512]{2,1,0:T(8,128)(2,1)S(1)} collective-permute-done((bf16[2,128,512]{2,1,0:T(8,128)(2,1)S(1)}, bf16[2,128,512]{2,1,0:T(8,128)(2,1)S(1)}, u32[]{:S(2)}, u32[]{:S(2)}) %collective-permute-start.22) | collective-permute-done | bytes 262176 | tf_op jit(solution)/shard_map/ppermute | solution.py:579
  209.3 4.5 %collective-permute-done.23.refs_5_ = bf16[2,128,512]{2,1,0:T(8,128)(2,1)S(1)} collective-permute-done((bf16[2,128,512]{2,1,0:T(8,128)(2,1)S(1)}, bf16[2,128,512]{2,1,0:T(8,128)(2,1)S(1)}, u32[]{:S(2)}, u32[]{:S(2)}) %collective-permute-start.23) | collective-permute-done | bytes 262176 | tf_op jit(solution)/shard_map/ppermute | solution.py:579
  (138 shorter events, 84.0 us)
Async XLA Ops:
  5.3 56.4 %collective-permute-start.8 = (bf16[2,1024,1024]{2,1,0:T(8,128)(2,1)}, bf16[2,1024,1024]{2,1,0:T(8,128)(2,1)}, u32[]{:S(2)}, u32[]{:S(2)}) collective-permute-start(bf16[2,1024,1024]{2,1,0:T(8,128)(2,1)} %dynamic-slice_bitcast_fusion), channel_id=1, source_target_pairs={{0,8},{8,0},{16,24},{24,16},{1,9},{9,1},{17,25},{25,17},{2,10},{10... | collective-permute-start | bytes 12582920 | tf_op jit(solution)/shard_map/ppermute | solution.py:560
  22.6 15.6 %collective-permute-start.12 = (f16[2,4,64,512]{3,2,1,0:T(8,128)(2,1)S(1)}, f16[2,4,64,512]{3,2,1,0:T(8,128)(2,1)S(1)}, u32[]{:S(2)}, u32[]{:S(2)}) collective-permute-start(f16[2,4,64,512]{3,2,1,0:T(8,128)(2,1)S(1)} %pad_maximum_fusion), channel_id=1, source_target_pairs={{0,1},{1,0},{2,3},{3,2},{4,5},{5,4},{6,7},{7,6},{8,9},{9,8},{10,11... | collective-permute-start | bytes 1572872 | tf_op jit(solution)/shard_map/ppermute | solution.py:542
  24.2 23.9 %collective-permute-start.14 = (f32[2,2]{1,0:T(2,128)S(1)}, f32[2,2]{1,0:T(2,128)S(1)}, u32[]{:S(2)}, u32[]{:S(2)}) collective-permute-start(f32[2,2]{1,0:T(2,128)S(1)} %pad_maximum_fusion.5), channel_id=1, source_target_pairs={{0,8},{8,0},{16,24},{24,16},{1,9},{9,1},{17,25},{25,17},{2,10},{10... | collective-permute-start | bytes 56 | tf_op jit(solution)/shard_map/ppermute | solution.py:556
  32.4 24.9 %collective-permute-start = (bf16[2,128,512]{2,1,0:T(8,128)(2,1)}, bf16[2,128,512]{2,1,0:T(8,128)(2,1)S(1)}, u32[]{:S(2)}, u32[]{:S(2)}) collective-permute-start(bf16[2,128,512]{2,1,0:T(8,128)(2,1)} %get-tuple-element.39), channel_id=1, source_target_pairs={{0,0},{1,1},{2,2},{3,3},{4,8},{5,9},{6,10},{7,11},{8,4},{9,5},{10,... | collective-permute-start | bytes 786440 | tf_op jit(solution)/shard_map/ppermute | solution.py:533
  34.0 23.4 %collective-permute-start.1 = (bf16[2,128,512]{2,1,0:T(8,128)(2,1)}, bf16[2,128,512]{2,1,0:T(8,128)(2,1)S(1)}, u32[]{:S(2)}, u32[]{:S(2)}) collective-permute-start(bf16[2,128,512]{2,1,0:T(8,128)(2,1)} %get-tuple-element.40), channel_id=1, source_target_pairs={{0,8},{1,9},{2,10},{3,11},{4,0},{5,1},{6,2},{7,3},{8,12},{9,13},{1... | collective-permute-start | bytes 786440 | tf_op jit(solution)/shard_map/ppermute | solution.py:533
  39.1 13.9 %collective-permute-start.13 = (f16[8,64,512]{2,1,0:T(8,128)(2,1)S(1)}, f16[8,64,512]{2,1,0:T(8,128)(2,1)S(1)}, u32[]{:S(2)}, u32[]{:S(2)}) collective-permute-start(f16[8,64,512]{2,1,0:T(8,128)(2,1)S(1)} %pad_maximum_fusion.1), channel_id=1, source_target_pairs={{0,16},{8,24},{16,0},{24,8},{1,17},{9,25},{17,1},{25,9},{2,18},{10... | collective-permute-start | bytes 1572872 | tf_op jit(solution)/shard_map/ppermute | solution.py:545
  57.4 15.3 %collective-permute-start.5 = (bf16[2,128,512]{2,1,0:T(8,128)(2,1)S(1)}, bf16[2,128,512]{2,1,0:T(8,128)(2,1)S(1)}, u32[]{:S(2)}, u32[]{:S(2)}) collective-permute-start(bf16[2,128,512]{2,1,0:T(8,128)(2,1)S(1)} %copy-done.15), channel_id=1, source_target_pairs={{0,10},{1,11},{2,8},{3,9},{4,2},{5,3},{6,0},{7,1},{8,14},{9,15},{1... | collective-permute-start | bytes 786440 | tf_op jit(solution)/shard_map/ppermute | solution.py:533
  60.5 21.3 %collective-permute-start.6 = (bf16[2,128,512]{2,1,0:T(8,128)(2,1)S(1)}, bf16[2,128,512]{2,1,0:T(8,128)(2,1)S(1)}, u32[]{:S(2)}, u32[]{:S(2)}) collective-permute-start(bf16[2,128,512]{2,1,0:T(8,128)(2,1)S(1)} %copy-done.14), channel_id=1, source_target_pairs={{0,3},{1,2},{2,1},{3,0},{4,11},{5,10},{6,9},{7,8},{8,7},{9,6},{10,... | collective-permute-start | bytes 786440 | tf_op jit(solution)/shard_map/ppermute | solution.py:533
  61.8 22.2 %collective-permute-start.7 = (bf16[2,128,512]{2,1,0:T(8,128)(2,1)S(1)}, bf16[2,128,512]{2,1,0:T(8,128)(2,1)S(1)}, u32[]{:S(2)}, u32[]{:S(2)}) collective-permute-start(bf16[2,128,512]{2,1,0:T(8,128)(2,1)S(1)} %copy-done.13), channel_id=1, source_target_pairs={{0,11},{1,10},{2,9},{3,8},{4,3},{5,2},{6,1},{7,0},{8,15},{9,14},{1... | collective-permute-start | bytes 786440 | tf_op jit(solution)/shard_map/ppermute | solution.py:533
  93.6 27.0 %collective-permute-start.26 = (bf16[2,4,128,512]{3,2,1,0:T(8,128)(2,1)}, bf16[2,4,128,512]{3,2,1,0:T(8,128)(2,1)S(1)}, u32[]{:S(2)}, u32[]{:S(2)}) collective-permute-start(bf16[2,4,128,512]{3,2,1,0:T(8,128)(2,1)} %get-tuple-element.66), channel_id=1, source_target_pairs={{0,1},{1,0},{2,3},{3,2},{4,5},{5,4},{6,7},{7,6},{8,9},{9,8},{10,11... | collective-permute-start | bytes 3145736 | tf_op jit(solution)/shard_map/ppermute | solution.py:567
  94.2 29.4 %collective-permute-start.15 = (bf16[2,512,512]{2,1,0:T(8,128)(2,1)S(1)}, bf16[2,512,512]{2,1,0:T(8,128)(2,1)}, u32[]{:S(2)}, u32[]{:S(2)}) collective-permute-start(bf16[2,512,512]{2,1,0:T(8,128)(2,1)S(1)} %get-tuple-element.50), channel_id=1, source_target_pairs={{0,8},{8,0},{16,24},{24,16},{1,9},{9,1},{17,25},{25,17},{2,10},{10... | collective-permute-start | bytes 3145736 | tf_op jit(solution)/shard_map/ppermute | solution.py:566
  96.6 14.1 %collective-permute-start.16 = (f16[8,64,512]{2,1,0:T(8,128)(2,1)}, f16[8,64,512]{2,1,0:T(8,128)(2,1)}, u32[]{:S(2)}, u32[]{:S(2)}) collective-permute-start(f16[8,64,512]{2,1,0:T(8,128)(2,1)} %pad_maximum_fusion.2), channel_id=1, source_target_pairs={{0,16},{8,24},{16,0},{24,8},{1,17},{9,25},{17,1},{25,9},{2,18},{10... | collective-permute-start | bytes 1572872 | tf_op jit(solution)/shard_map/ppermute | solution.py:545
  122.3 13.5 %collective-permute-start.27 = (bf16[4,64,512]{2,1,0:T(8,128)(2,1)S(1)}, bf16[4,64,512]{2,1,0:T(8,128)(2,1)S(1)}, u32[]{:S(2)}, u32[]{:S(2)}) collective-permute-start(bf16[4,64,512]{2,1,0:T(8,128)(2,1)S(1)} %get-tuple-element.68), channel_id=1, source_target_pairs={{0,16},{8,24},{16,0},{24,8},{1,17},{9,25},{17,1},{25,9},{2,18},{10... | collective-permute-start | bytes 786440 | tf_op jit(solution)/shard_map/ppermute | solution.py:588
  134.6 29.6 %collective-permute-start.17 = (bf16[2,512,512]{2,1,0:T(8,128)(2,1)}, bf16[2,512,512]{2,1,0:T(8,128)(2,1)S(1)}, u32[]{:S(2)}, u32[]{:S(2)}) collective-permute-start(bf16[2,512,512]{2,1,0:T(8,128)(2,1)} %get-tuple-element.54), channel_id=1, source_target_pairs={{0,8},{8,0},{16,24},{24,16},{1,9},{9,1},{17,25},{25,17},{2,10},{10... | collective-permute-start | bytes 3145736 | tf_op jit(solution)/shard_map/ppermute | solution.py:570
  134.6 25.8 %collective-permute-start.31 = (bf16[2,4,64,1024]{3,2,1,0:T(8,128)(2,1)}, bf16[2,4,64,1024]{3,2,1,0:T(8,128)(2,1)S(1)}, u32[]{:S(2)}, u32[]{:S(2)}) collective-permute-start(bf16[2,4,64,1024]{3,2,1,0:T(8,128)(2,1)} %get-tuple-element.70), channel_id=1, source_target_pairs={{0,1},{1,0},{2,3},{3,2},{4,5},{5,4},{6,7},{7,6},{8,9},{9,8},{10,11... | collective-permute-start | bytes 3145736 | tf_op jit(solution)/shard_map/ppermute | solution.py:571
  144.4 18.5 %collective-permute-start.29 = (bf16[64,512]{1,0:T(8,128)(2,1)S(1)}, bf16[64,512]{1,0:T(8,128)(2,1)S(1)}, u32[]{:S(2)}, u32[]{:S(2)}) collective-permute-start(bf16[64,512]{1,0:T(8,128)(2,1)S(1)} %fusion.6), channel_id=1, source_target_pairs={{0,4},{1,5},{2,6},{3,7},{4,0},{5,1},{6,2},{7,3},{8,12},{9,13},{10,... | collective-permute-start | bytes 196616 | tf_op jit(solution)/shard_map/ppermute | solution.py:594
  167.2 25.0 %collective-permute-start.20 = (bf16[2,128,512]{2,1,0:T(8,128)(2,1)S(1)}, bf16[2,128,512]{2,1,0:T(8,128)(2,1)S(1)}, u32[]{:S(2)}, u32[]{:S(2)}) collective-permute-start(bf16[2,128,512]{2,1,0:T(8,128)(2,1)S(1)} %get-tuple-element.57), channel_id=1, source_target_pairs={{1,0},{0,1},{3,2},{2,3},{9,4},{8,5},{11,6},{10,7},{5,8},{4,9},{7,1... | collective-permute-start | bytes 786440 | tf_op jit(solution)/shard_map/ppermute | solution.py:579
  168.5 24.8 %collective-permute-start.21 = (bf16[2,128,512]{2,1,0:T(8,128)(2,1)S(1)}, bf16[2,128,512]{2,1,0:T(8,128)(2,1)S(1)}, u32[]{:S(2)}, u32[]{:S(2)}) collective-permute-start(bf16[2,128,512]{2,1,0:T(8,128)(2,1)S(1)} %get-tuple-element.58), channel_id=1, source_target_pairs={{9,0},{8,1},{11,2},{10,3},{1,4},{0,5},{3,6},{2,7},{13,8},{12,9},{1... | collective-permute-start | bytes 786440 | tf_op jit(solution)/shard_map/ppermute | solution.py:579
  169.8 23.5 %collective-permute-start.24 = (bf16[2,128,512]{2,1,0:T(8,128)(2,1)S(1)}, bf16[2,128,512]{2,1,0:T(8,128)(2,1)S(1)}, u32[]{:S(2)}, u32[]{:S(2)}) collective-permute-start(bf16[2,128,512]{2,1,0:T(8,128)(2,1)S(1)} %get-tuple-element.61), channel_id=1, source_target_pairs={{3,0},{2,1},{1,2},{0,3},{11,4},{10,5},{9,6},{8,7},{7,8},{6,9},{5,1... | collective-permute-start | bytes 786440 | tf_op jit(solution)/shard_map/ppermute | solution.py:579
  172.2 21.2 %collective-permute-start.33 = (bf16[2,64,512]{2,1,0:T(8,128)(2,1)S(1)}, bf16[2,64,512]{2,1,0:T(8,128)(2,1)S(1)}, u32[]{:S(2)}, u32[]{:S(2)}) collective-permute-start(bf16[2,64,512]{2,1,0:T(8,128)(2,1)S(1)} %fusion.3), channel_id=1, source_target_pairs={{0,2},{1,3},{2,0},{3,1},{4,6},{5,7},{6,4},{7,5},{8,10},{9,11},{10,... | collective-permute-start | bytes 393224 | tf_op jit(solution)/shard_map/ppermute | solution.py:591
  175.7 21.6 %collective-permute-start.25 = (bf16[2,128,512]{2,1,0:T(8,128)(2,1)S(1)}, bf16[2,128,512]{2,1,0:T(8,128)(2,1)S(1)}, u32[]{:S(2)}, u32[]{:S(2)}) collective-permute-start(bf16[2,128,512]{2,1,0:T(8,128)(2,1)S(1)} %get-tuple-element.62), channel_id=1, source_target_pairs={{11,0},{10,1},{9,2},{8,3},{3,4},{2,5},{1,6},{0,7},{15,8},{14,9},{1... | collective-permute-start | bytes 786440 | tf_op jit(solution)/shard_map/ppermute | solution.py:579
  193.3 15.9 %collective-permute-start.22 = (bf16[2,128,512]{2,1,0:T(8,128)(2,1)S(1)}, bf16[2,128,512]{2,1,0:T(8,128)(2,1)S(1)}, u32[]{:S(2)}, u32[]{:S(2)}) collective-permute-start(bf16[2,128,512]{2,1,0:T(8,128)(2,1)S(1)} %get-tuple-element.59), channel_id=1, source_target_pairs={{2,0},{3,1},{0,2},{1,3},{10,4},{11,5},{8,6},{9,7},{6,8},{7,9},{4,1... | collective-permute-start | bytes 786440 | tf_op jit(solution)/shard_map/ppermute | solution.py:579
  193.4 20.4 %collective-permute-start.23 = (bf16[2,128,512]{2,1,0:T(8,128)(2,1)S(1)}, bf16[2,128,512]{2,1,0:T(8,128)(2,1)S(1)}, u32[]{:S(2)}, u32[]{:S(2)}) collective-permute-start(bf16[2,128,512]{2,1,0:T(8,128)(2,1)S(1)} %get-tuple-element.60), channel_id=1, source_target_pairs={{10,0},{11,1},{8,2},{9,3},{2,4},{3,5},{0,6},{1,7},{14,8},{15,9},{1... | collective-permute-start | bytes 786440 | tf_op jit(solution)/shard_map/ppermute | solution.py:579
  197.3 20.8 %collective-permute-start.34 = (bf16[64,512]{1,0:T(8,128)(2,1)S(1)}, bf16[64,512]{1,0:T(8,128)(2,1)S(1)}, u32[]{:S(2)}, u32[]{:S(2)}) collective-permute-start(bf16[64,512]{1,0:T(8,128)(2,1)S(1)} %fusion.7), channel_id=1, source_target_pairs={{0,4},{1,5},{2,6},{3,7},{4,0},{5,1},{6,2},{7,3},{8,12},{9,13},{10,... | collective-permute-start | bytes 196616 | tf_op jit(solution)/shard_map/ppermute | solution.py:594
  (33 other events, 298.1 us)
